TPU v7x, 32 devices: a whole 2x2x4 slice. The times are simulated.
32 devices in a mesh: groups: 2 (over y), dp: 16 (over z, x, core).
Axes of the slice: x: 2, y: 2, z: 4, core: 2. Of those that a mesh axis runs over, the one named last changes fastest.
Arguments:
- merger_input: bfloat16 [3072, 2304], P(('groups', 'dp')), parts along dimension 0, may hold values from -6 to 6
- merger_weight: bfloat16 [2304, 2048], P('dp'), may hold values from -0.125 to 0.125
- merger_bias: float32 [2048], replicated, may hold values from -3 to 3
- norm_gain: float32 [2048], replicated, may hold values from 0.5 to 1.5
- gate_weight: bfloat16 [16, 2048, 768], P('dp'), may hold values from -0.125 to 0.125
- up_weight: bfloat16 [16, 2048, 768], P('dp'), may hold values from -0.125 to 0.125
- down_weight: bfloat16 [16, 768, 2048], P('dp'), may hold values from -0.21875 to 0.21875
- expert_ids: int32 [3072, 8], P(('groups', 'dp')), parts along dimension 0, may hold values from 0 to 15, all different within a row; in each aligned block of 96 rows (0 to 95, 96 to 191, ...) at most 72 rows name the same one
- combine_ints: int32 [3072, 8], P(('groups', 'dp')), parts along dimension 0, may hold values from 1 to 16
Outputs:
- mixed: bfloat16 [3072, 2048], P(('groups', 'dp')), parts along dimension 0
There are 2 independent parts, one for each index of `groups`. A program takes and returns all parts, laid end to end along the dimension named above; an argument that names none is the same for every part. Nothing has to cross between parts.
Inputs may be any that keep to these rules, and one draw needn't show every extreme that they name: `expert_ids`: each row names 8 different experts; in the rows of one device no expert is named more than 72 times, and that many is reached.
All inputs are finite; a program needn't handle non-finite values.
Results may differ from a plain program's by a relative error of at most 0.0051.
Values may be sent and summed in bfloat16 or wider, within the bound.
No kernel may reach another device: no remote copies, remote signals or barrier semaphores. Data moves between devices by JAX's collectives and lax.ppermute only.
A program may use at most 128 MiB of HBM per device.

v0:
```python
import functools

import jax
import jax.numpy as jnp
from jax import lax
from jax.experimental import pallas as pl
from jax.experimental.pallas import tpu as pltpu
from jax.sharding import PartitionSpec as P


def run_experts(received, gate_weight, up_weight, down_weight, ndevices):
    local = gate_weight.shape[0]
    slots = received.shape[1]
    width = received.shape[2]
    inputs = received.reshape(ndevices, local, slots, width)
    gate = jnp.einsum("jlcd,ldh->jlch", inputs, gate_weight, preferred_element_type=jnp.float32)
    up = jnp.einsum("jlcd,ldh->jlch", inputs, up_weight, preferred_element_type=jnp.float32)
    hidden = (jax.nn.silu(gate) * up).astype(jnp.bfloat16)
    output = jnp.einsum("jlch,lhd->jlcd", hidden, down_weight, preferred_element_type=jnp.float32)
    return output.astype(jnp.bfloat16).reshape(ndevices * local, slots, width)


def routed(
    merger_input,
    merger_weight,
    merger_bias,
    norm_gain,
    gate_weight,
    up_weight,
    down_weight,
    expert_ids,
    combine_ints,
):
    ndevices = lax.axis_size("dp")
    rows = merger_input.shape[0]
    width = merger_weight.shape[1]
    choose = expert_ids.shape[1]
    experts_all = gate_weight.shape[0] * ndevices
    capacity = (3 * rows * choose + 2 * ndevices - 1) // (2 * ndevices)
    act = jax.nn.gelu(merger_input.astype(jnp.float32), approximate=False).astype(jnp.bfloat16)
    merged = jnp.dot(
        act,
        lax.all_gather(merger_weight, "dp", axis=0, tiled=True),
        preferred_element_type=jnp.float32,
    )
    merged = merged + merger_bias
    scale = lax.rsqrt(jnp.mean(merged * merged, axis=1, keepdims=True) + 1e-06)
    normed = (merged * scale * norm_gain).astype(jnp.bfloat16)
    onehot = (
        expert_ids[:, :, None] == jnp.arange(experts_all, dtype=jnp.int32)[None, None, :]
    ).astype(jnp.int32)
    flat_hot = onehot.reshape(rows * choose, experts_all)
    before = jnp.cumsum(flat_hot, axis=0) - flat_hot
    position = jnp.sum(before * flat_hot, axis=1)
    slot_flat = expert_ids.reshape(rows * choose) * capacity + position
    repeated = jnp.repeat(normed, choose, axis=0)
    outgoing = jnp.zeros((experts_all * capacity, width), jnp.bfloat16).at[slot_flat].set(repeated)
    outgoing = outgoing.reshape(experts_all, capacity, width)
    received = lax.all_to_all(outgoing, "dp", split_axis=0, concat_axis=0, tiled=True)
    served = run_experts(received, gate_weight, up_weight, down_weight, ndevices)
    returned = lax.all_to_all(served, "dp", split_axis=0, concat_axis=0, tiled=True)
    returned = returned.reshape(experts_all * capacity, width)
    picked = returned[slot_flat].reshape(rows, choose, width)
    counts = combine_ints.astype(jnp.float32)
    weights = counts / jnp.sum(counts, axis=1, keepdims=True)
    combined = jnp.sum(weights[:, :, None] * picked.astype(jnp.float32), axis=1)
    return (merged + combined).astype(jnp.bfloat16)


LANES = 128


def swap_pairs(n):
    return [(i, i ^ 1) for i in range(n)]


def ring_order(chips):
    half = chips // 2
    return [2 * z for z in range(half)] + [2 * z + 1 for z in reversed(range(half))]


def ring_pairs(chips, by):
    order = ring_order(chips)
    pairs = []
    for spot, chip in enumerate(order):
        target = order[(spot + by) % chips]
        pairs += [(2 * chip, 2 * target), (2 * chip + 1, 2 * target + 1)]
    return pairs


def tile_of(extent, most):
    return max(t for t in range(LANES, most + 1, LANES) if extent % t == 0)


def serve_body(columns, blocks, *refs):
    ins, share_ref = refs[:blocks], refs[blocks]
    gate_ref, up_ref, down_ref, own_ref, other_ref, x_ref, h_ref = refs[blocks + 1 :]
    width, wide = gate_ref.shape
    start = 0
    share = []
    for ref, (column, low, high) in zip(ins, columns):
        size = ref.shape[0]
        x_ref[start : start + size, :] = ref[...]
        share.append(share_ref[low:high, column : column + 1])
        start += size
    share = jnp.concatenate(share, axis=0)
    tile = tile_of(wide, 256)
    for at in range(0, wide, tile):
        x = x_ref[...]
        gate = jnp.dot(x, gate_ref[:, at : at + tile], preferred_element_type=jnp.float32)
        up = jnp.dot(x, up_ref[:, at : at + tile], preferred_element_type=jnp.float32)
        h_ref[:, at : at + tile] = (gate * (1.0 / (1.0 + jnp.exp(-gate))) * up * share).astype(jnp.bfloat16)
    half = start // 2
    tile = tile_of(width, 512)
    for at in range(0, width, tile):
        out = jnp.dot(h_ref[...], down_ref[:, at : at + tile], preferred_element_type=jnp.float32)
        own_ref[:, at : at + tile] = out[:half].astype(jnp.bfloat16)
        other_ref[:, at : at + tile] = out[half:].astype(jnp.bfloat16)


def serve(ins, columns, share, experts):
    rows = sum(x.shape[0] for x in ins)
    width, wide = experts[0].shape
    vmem = pl.BlockSpec(memory_space=pltpu.VMEM)
    return pl.pallas_call(
        functools.partial(serve_body, columns, len(ins)),
        out_shape=[jax.ShapeDtypeStruct((rows // 2, width), jnp.bfloat16)] * 2,
        in_specs=[vmem] * (len(ins) + 4),
        out_specs=[vmem, vmem],
        scratch_shapes=[pltpu.VMEM((rows, width), jnp.bfloat16), pltpu.VMEM((rows, wide), jnp.bfloat16)],
        compiler_params=pltpu.CompilerParams(vmem_limit_bytes=VMEM_LIMIT),
        cost_estimate=pl.CostEstimate(
            flops=6 * rows * width * wide, bytes_accessed=6 * width * wide, transcendentals=rows * wide
        ),
        name="serve",
    )(*ins, share, *experts)


VMEM_LIMIT = 24 * 1024 * 1024


def around(array, order, spot):
    ring = jnp.stack([array[chip] for chip in order] * 2)
    zero = jnp.uint32(0)
    return lax.dynamic_slice(ring, (spot,) + (zero,) * (array.ndim - 1), array.shape)


def dense(
    merger_input,
    merger_weight,
    merger_bias,
    norm_gain,
    gate_weight,
    up_weight,
    down_weight,
    expert_ids,
    combine_ints,
):
    n = lax.axis_size("dp")
    chips = n // 2
    far = chips // 2
    rows = merger_input.shape[0]
    depth, _ = merger_weight.shape
    order = ring_order(chips)
    me = lax.axis_index("dp").astype(jnp.uint32)
    core = me & 1
    spot = jnp.where((me & 2) == 0, me >> 2, jnp.uint32(chips - 1) - (me >> 2))

    swap = functools.partial(lax.ppermute, axis_name="dp", perm=swap_pairs(n))
    ahead = functools.partial(lax.ppermute, axis_name="dp", perm=ring_pairs(chips, 1))
    back = functools.partial(lax.ppermute, axis_name="dp", perm=ring_pairs(chips, -1))

    counts = combine_ints.astype(jnp.float32)
    weights = counts / jnp.sum(counts, axis=1, keepdims=True)
    named = expert_ids[:, :, None] == jnp.arange(n, dtype=jnp.int32)[None, None, :]
    spread = jnp.sum(jnp.where(named, weights[:, :, None], 0.0), axis=1)
    share = lax.all_to_all(spread.T, "dp", split_axis=0, concat_axis=0, tiled=True)
    share = share.reshape(chips, 2, rows)
    share = jnp.where(core == 0, share, share[:, ::-1])
    share = around(share, order, spot).reshape(n, rows).T

    act = jax.nn.gelu(merger_input.astype(jnp.float32), approximate=False).astype(jnp.bfloat16)
    act = act.reshape(rows, chips, 2, depth)
    first, second = act[:, :, 0], act[:, :, 1]
    kept = jnp.where(core == 0, first, second)
    given = jnp.where(core == 0, second, first)
    both = jnp.concatenate([kept, swap(given)], axis=0).transpose(1, 0, 2)
    both = around(both, order, spot)

    def term(offset, weight, low, high):
        block = both[offset % chips]
        return jnp.dot(block[:, low:high], weight, preferred_element_type=jnp.float32)

    left = right = merger_weight
    total = term(0, merger_weight, 0, depth)
    for step in range(1, far):
        left, right = ahead(left), back(right)
        total = total + term(-step, left, 0, depth) + term(step, right, 0, depth)
    mid = depth // 2
    total = total + term(far, ahead(left[:mid]), 0, mid) + term(far, back(right[mid:]), mid, depth)
    merged = total[:rows] + swap(total[rows:]) + merger_bias
    scale = lax.rsqrt(jnp.mean(merged * merged, axis=1, keepdims=True) + 1e-06)
    normed = (merged * scale * norm_gain).astype(jnp.bfloat16)

    experts = [w[0] for w in (gate_weight, up_weight, down_weight)]
    cut = rows // 2
    left = right = normed
    other = swap(normed)
    outs = [serve([normed, other], [(0, 0, rows), (1, 0, rows)], share, experts)]
    for step in range(1, far + 1):
        if step < far:
            lo, hi = 2 * (chips - step), 2 * step
            columns = [(lo, 0, rows), (hi, 0, rows), (lo + 1, 0, rows), (hi + 1, 0, rows)]
        else:
            left, right = left[:cut], right[cut:]
            lo = 2 * far
            columns = [(lo, 0, cut), (lo, cut, rows), (lo + 1, 0, cut), (lo + 1, cut, rows)]
        left = ahead(left)
        right = back(right)
        left_other, right_other = swap(left), swap(right)
        outs.append(serve([left, right, left_other, right_other], columns, share, experts))
    sums = [own.astype(jnp.float32) + swap(other).astype(jnp.float32) for own, other in outs]
    top, bottom = ahead(sums[far][:cut].astype(jnp.bfloat16)), back(sums[far][cut:].astype(jnp.bfloat16))
    top = jnp.pad(top, ((0, rows - cut), (0, 0)))
    bottom = jnp.pad(bottom, ((cut, 0), (0, 0)))
    for step in reversed(range(1, far)):
        to_back, to_ahead = sums[step][:rows], sums[step][rows:]
        top = ahead((to_ahead + top.astype(jnp.float32)).astype(jnp.bfloat16))
        bottom = back((to_back + bottom.astype(jnp.float32)).astype(jnp.bfloat16))
    combined = sums[0] + top.astype(jnp.float32) + bottom.astype(jnp.float32)
    return (merged + combined).astype(jnp.bfloat16)


def shards(*arrays):
    gate_weight, expert_ids = arrays[4], arrays[7]
    n = lax.axis_size("dp")
    rows, choose = expert_ids.shape
    capacity = (3 * rows * choose + 2 * n - 1) // (2 * n)
    if gate_weight.shape[0] == 1 and n % 4 == 0 and n >= 8 and 2 * capacity >= rows:
        return dense(*arrays)
    return routed(*arrays)


def solution(mesh):
    placed = (
        P(("groups", "dp"), None),
        P("dp", None),
        P(),
        P(),
        P("dp", None, None),
        P("dp", None, None),
        P("dp", None, None),
        P(("groups", "dp"), None),
        P(("groups", "dp"), None),
    )
    return jax.shard_map(
        shards, mesh=mesh, in_specs=placed, out_specs=P(("groups", "dp"), None), check_vma=False
    )
```

profile of v0, /device:TPU:0, one launch (start us, length us, event | category | flops | bytes accessed | tf_op | source)
XLA Modules:
  0.0 167.3 jit_solution(16912421346674509595)
XLA Ops:
  0.0 3.1 %collective-permute-start.1 = (bf16[144,2048]{1,0:T(8,128)(2,1)}, bf16[144,2048]{1,0:T(8,128)(2,1)S(1)}, u32[]{:S(2)}, u32[]{:S(2)}) collective-permute-start(bf16[144,2048]{1,0:T(8,128)(2,1)} %param.10), channel_id=1, source_target_pairs={{0,4},{1,5},{4,8},{5,9},{8,12},{9,13},{12,14},{13,15},{14,10},{15,... | collective-permute-start | bytes 1769480 | tf_op jit(solution)/shard_map/ppermute | solution.py:197
  3.1 0.7 convert_reduce_fusion
  3.8 0.7 convert_divide_fusion
  4.5 1.3 select_reduce_fusion
  5.8 6.4 %all-to-all-start = ((f32[16,1,96]{2,1,0:T(1,128)}), f32[16,1,96]{2,1,0:T(1,128)S(1)}, u32[]{:S(2)}, u32[]{:S(2)}) async-start(f32[16,1,96]{2,1,0:T(1,128)} %bitcast.14), calls=%async_computation | async-start | bytes 16384 | tf_op jit(solution)/shard_map/all_to_all | solution.py:177
  12.1 1.3 copy.24
  13.4 2.6 %fusion.5 = bf16[96,2304]{0,1:T(8,128)(2,1)S(1)} fusion(bf16[96,2304]{0,1:T(8,128)(2,1)S(1)} %copy.24), kind=kLoop, calls=%fused_computation.15 | loop fusion | flops 14598144 | bytes 884736 | tf_op jit(solution)/shard_map/convert_element_type | solution.py:182
  16.6 3.5 %all-to-all-done = f32[16,1,96]{2,1,0:T(1,128)S(1)} async-done(((f32[16,1,96]{2,1,0:T(1,128)}), f32[16,1,96]{2,1,0:T(1,128)S(1)}, u32[]{:S(2)}, u32[]{:S(2)}) %all-to-all-start) | async-done | bytes 6176 | tf_op jit(solution)/shard_map/all_to_all | solution.py:177
  20.8 0.6 collective-permute-start.3
  22.0 1.5 collective-permute-start.4
  24.0 12.0 %collective-permute-done.3 = bf16[144,2048]{1,0:T(8,128)(2,1)S(1)} collective-permute-done((bf16[144,2048]{1,0:T(8,128)(2,1)S(1)}, bf16[144,2048]{1,0:T(8,128)(2,1)S(1)}, u32[]{:S(2)}, u32[]{:S(2)}) %collective-permute-start.3) | collective-permute-done | bytes 589856 | tf_op jit(solution)/shard_map/ppermute | solution.py:197
  35.9 0.6 collective-permute-start.5
  37.2 1.5 collective-permute-start.6
  39.0 11.1 %collective-permute-done.5 = bf16[144,2048]{1,0:T(8,128)(2,1)S(1)} collective-permute-done((bf16[144,2048]{1,0:T(8,128)(2,1)S(1)}, bf16[144,2048]{1,0:T(8,128)(2,1)S(1)}, u32[]{:S(2)}, u32[]{:S(2)}) %collective-permute-start.5) | collective-permute-done | bytes 589856 | tf_op jit(solution)/shard_map/ppermute | solution.py:197
  50.2 0.6 collective-permute-start.7
  51.4 1.5 collective-permute-start.8
  53.3 3.9 %collective-permute-done.7 = bf16[72,2048]{1,0:T(8,128)(2,1)S(1)} collective-permute-done((bf16[72,2048]{1,0:T(8,128)(2,1)S(1)}, bf16[72,2048]{1,0:T(8,128)(2,1)S(1)}, u32[]{:S(2)}, u32[]{:S(2)}) %collective-permute-start.7) | collective-permute-done | bytes 294944 | tf_op jit(solution)/shard_map/ppermute | solution.py:200
  57.7 0.8 collective-permute-done.8
  58.9 0.5 fusion.3
  59.6 2.2 %collective-permute-done.9 = f32[96,2048]{1,0:T(8,128)S(1)} collective-permute-done((f32[96,2048]{1,0:T(8,128)S(1)}, f32[96,2048]{1,0:T(8,128)S(1)}, u32[]{:S(2)}, u32[]{:S(2)}) %collective-permute-start.9) | collective-permute-done | bytes 786464 | tf_op jit(solution)/shard_map/ppermute | solution.py:201
  62.2 0.7 collective-permute-start.12
  63.0 1.3 collective-permute-start.13
  64.3 9.2 %collective-permute-done.12.refs_0_ = bf16[96,2048]{1,0:T(8,128)(2,1)} collective-permute-done((bf16[96,2048]{1,0:T(8,128)(2,1)S(1)}, bf16[96,2048]{1,0:T(8,128)(2,1)}, u32[]{:S(2)}, u32[]{:S(2)}) %collective-permute-start.12) | collective-permute-done | bytes 393248 | tf_op jit(solution)/shard_map/ppermute | solution.py:218
  73.6 0.7 collective-permute-start.17
  74.2 1.3 collective-permute-start.18
  75.6 8.5 %collective-permute-done.17.refs_0_ = bf16[96,2048]{1,0:T(8,128)(2,1)S(1)} collective-permute-done((bf16[96,2048]{1,0:T(8,128)(2,1)}, bf16[96,2048]{1,0:T(8,128)(2,1)S(1)}, u32[]{:S(2)}, u32[]{:S(2)}) %collective-permute-start.17) | collective-permute-done | bytes 393248 | tf_op jit(solution)/shard_map/ppermute | solution.py:218
  84.1 0.7 collective-permute-start.22
  84.8 1.3 collective-permute-start.23
  86.1 0.5 collective-permute-start.15
  86.6 6.9 %collective-permute-done.22.refs_0_ = bf16[96,2048]{1,0:T(8,128)(2,1)S(1)} collective-permute-done((bf16[96,2048]{1,0:T(8,128)(2,1)S(1)}, bf16[96,2048]{1,0:T(8,128)(2,1)S(1)}, u32[]{:S(2)}, u32[]{:S(2)}) %collective-permute-start.22) | collective-permute-done | bytes 393248 | tf_op jit(solution)/shard_map/ppermute | solution.py:218
  93.5 0.7 copy-done.6
  94.3 0.7 slice.194
  95.0 0.7 collective-permute-start.27
  95.6 0.8 copy-done.8
  96.4 0.7 slice.195
  97.1 1.3 collective-permute-start.28
  98.5 0.7 copy.26
  99.2 1.9 %copy-done.1 = bf16[1,2048,768]{2,1,0:T(8,128)(2,1)S(1)} copy-done((bf16[1,2048,768]{2,1,0:T(8,128)(2,1)S(1)}, bf16[1,2048,768]{2,1,0:T(8,128)(2,1)}, u32[]{:S(2)}) %copy-start.1) | copy-done | bytes 3145752
  101.1 1.9 %copy-done.3 = bf16[1,768,2048]{2,1,0:T(8,128)(2,1)S(1)} copy-done((bf16[1,768,2048]{2,1,0:T(8,128)(2,1)S(1)}, bf16[1,768,2048]{2,1,0:T(8,128)(2,1)}, u32[]{:S(2)}) %copy-start.3) | copy-done | bytes 3145752
  103.0 0.8 copy-done.4
  103.8 3.2 %serve.5 = (bf16[96,2048]{1,0:T(8,128)(2,1)S(1)}, bf16[96,2048]{1,0:T(8,128)(2,1)S(1)}) custom-call(bf16[96,2048]{1,0:T(8,128)(2,1)S(1)} %multiply_convert_fusion.refs_0_, bf16[96,2048]{1,0:T(8,128)(2,1)} %collective-permute-done.10.refs_1_, f32[96,16]{1,0:T(8,128)S(1)} %bitcast.68, bf16[2048,768]{1,0:T(8,128)(2,1)S(1)} %bitcast.53, ...), custom_call_target="tpu_custom_call" | custom-call | flops 1811939328 | bytes 9437184 | tf_op jit(solution)/shard_map/serve/pallas_call | solution.py:125
  107.1 0.5 collective-permute-start.19
  108.2 5.2 %serve.6 = (bf16[192,2048]{1,0:T(8,128)(2,1)S(1)}, bf16[192,2048]{1,0:T(8,128)(2,1)S(1)}) custom-call(bf16[96,2048]{1,0:T(8,128)(2,1)} %collective-permute-done.12.refs_0_, bf16[96,2048]{1,0:T(8,128)(2,1)} %collective-permute-done.13.refs_1_, bf16[96,2048]{1,0:T(8,128)(2,1)} %collective-permute-done.14.refs_2_, ...), custom_call_target="tpu_custom_call" | custom-call | flops 3623878656 | bytes 9437184 | tf_op jit(solution)/shard_map/serve/pallas_call | solution.py:125
  113.4 0.5 collective-permute-start.24
  114.0 3.0 %serve.9 = (bf16[96,2048]{1,0:T(8,128)(2,1)S(1)}, bf16[96,2048]{1,0:T(8,128)(2,1)S(1)}) custom-call(bf16[48,2048]{1,0:T(8,128)(2,1)} %collective-permute-done.27.refs_0_, bf16[48,2048]{1,0:T(8,128)(2,1)} %collective-permute-done.28.refs_1_, bf16[48,2048]{1,0:T(8,128)(2,1)S(1)} %collective-permute-done.29.refs_2_, ...), custom_call_target="tpu_custom_call" | custom-call | flops 1811939328 | bytes 9437184 | tf_op jit(solution)/shard_map/serve/pallas_call | solution.py:125
  117.0 0.5 collective-permute-start.16
  117.6 3.8 %serve.7 = (bf16[192,2048]{1,0:T(8,128)(2,1)S(1)}, bf16[192,2048]{1,0:T(8,128)(2,1)S(1)}) custom-call(bf16[96,2048]{1,0:T(8,128)(2,1)S(1)} %copy-done.11, bf16[96,2048]{1,0:T(8,128)(2,1)S(1)} %copy-done.13, bf16[96,2048]{1,0:T(8,128)(2,1)S(1)} %collective-permute-done.19.refs_2_, bf16[96,2048]{1,0:T(8,128)(2,1)S(1)} %collective-permute-done.20.refs_3_, ...), custom_call_target="tpu_custom_call" | custom-call | flops 3623878656 | bytes 9437184 | tf_op jit(solution)/shard_map/serve/pallas_call | solution.py:125
  121.9 4.1 %serve.8 = (bf16[192,2048]{1,0:T(8,128)(2,1)S(1)}, bf16[192,2048]{1,0:T(8,128)(2,1)S(1)}) custom-call(bf16[96,2048]{1,0:T(8,128)(2,1)S(1)} %copy-done.7, bf16[96,2048]{1,0:T(8,128)(2,1)S(1)} %copy-done.9, bf16[96,2048]{1,0:T(8,128)(2,1)S(1)} %collective-permute-done.24.refs_2_, bf16[96,2048]{1,0:T(8,128)(2,1)S(1)} %collective-permute-done.25.refs_3_, ...), custom_call_target="tpu_custom_call" | custom-call | flops 3623878656 | bytes 9437184 | tf_op jit(solution)/shard_map/serve/pallas_call | solution.py:125
  126.3 0.7 collective-permute-start.32
  127.0 1.3 collective-permute-done.26
  128.3 1.5 collective-permute-start.36
  130.0 3.5 %collective-permute-done.32 = bf16[48,2048]{1,0:T(8,128)(2,1)S(1)} collective-permute-done((bf16[48,2048]{1,0:T(8,128)(2,1)S(1)}, bf16[48,2048]{1,0:T(8,128)(2,1)S(1)}, u32[]{:S(2)}, u32[]{:S(2)}) %collective-permute-start.32) | collective-permute-done | bytes 196640 | tf_op jit(solution)/shard_map/ppermute | solution.py:223
  133.6 1.7 %collective-permute-done.36 = bf16[48,2048]{1,0:T(8,128)(2,1)S(1)} collective-permute-done((bf16[48,2048]{1,0:T(8,128)(2,1)S(1)}, bf16[48,2048]{1,0:T(8,128)(2,1)S(1)}, u32[]{:S(2)}, u32[]{:S(2)}) %collective-permute-start.36) | collective-permute-done | bytes 196640 | tf_op jit(solution)/shard_map/ppermute | solution.py:223
  135.4 0.7 collective-permute-start.33
  136.2 1.3 collective-permute-start.37
  137.7 8.0 %collective-permute-done.33 = bf16[96,2048]{1,0:T(8,128)(2,1)S(1)} collective-permute-done((bf16[96,2048]{1,0:T(8,128)(2,1)S(1)}, bf16[96,2048]{1,0:T(8,128)(2,1)S(1)}, u32[]{:S(2)}, u32[]{:S(2)}) %collective-permute-start.33) | collective-permute-done | bytes 393248 | tf_op jit(solution)/shard_map/ppermute | solution.py:228
  146.4 1.6 collective-permute-start.34
  148.7 6.9 %collective-permute-done.34 = bf16[96,2048]{1,0:T(8,128)(2,1)S(1)} collective-permute-done((bf16[96,2048]{1,0:T(8,128)(2,1)S(1)}, bf16[96,2048]{1,0:T(8,128)(2,1)S(1)}, u32[]{:S(2)}, u32[]{:S(2)}) %collective-permute-start.34) | collective-permute-done | bytes 393248 | tf_op jit(solution)/shard_map/ppermute | solution.py:228
  155.6 1.3 collective-permute-done.38
  157.0 1.5 collective-permute-start.35
  158.5 0.6 collective-permute-start.39
  159.1 6.0 %collective-permute-done.35 = bf16[96,2048]{1,0:T(8,128)(2,1)S(1)} collective-permute-done((bf16[96,2048]{1,0:T(8,128)(2,1)S(1)}, bf16[96,2048]{1,0:T(8,128)(2,1)S(1)}, u32[]{:S(2)}, u32[]{:S(2)}) %collective-permute-start.35) | collective-permute-done | bytes 393248 | tf_op jit(solution)/shard_map/ppermute | solution.py:228
  165.1 1.2 collective-permute-done.39
  166.3 1.0 add_convert_fusion
  (127 shorter events, 9.2 us)
Async XLA Ops:
  0.0 20.8 %collective-permute-start.1 = (bf16[144,2048]{1,0:T(8,128)(2,1)}, bf16[144,2048]{1,0:T(8,128)(2,1)S(1)}, u32[]{:S(2)}, u32[]{:S(2)}) collective-permute-start(bf16[144,2048]{1,0:T(8,128)(2,1)} %param.10), channel_id=1, source_target_pairs={{0,4},{1,5},{4,8},{5,9},{8,12},{9,13},{12,14},{13,15},{14,10},{15,... | collective-permute-start | bytes 1769480 | tf_op jit(solution)/shard_map/ppermute | solution.py:197
  3.1 19.0 %collective-permute-start.2 = (bf16[144,2048]{1,0:T(8,128)(2,1)}, bf16[144,2048]{1,0:T(8,128)(2,1)S(1)}, u32[]{:S(2)}, u32[]{:S(2)}) collective-permute-start(bf16[144,2048]{1,0:T(8,128)(2,1)} %param.10), channel_id=1, source_target_pairs={{0,2},{1,3},{4,0},{5,1},{8,4},{9,5},{12,8},{13,9},{14,12},{15,13},... | collective-permute-start | bytes 1769480 | tf_op jit(solution)/shard_map/ppermute | solution.py:197
  5.8 14.4 %all-to-all-start = ((f32[16,1,96]{2,1,0:T(1,128)}), f32[16,1,96]{2,1,0:T(1,128)S(1)}, u32[]{:S(2)}, u32[]{:S(2)}) async-start(f32[16,1,96]{2,1,0:T(1,128)} %bitcast.14), calls=%async_computation | async-start | bytes 16384 | tf_op jit(solution)/shard_map/all_to_all | solution.py:177
  16.1 4.1 %collective-permute-start = (bf16[96,8,144]{0,2,1:T(8,128)(2,1)S(1)}, bf16[96,8,144]{0,2,1:T(8,128)(2,1)S(1)}, u32[]{:S(2)}, u32[]{:S(2)}) collective-permute-start(bf16[96,8,144]{0,2,1:T(8,128)(2,1)S(1)} %get-tuple-element.34), channel_id=1, source_target_pairs={{0,1},{1,0},{2,3},{3,2},{4,5},{5,4},{6,7},{7,6},{8,9},{9,8},{10,11... | collective-permute-start | bytes 663560 | tf_op jit(solution)/shard_map/ppermute | solution.py:187
  20.5 1.1 copy-start.16
  20.8 15.1 %collective-permute-start.3 = (bf16[144,2048]{1,0:T(8,128)(2,1)S(1)}, bf16[144,2048]{1,0:T(8,128)(2,1)S(1)}, u32[]{:S(2)}, u32[]{:S(2)}) collective-permute-start(bf16[144,2048]{1,0:T(8,128)(2,1)S(1)} %collective-permute-done.1), channel_id=1, source_target_pairs={{0,4},{1,5},{4,8},{5,9},{8,12},{9,13},{12,14},{13,15},{14,10},{15,... | collective-permute-start | bytes 1769480 | tf_op jit(solution)/shard_map/ppermute | solution.py:197
  22.0 15.1 %collective-permute-start.4 = (bf16[144,2048]{1,0:T(8,128)(2,1)S(1)}, bf16[144,2048]{1,0:T(8,128)(2,1)S(1)}, u32[]{:S(2)}, u32[]{:S(2)}) collective-permute-start(bf16[144,2048]{1,0:T(8,128)(2,1)S(1)} %collective-permute-done.2), channel_id=1, source_target_pairs={{0,2},{1,3},{4,0},{5,1},{8,4},{9,5},{12,8},{13,9},{14,12},{15,13},... | collective-permute-start | bytes 1769480 | tf_op jit(solution)/shard_map/ppermute | solution.py:197
  35.9 14.2 %collective-permute-start.5 = (bf16[144,2048]{1,0:T(8,128)(2,1)S(1)}, bf16[144,2048]{1,0:T(8,128)(2,1)S(1)}, u32[]{:S(2)}, u32[]{:S(2)}) collective-permute-start(bf16[144,2048]{1,0:T(8,128)(2,1)S(1)} %collective-permute-done.3), channel_id=1, source_target_pairs={{0,4},{1,5},{4,8},{5,9},{8,12},{9,13},{12,14},{13,15},{14,10},{15,... | collective-permute-start | bytes 1769480 | tf_op jit(solution)/shard_map/ppermute | solution.py:197
  37.2 14.2 %collective-permute-start.6 = (bf16[144,2048]{1,0:T(8,128)(2,1)S(1)}, bf16[144,2048]{1,0:T(8,128)(2,1)S(1)}, u32[]{:S(2)}, u32[]{:S(2)}) collective-permute-start(bf16[144,2048]{1,0:T(8,128)(2,1)S(1)} %collective-permute-done.4), channel_id=1, source_target_pairs={{0,2},{1,3},{4,0},{5,1},{8,4},{9,5},{12,8},{13,9},{14,12},{15,13},... | collective-permute-start | bytes 1769480 | tf_op jit(solution)/shard_map/ppermute | solution.py:197
  50.2 7.1 %collective-permute-start.7 = (bf16[72,2048]{1,0:T(8,128)(2,1)S(1)}, bf16[72,2048]{1,0:T(8,128)(2,1)S(1)}, u32[]{:S(2)}, u32[]{:S(2)}) collective-permute-start(bf16[72,2048]{1,0:T(8,128)(2,1)S(1)} %slice.179), channel_id=1, source_target_pairs={{0,4},{1,5},{4,8},{5,9},{8,12},{9,13},{12,14},{13,15},{14,10},{15,... | collective-permute-start | bytes 884744 | tf_op jit(solution)/shard_map/ppermute | solution.py:200
  51.4 7.1 %collective-permute-start.8 = (bf16[72,2048]{1,0:T(8,128)(2,1)S(1)}, bf16[72,2048]{1,0:T(8,128)(2,1)S(1)}, u32[]{:S(2)}, u32[]{:S(2)}) collective-permute-start(bf16[72,2048]{1,0:T(8,128)(2,1)S(1)} %slice.181), channel_id=1, source_target_pairs={{0,2},{1,3},{4,0},{5,1},{8,4},{9,5},{12,8},{13,9},{14,12},{15,13},... | collective-permute-start | bytes 884744 | tf_op jit(solution)/shard_map/ppermute | solution.py:200
  59.4 2.4 %copy-start.18 = (f32[2048]{0:T(1024)S(1)}, f32[2048]{0:T(1024)}, u32[]{:S(2)}) copy-start(f32[2048]{0:T(1024)} %param.11) | copy-start | bytes 24580
  59.5 2.4 %collective-permute-start.9 = (f32[96,2048]{1,0:T(8,128)S(1)}, f32[96,2048]{1,0:T(8,128)S(1)}, u32[]{:S(2)}, u32[]{:S(2)}) collective-permute-start(f32[96,2048]{1,0:T(8,128)S(1)} %slice.183), channel_id=1, source_target_pairs={{0,1},{1,0},{2,3},{3,2},{4,5},{5,4},{6,7},{7,6},{8,9},{9,8},{10,11... | collective-permute-start | bytes 2359304 | tf_op jit(solution)/shard_map/ppermute | solution.py:201
  59.6 2.5 %copy-start.17 = (f32[2048]{0:T(1024)S(1)}, f32[2048]{0:T(1024)}, u32[]{:S(2)}) copy-start(f32[2048]{0:T(1024)} %param.12) | copy-start | bytes 24580
  61.8 37.3 %copy-start = (bf16[1,2048,768]{2,1,0:T(8,128)(2,1)S(1)}, bf16[1,2048,768]{2,1,0:T(8,128)(2,1)}, u32[]{:S(2)}) copy-start(bf16[1,2048,768]{2,1,0:T(8,128)(2,1)} %param.13) | copy-start | bytes 9437188
  62.1 36.4 %copy-start.14 = (f32[96,2048]{1,0:T(8,128)}, f32[96,2048]{1,0:T(8,128)S(1)}, u32[]{:S(2)}) copy-start(f32[96,2048]{1,0:T(8,128)S(1)} %get-tuple-element.26) | copy-start | bytes 2359300
  62.2 11.3 %collective-permute-start.12 = (bf16[96,2048]{1,0:T(8,128)(2,1)S(1)}, bf16[96,2048]{1,0:T(8,128)(2,1)}, u32[]{:S(2)}, u32[]{:S(2)}) collective-permute-start(bf16[96,2048]{1,0:T(8,128)(2,1)S(1)} %multiply_convert_fusion.refs_0_), channel_id=1, source_target_pairs={{0,4},{1,5},{4,8},{5,9},{8,12},{9,13},{12,14},{13,15},{14,10},{15,... | collective-permute-start | bytes 1179656 | tf_op jit(solution)/shard_map/ppermute | solution.py:218
  63.0 11.3 %collective-permute-start.13 = (bf16[96,2048]{1,0:T(8,128)(2,1)S(1)}, bf16[96,2048]{1,0:T(8,128)(2,1)}, u32[]{:S(2)}, u32[]{:S(2)}) collective-permute-start(bf16[96,2048]{1,0:T(8,128)(2,1)S(1)} %multiply_convert_fusion.refs_0_), channel_id=1, source_target_pairs={{0,2},{1,3},{4,0},{5,1},{8,4},{9,5},{12,8},{13,9},{14,12},{15,13},... | collective-permute-start | bytes 1179656 | tf_op jit(solution)/shard_map/ppermute | solution.py:219
  73.6 10.5 %collective-permute-start.17 = (bf16[96,2048]{1,0:T(8,128)(2,1)}, bf16[96,2048]{1,0:T(8,128)(2,1)S(1)}, u32[]{:S(2)}, u32[]{:S(2)}) collective-permute-start(bf16[96,2048]{1,0:T(8,128)(2,1)} %collective-permute-done.12.refs_0_), channel_id=1, source_target_pairs={{0,4},{1,5},{4,8},{5,9},{8,12},{9,13},{12,14},{13,15},{14,10},{15,... | collective-permute-start | bytes 1179656 | tf_op jit(solution)/shard_map/ppermute | solution.py:218
  74.2 10.5 %collective-permute-start.18 = (bf16[96,2048]{1,0:T(8,128)(2,1)}, bf16[96,2048]{1,0:T(8,128)(2,1)S(1)}, u32[]{:S(2)}, u32[]{:S(2)}) collective-permute-start(bf16[96,2048]{1,0:T(8,128)(2,1)} %collective-permute-done.13.refs_1_), channel_id=1, source_target_pairs={{0,2},{1,3},{4,0},{5,1},{8,4},{9,5},{12,8},{13,9},{14,12},{15,13},... | collective-permute-start | bytes 1179656 | tf_op jit(solution)/shard_map/ppermute | solution.py:219
  75.6 23.6 %collective-permute-start.10 = (bf16[96,2048]{1,0:T(8,128)(2,1)S(1)}, bf16[96,2048]{1,0:T(8,128)(2,1)}, u32[]{:S(2)}, u32[]{:S(2)}) collective-permute-start(bf16[96,2048]{1,0:T(8,128)(2,1)S(1)} %multiply_convert_fusion.refs_0_), channel_id=1, source_target_pairs={{0,1},{1,0},{2,3},{3,2},{4,5},{5,4},{6,7},{7,6},{8,9},{9,8},{10,11... | collective-permute-start | bytes 1179656 | tf_op jit(solution)/shard_map/ppermute | solution.py:208
  84.1 13.0 %copy-start.10 = (bf16[96,2048]{1,0:T(8,128)(2,1)}, bf16[96,2048]{1,0:T(8,128)(2,1)S(1)}, u32[]{:S(2)}) copy-start(bf16[96,2048]{1,0:T(8,128)(2,1)S(1)} %collective-permute-done.17.refs_0_) | copy-start | bytes 1179652
  84.1 9.4 %collective-permute-start.22 = (bf16[96,2048]{1,0:T(8,128)(2,1)S(1)}, bf16[96,2048]{1,0:T(8,128)(2,1)S(1)}, u32[]{:S(2)}, u32[]{:S(2)}) collective-permute-start(bf16[96,2048]{1,0:T(8,128)(2,1)S(1)} %collective-permute-done.17.refs_0_), channel_id=1, source_target_pairs={{0,4},{1,5},{4,8},{5,9},{8,12},{9,13},{12,14},{13,15},{14,10},{15,... | collective-permute-start | bytes 1179656 | tf_op jit(solution)/shard_map/ppermute | solution.py:218
  84.8 13.7 %copy-start.12 = (bf16[96,2048]{1,0:T(8,128)(2,1)}, bf16[96,2048]{1,0:T(8,128)(2,1)S(1)}, u32[]{:S(2)}) copy-start(bf16[96,2048]{1,0:T(8,128)(2,1)S(1)} %collective-permute-done.18.refs_1_) | copy-start | bytes 1179652
  84.8 10.9 %collective-permute-start.23 = (bf16[96,2048]{1,0:T(8,128)(2,1)S(1)}, bf16[96,2048]{1,0:T(8,128)(2,1)S(1)}, u32[]{:S(2)}, u32[]{:S(2)}) collective-permute-start(bf16[96,2048]{1,0:T(8,128)(2,1)S(1)} %collective-permute-done.18.refs_1_), channel_id=1, source_target_pairs={{0,2},{1,3},{4,0},{5,1},{8,4},{9,5},{12,8},{13,9},{14,12},{15,13},... | collective-permute-start | bytes 1179656 | tf_op jit(solution)/shard_map/ppermute | solution.py:219
  86.1 20.9 %collective-permute-start.14 = (bf16[96,2048]{1,0:T(8,128)(2,1)}, bf16[96,2048]{1,0:T(8,128)(2,1)}, u32[]{:S(2)}, u32[]{:S(2)}) collective-permute-start(bf16[96,2048]{1,0:T(8,128)(2,1)} %collective-permute-done.12.refs_0_), channel_id=1, source_target_pairs={{0,1},{1,0},{2,3},{3,2},{4,5},{5,4},{6,7},{7,6},{8,9},{9,8},{10,11... | collective-permute-start | bytes 1179656 | tf_op jit(solution)/shard_map/ppermute | solution.py:220
  86.1 21.4 %collective-permute-start.15 = (bf16[96,2048]{1,0:T(8,128)(2,1)}, bf16[96,2048]{1,0:T(8,128)(2,1)}, u32[]{:S(2)}, u32[]{:S(2)}) collective-permute-start(bf16[96,2048]{1,0:T(8,128)(2,1)} %collective-permute-done.13.refs_1_), channel_id=1, source_target_pairs={{0,1},{1,0},{2,3},{3,2},{4,5},{5,4},{6,7},{7,6},{8,9},{9,8},{10,11... | collective-permute-start | bytes 1179656 | tf_op jit(solution)/shard_map/ppermute | solution.py:220
  93.5 0.7 copy-start.6
  95.0 12.7 %collective-permute-start.27 = (bf16[48,2048]{1,0:T(8,128)(2,1)}, bf16[48,2048]{1,0:T(8,128)(2,1)}, u32[]{:S(2)}, u32[]{:S(2)}) collective-permute-start(bf16[48,2048]{1,0:T(8,128)(2,1)} %slice.194), channel_id=1, source_target_pairs={{0,4},{1,5},{4,8},{5,9},{8,12},{9,13},{12,14},{13,15},{14,10},{15,... | collective-permute-start | bytes 589832 | tf_op jit(solution)/shard_map/ppermute | solution.py:218
  95.6 0.8 copy-start.8
  97.1 11.0 %collective-permute-start.28 = (bf16[48,2048]{1,0:T(8,128)(2,1)}, bf16[48,2048]{1,0:T(8,128)(2,1)}, u32[]{:S(2)}, u32[]{:S(2)}) collective-permute-start(bf16[48,2048]{1,0:T(8,128)(2,1)} %slice.195), channel_id=1, source_target_pairs={{0,2},{1,3},{4,0},{5,1},{8,4},{9,5},{12,8},{13,9},{14,12},{15,13},... | collective-permute-start | bytes 589832 | tf_op jit(solution)/shard_map/ppermute | solution.py:219
  99.2 1.9 %copy-start.1 = (bf16[1,2048,768]{2,1,0:T(8,128)(2,1)S(1)}, bf16[1,2048,768]{2,1,0:T(8,128)(2,1)}, u32[]{:S(2)}) copy-start(bf16[1,2048,768]{2,1,0:T(8,128)(2,1)} %param.14) | copy-start | bytes 9437188
  101.1 1.9 %copy-start.3 = (bf16[1,768,2048]{2,1,0:T(8,128)(2,1)S(1)}, bf16[1,768,2048]{2,1,0:T(8,128)(2,1)}, u32[]{:S(2)}) copy-start(bf16[1,768,2048]{2,1,0:T(8,128)(2,1)} %param.15) | copy-start | bytes 9437188
  103.0 0.8 copy-start.4
  103.8 3.3 %copy-start.11 = (bf16[96,2048]{1,0:T(8,128)(2,1)S(1)}, bf16[96,2048]{1,0:T(8,128)(2,1)}, u32[]{:S(2)}) copy-start(bf16[96,2048]{1,0:T(8,128)(2,1)} %copy-done.10) | copy-start | bytes 1179652
  103.8 3.8 %copy-start.13 = (bf16[96,2048]{1,0:T(8,128)(2,1)S(1)}, bf16[96,2048]{1,0:T(8,128)(2,1)}, u32[]{:S(2)}) copy-start(bf16[96,2048]{1,0:T(8,128)(2,1)} %copy-done.12) | copy-start | bytes 1179652
  103.8 4.4 %copy-start.2 = (bf16[1,2048,768]{2,1,0:T(8,128)(2,1)S(1)}, bf16[1,2048,768]{2,1,0:T(8,128)(2,1)}, u32[]{:S(2)}) copy-start(bf16[1,2048,768]{2,1,0:T(8,128)(2,1)} %param.14) | copy-start | bytes 9437188
  103.8 4.4 %copy-start.5 = (f32[16,96]{0,1:T(8,128)S(1)}, f32[16,96]{0,1:T(8,128)}, u32[]{:S(2)}) copy-start(f32[16,96]{0,1:T(8,128)} %copy.26) | copy-start | bytes 18436
  106.9 6.4 %copy-start.7 = (bf16[96,2048]{1,0:T(8,128)(2,1)S(1)}, bf16[96,2048]{1,0:T(8,128)(2,1)}, u32[]{:S(2)}) copy-start(bf16[96,2048]{1,0:T(8,128)(2,1)} %copy-done.6) | copy-start | bytes 1179652
  106.9 6.9 %copy-start.9 = (bf16[96,2048]{1,0:T(8,128)(2,1)S(1)}, bf16[96,2048]{1,0:T(8,128)(2,1)}, u32[]{:S(2)}) copy-start(bf16[96,2048]{1,0:T(8,128)(2,1)} %copy-done.8) | copy-start | bytes 1179652
  107.0 52.2 %collective-permute-start.11 = (bf16[96,2048]{1,0:T(8,128)(2,1)S(1)}, bf16[96,2048]{1,0:T(8,128)(2,1)S(1)}, u32[]{:S(2)}, u32[]{:S(2)}) collective-permute-start(bf16[96,2048]{1,0:T(8,128)(2,1)S(1)} %get-tuple-element.16), channel_id=1, source_target_pairs={{0,1},{1,0},{2,3},{3,2},{4,5},{5,4},{6,7},{7,6},{8,9},{9,8},{10,11... | collective-permute-start | bytes 1179656 | tf_op jit(solution)/shard_map/ppermute | solution.py:222
  107.1 9.9 %collective-permute-start.19 = (bf16[96,2048]{1,0:T(8,128)(2,1)S(1)}, bf16[96,2048]{1,0:T(8,128)(2,1)S(1)}, u32[]{:S(2)}, u32[]{:S(2)}) collective-permute-start(bf16[96,2048]{1,0:T(8,128)(2,1)S(1)} %copy-done.11), channel_id=1, source_target_pairs={{0,1},{1,0},{2,3},{3,2},{4,5},{5,4},{6,7},{7,6},{8,9},{9,8},{10,11... | collective-permute-start | bytes 1179656 | tf_op jit(solution)/shard_map/ppermute | solution.py:220
  107.5 9.9 %collective-permute-start.20 = (bf16[96,2048]{1,0:T(8,128)(2,1)S(1)}, bf16[96,2048]{1,0:T(8,128)(2,1)S(1)}, u32[]{:S(2)}, u32[]{:S(2)}) collective-permute-start(bf16[96,2048]{1,0:T(8,128)(2,1)S(1)} %copy-done.13), channel_id=1, source_target_pairs={{0,1},{1,0},{2,3},{3,2},{4,5},{5,4},{6,7},{7,6},{8,9},{9,8},{10,11... | collective-permute-start | bytes 1179656 | tf_op jit(solution)/shard_map/ppermute | solution.py:220
  107.6 5.7 %collective-permute-start.29 = (bf16[48,2048]{1,0:T(8,128)(2,1)}, bf16[48,2048]{1,0:T(8,128)(2,1)S(1)}, u32[]{:S(2)}, u32[]{:S(2)}) collective-permute-start(bf16[48,2048]{1,0:T(8,128)(2,1)} %collective-permute-done.27.refs_0_), channel_id=1, source_target_pairs={{0,1},{1,0},{2,3},{3,2},{4,5},{5,4},{6,7},{7,6},{8,9},{9,8},{10,11... | collective-permute-start | bytes 589832 | tf_op jit(solution)/shard_map/ppermute | solution.py:220
  108.1 5.8 %collective-permute-start.30 = (bf16[48,2048]{1,0:T(8,128)(2,1)}, bf16[48,2048]{1,0:T(8,128)(2,1)S(1)}, u32[]{:S(2)}, u32[]{:S(2)}) collective-permute-start(bf16[48,2048]{1,0:T(8,128)(2,1)} %collective-permute-done.28.refs_1_), channel_id=1, source_target_pairs={{0,1},{1,0},{2,3},{3,2},{4,5},{5,4},{6,7},{7,6},{8,9},{9,8},{10,11... | collective-permute-start | bytes 589832 | tf_op jit(solution)/shard_map/ppermute | solution.py:220
  113.4 8.1 %collective-permute-start.24 = (bf16[96,2048]{1,0:T(8,128)(2,1)S(1)}, bf16[96,2048]{1,0:T(8,128)(2,1)S(1)}, u32[]{:S(2)}, u32[]{:S(2)}) collective-permute-start(bf16[96,2048]{1,0:T(8,128)(2,1)S(1)} %copy-done.7), channel_id=1, source_target_pairs={{0,1},{1,0},{2,3},{3,2},{4,5},{5,4},{6,7},{7,6},{8,9},{9,8},{10,11... | collective-permute-start | bytes 1179656 | tf_op jit(solution)/shard_map/ppermute | solution.py:220
  113.9 8.1 %collective-permute-start.25 = (bf16[96,2048]{1,0:T(8,128)(2,1)S(1)}, bf16[96,2048]{1,0:T(8,128)(2,1)S(1)}, u32[]{:S(2)}, u32[]{:S(2)}) collective-permute-start(bf16[96,2048]{1,0:T(8,128)(2,1)S(1)} %copy-done.9), channel_id=1, source_target_pairs={{0,1},{1,0},{2,3},{3,2},{4,5},{5,4},{6,7},{7,6},{8,9},{9,8},{10,11... | collective-permute-start | bytes 1179656 | tf_op jit(solution)/shard_map/ppermute | solution.py:220
  117.0 31.4 %collective-permute-start.16 = (bf16[192,2048]{1,0:T(8,128)(2,1)S(1)}, bf16[192,2048]{1,0:T(8,128)(2,1)S(1)}, u32[]{:S(2)}, u32[]{:S(2)}) collective-permute-start(bf16[192,2048]{1,0:T(8,128)(2,1)S(1)} %get-tuple-element.18), channel_id=1, source_target_pairs={{0,1},{1,0},{2,3},{3,2},{4,5},{5,4},{6,7},{7,6},{8,9},{9,8},{10,11... | collective-permute-start | bytes 2359304 | tf_op jit(solution)/shard_map/ppermute | solution.py:222
  117.5 8.6 %collective-permute-start.31 = (bf16[96,2048]{1,0:T(8,128)(2,1)S(1)}, bf16[96,2048]{1,0:T(8,128)(2,1)S(1)}, u32[]{:S(2)}, u32[]{:S(2)}) collective-permute-start(bf16[96,2048]{1,0:T(8,128)(2,1)S(1)} %get-tuple-element.24), channel_id=1, source_target_pairs={{0,1},{1,0},{2,3},{3,2},{4,5},{5,4},{6,7},{7,6},{8,9},{9,8},{10,11... | collective-permute-start | bytes 1179656 | tf_op jit(solution)/shard_map/ppermute | solution.py:222
  121.4 16.1 %collective-permute-start.21 = (bf16[192,2048]{1,0:T(8,128)(2,1)S(1)}, bf16[192,2048]{1,0:T(8,128)(2,1)S(1)}, u32[]{:S(2)}, u32[]{:S(2)}) collective-permute-start(bf16[192,2048]{1,0:T(8,128)(2,1)S(1)} %get-tuple-element.20), channel_id=1, source_target_pairs={{0,1},{1,0},{2,3},{3,2},{4,5},{5,4},{6,7},{7,6},{8,9},{9,8},{10,11... | collective-permute-start | bytes 2359304 | tf_op jit(solution)/shard_map/ppermute | solution.py:222
  126.0 2.4 %collective-permute-start.26 = (bf16[192,2048]{1,0:T(8,128)(2,1)S(1)}, bf16[192,2048]{1,0:T(8,128)(2,1)S(1)}, u32[]{:S(2)}, u32[]{:S(2)}) collective-permute-start(bf16[192,2048]{1,0:T(8,128)(2,1)S(1)} %get-tuple-element.22), channel_id=1, source_target_pairs={{0,1},{1,0},{2,3},{3,2},{4,5},{5,4},{6,7},{7,6},{8,9},{9,8},{10,11... | collective-permute-start | bytes 2359304 | tf_op jit(solution)/shard_map/ppermute | solution.py:222
  126.3 7.3 %collective-permute-start.32 = (bf16[48,2048]{1,0:T(8,128)(2,1)S(1)}, bf16[48,2048]{1,0:T(8,128)(2,1)S(1)}, u32[]{:S(2)}, u32[]{:S(2)}) collective-permute-start(bf16[48,2048]{1,0:T(8,128)(2,1)S(1)} %get-tuple-element.35), channel_id=1, source_target_pairs={{0,4},{1,5},{4,8},{5,9},{8,12},{9,13},{12,14},{13,15},{14,10},{15,... | collective-permute-start | bytes 589832 | tf_op jit(solution)/shard_map/ppermute | solution.py:223
  128.3 6.9 %collective-permute-start.36 = (bf16[48,2048]{1,0:T(8,128)(2,1)S(1)}, bf16[48,2048]{1,0:T(8,128)(2,1)S(1)}, u32[]{:S(2)}, u32[]{:S(2)}) collective-permute-start(bf16[48,2048]{1,0:T(8,128)(2,1)S(1)} %get-tuple-element.36), channel_id=1, source_target_pairs={{0,2},{1,3},{4,0},{5,1},{8,4},{9,5},{12,8},{13,9},{14,12},{15,13},... | collective-permute-start | bytes 589832 | tf_op jit(solution)/shard_map/ppermute | solution.py:223
  135.4 10.4 %collective-permute-start.33 = (bf16[96,2048]{1,0:T(8,128)(2,1)S(1)}, bf16[96,2048]{1,0:T(8,128)(2,1)S(1)}, u32[]{:S(2)}, u32[]{:S(2)}) collective-permute-start(bf16[96,2048]{1,0:T(8,128)(2,1)S(1)} %get-tuple-element.31), channel_id=1, source_target_pairs={{0,4},{1,5},{4,8},{5,9},{8,12},{9,13},{12,14},{13,15},{14,10},{15,... | collective-permute-start | bytes 1179656 | tf_op jit(solution)/shard_map/ppermute | solution.py:228
  136.2 10.0 %collective-permute-start.37 = (bf16[96,2048]{1,0:T(8,128)(2,1)S(1)}, bf16[96,2048]{1,0:T(8,128)(2,1)S(1)}, u32[]{:S(2)}, u32[]{:S(2)}) collective-permute-start(bf16[96,2048]{1,0:T(8,128)(2,1)S(1)} %get-tuple-element.32), channel_id=1, source_target_pairs={{0,2},{1,3},{4,0},{5,1},{8,4},{9,5},{12,8},{13,9},{14,12},{15,13},... | collective-permute-start | bytes 1179656 | tf_op jit(solution)/shard_map/ppermute | solution.py:229
  146.4 9.2 %collective-permute-start.34 = (bf16[96,2048]{1,0:T(8,128)(2,1)S(1)}, bf16[96,2048]{1,0:T(8,128)(2,1)S(1)}, u32[]{:S(2)}, u32[]{:S(2)}) collective-permute-start(bf16[96,2048]{1,0:T(8,128)(2,1)S(1)} %get-tuple-element.29), channel_id=1, source_target_pairs={{0,4},{1,5},{4,8},{5,9},{8,12},{9,13},{12,14},{13,15},{14,10},{15,... | collective-permute-start | bytes 1179656 | tf_op jit(solution)/shard_map/ppermute | solution.py:228
  148.0 8.9 %collective-permute-start.38 = (bf16[96,2048]{1,0:T(8,128)(2,1)S(1)}, bf16[96,2048]{1,0:T(8,128)(2,1)S(1)}, u32[]{:S(2)}, u32[]{:S(2)}) collective-permute-start(bf16[96,2048]{1,0:T(8,128)(2,1)S(1)} %get-tuple-element.30), channel_id=1, source_target_pairs={{0,2},{1,3},{4,0},{5,1},{8,4},{9,5},{12,8},{13,9},{14,12},{15,13},... | collective-permute-start | bytes 1179656 | tf_op jit(solution)/shard_map/ppermute | solution.py:229
  148.7 17.7 %copy-start.15 = (f32[96,2048]{1,0:T(8,128)S(1)}, f32[96,2048]{1,0:T(8,128)}, u32[]{:S(2)}) copy-start(f32[96,2048]{1,0:T(8,128)} %copy-done.14) | copy-start | bytes 2359300
  157.0 8.1 %collective-permute-start.35 = (bf16[96,2048]{1,0:T(8,128)(2,1)S(1)}, bf16[96,2048]{1,0:T(8,128)(2,1)S(1)}, u32[]{:S(2)}, u32[]{:S(2)}) collective-permute-start(bf16[96,2048]{1,0:T(8,128)(2,1)S(1)} %get-tuple-element.27), channel_id=1, source_target_pairs={{0,4},{1,5},{4,8},{5,9},{8,12},{9,13},{12,14},{13,15},{14,10},{15,... | collective-permute-start | bytes 1179656 | tf_op jit(solution)/shard_map/ppermute | solution.py:228
  158.5 7.8 %collective-permute-start.39 = (bf16[96,2048]{1,0:T(8,128)(2,1)S(1)}, bf16[96,2048]{1,0:T(8,128)(2,1)S(1)}, u32[]{:S(2)}, u32[]{:S(2)}) collective-permute-start(bf16[96,2048]{1,0:T(8,128)(2,1)S(1)} %get-tuple-element.28), channel_id=1, source_target_pairs={{0,2},{1,3},{4,0},{5,1},{8,4},{9,5},{12,8},{13,9},{14,12},{15,13},... | collective-permute-start | bytes 1179656 | tf_op jit(solution)/shard_map/ppermute | solution.py:229
where the time goes:
time: 168 us; the launch traced here: 167 us
  waiting for transfers between devices  89.1 us (53%)
  starting transfers between devices  36.4 us (22%)
  Pallas kernels  19.3 us (11%)
  local copies, waits for them, and re-layouts  10.1 us (6%)
  other arithmetic  8.24 us (5%)
  matrix products  3.69 us (2%)
    ppermute x4, waiting for transfers between devices, dense(): left = ahead(left)  24.6 us
    ppermute x6, waiting for transfers between devices, dense(): left, right = (ahead(left), back(right))  23.5 us
    ppermute x3, waiting for transfers between devices, dense(): top = ahead((to_ahead + top.astype(jnp.float32)).astype(jnp.bfloat16))  20.9 us
    pallas_call x5, Pallas kernels, serve(): pl.pallas_call(functools.partial(serve_body, columns, len(ins)), out_shap...  19.3 us
    unnamed x65, local copies, waits for them, and re-layouts  7.87 us
    ppermute x6, starting transfers between devices, dense(): left, right = (ahead(left), back(right))  7.26 us
    all_to_all x1, starting transfers between devices, dense(): lax.all_to_all(spread.T, 'dp', split_axis=0, concat_axis=0, tiled=True)  6.36 us
    ppermute x4, starting transfers between devices, dense(): right = back(right)  5.38 us
  transfers between devices with their start and end apart: 41, of which 20 were waited for; matrix products, arithmetic and copies ran while one was open for 8% of the time, Pallas kernels for 12%

commit v1 on v0

--- a/solution.py
+++ b/solution.py
@@ -139,10 +139,10 @@
 VMEM_LIMIT = 24 * 1024 * 1024
 
 
-def around(array, order, spot):
-    ring = jnp.stack([array[chip] for chip in order] * 2)
+def around(array, spot):
+    ring = [array[0::2], array[1::2][::-1]] * 2
     zero = jnp.uint32(0)
-    return lax.dynamic_slice(ring, (spot,) + (zero,) * (array.ndim - 1), array.shape)
+    return lax.dynamic_slice(jnp.concatenate(ring), (spot,) + (zero,) * (array.ndim - 1), array.shape)
 
 
 def dense(
@@ -160,15 +160,44 @@
     chips = n // 2
     far = chips // 2
     rows = merger_input.shape[0]
-    depth, _ = merger_weight.shape
-    order = ring_order(chips)
+    depth, width = merger_weight.shape
+    half = depth // 2
     me = lax.axis_index("dp").astype(jnp.uint32)
-    core = me & 1
+    first_core = (me & 1) == 0
+    first_group = lax.axis_index("groups") == 0
     spot = jnp.where((me & 2) == 0, me >> 2, jnp.uint32(chips - 1) - (me >> 2))
 
     swap = functools.partial(lax.ppermute, axis_name="dp", perm=swap_pairs(n))
+    cross = functools.partial(lax.ppermute, axis_name="groups", perm=swap_pairs(2))
     ahead = functools.partial(lax.ppermute, axis_name="dp", perm=ring_pairs(chips, 1))
     back = functools.partial(lax.ppermute, axis_name="dp", perm=ring_pairs(chips, -1))
+
+    left = right = jnp.where(first_group, merger_weight[:half], merger_weight[half:])
+    act = jax.nn.gelu(merger_input.astype(jnp.float32), approximate=False).astype(jnp.bfloat16)
+    act = act.reshape(rows, chips, 2, 2, half)
+    kept = jnp.where(first_core, act[:, :, 0], act[:, :, 1])
+    given = jnp.where(first_core, act[:, :, 1], act[:, :, 0])
+    act = jnp.concatenate([kept, swap(given)], axis=0)
+    kept = jnp.where(first_group, act[:, :, 0], act[:, :, 1])
+    given = jnp.where(first_group, act[:, :, 1], act[:, :, 0])
+    act = jnp.concatenate([kept, cross(given)], axis=0)
+    act = around(act.transpose(1, 0, 2), spot)
+
+    def term(offset, weight, low, high):
+        return jnp.dot(act[offset % chips][:, low:high], weight, preferred_element_type=jnp.float32)
+
+    total = term(0, left, 0, half)
+    for step in range(1, far):
+        left = ahead(left)
+        right = back(right)
+        total = total + term(-step, left, 0, half) + term(step, right, 0, half)
+    mid = (half + 15) // 16 * 8
+    total = total + term(far, ahead(left[:mid]), 0, mid) + term(far, back(right[mid:]), mid, half)
+    total = total.reshape(4, rows, width)
+    theirs = (total[2] + swap(total[3])).astype(jnp.bfloat16)
+    merged = total[0] + swap(total[1]) + merger_bias + cross(theirs).astype(jnp.float32)
+    scale = lax.rsqrt(jnp.mean(merged * merged, axis=1, keepdims=True) + 1e-06)
+    normed = (merged * scale * norm_gain).astype(jnp.bfloat16)
 
     counts = combine_ints.astype(jnp.float32)
     weights = counts / jnp.sum(counts, axis=1, keepdims=True)
@@ -176,31 +205,8 @@
     spread = jnp.sum(jnp.where(named, weights[:, :, None], 0.0), axis=1)
     share = lax.all_to_all(spread.T, "dp", split_axis=0, concat_axis=0, tiled=True)
     share = share.reshape(chips, 2, rows)
-    share = jnp.where(core == 0, share, share[:, ::-1])
-    share = around(share, order, spot).reshape(n, rows).T
-
-    act = jax.nn.gelu(merger_input.astype(jnp.float32), approximate=False).astype(jnp.bfloat16)
-    act = act.reshape(rows, chips, 2, depth)
-    first, second = act[:, :, 0], act[:, :, 1]
-    kept = jnp.where(core == 0, first, second)
-    given = jnp.where(core == 0, second, first)
-    both = jnp.concatenate([kept, swap(given)], axis=0).transpose(1, 0, 2)
-    both = around(both, order, spot)
-
-    def term(offset, weight, low, high):
-        block = both[offset % chips]
-        return jnp.dot(block[:, low:high], weight, preferred_element_type=jnp.float32)
-
-    left = right = merger_weight
-    total = term(0, merger_weight, 0, depth)
-    for step in range(1, far):
-        left, right = ahead(left), back(right)
-        total = total + term(-step, left, 0, depth) + term(step, right, 0, depth)
-    mid = depth // 2
-    total = total + term(far, ahead(left[:mid]), 0, mid) + term(far, back(right[mid:]), mid, depth)
-    merged = total[:rows] + swap(total[rows:]) + merger_bias
-    scale = lax.rsqrt(jnp.mean(merged * merged, axis=1, keepdims=True) + 1e-06)
-    normed = (merged * scale * norm_gain).astype(jnp.bfloat16)
+    share = jnp.where(first_core, share, share[:, ::-1])
+    share = around(share, spot).reshape(n, rows).T
 
     experts = [w[0] for w in (gate_weight, up_weight, down_weight)]
     cut = rows // 2
@@ -236,7 +242,7 @@
     n = lax.axis_size("dp")
     rows, choose = expert_ids.shape
     capacity = (3 * rows * choose + 2 * n - 1) // (2 * n)
-    if gate_weight.shape[0] == 1 and n % 4 == 0 and n >= 8 and 2 * capacity >= rows:
+    if lax.axis_size("groups") == 2 and gate_weight.shape[0] == 1 and n % 4 == 0 and n >= 8 and 2 * capacity >= rows:
         return dense(*arrays)
     return routed(*arrays)
 

time: 168 us -> 169 us (level)
  waiting for transfers between devices: 89.1 us -> 74.9 us
  blocking collectives: 0 us -> 11.2 us
  matrix products: 3.69 us -> 9.6 us
  starting transfers between devices: 36.4 us -> 32.7 us
  Pallas kernels: 19.3 us -> 21.5 us
    ppermute x4 -> x7, waiting for transfers between devices: 24.6 us -> 0.33 us  [dense(): left = ahead(left)]
    ppermute x4 -> x7, waiting for transfers between devices: 0.01 us -> 22.7 us  [dense(): right = back(right)]
    all_to_all x0 -> x1, blocking collectives: none -> 11.2 us  [dense(): lax.all_to_all(spread.T, 'dp', split_axis=0, concat_axis=0, tiled=True)]
    ppermute x8 -> x5, waiting for transfers between devices: 25.7 us -> 18.2 us  [the longest x1 9.61 us: dense(): cross(theirs).astype(jnp.float32)]
    all_to_all x1 -> x0, starting transfers between devices: 6.36 us -> none  [dense(): lax.all_to_all(spread.T, 'dp', split_axis=0, concat_axis=0, tiled=True)]
    dot_general x9, matrix products: 3.69 us -> 9.6 us  [term(): jnp.dot(act[offset % chips][:, low:high], weight, preferred_element_type=...]
    ppermute x4 -> x7, starting transfers between devices: 5.38 us -> 10.7 us  [dense(): right = back(right)]
    ppermute x8 -> x5, starting transfers between devices: 7.8 us -> 4.21 us  [the longest x1 1.97 us: dense(): act = jnp.concatenate([kept, cross(given)], axis=0)]
  transfers between devices with their start and end apart: 41 -> 43, of which waited for: 20 -> 19; matrix products, arithmetic and copies ran while one was open for 8% -> 8% of each run, Pallas kernels for 12% -> 13%
where the time goes in v1:
time: 169 us; the launch traced here: 168 us
  waiting for transfers between devices  74.9 us (44%)
  starting transfers between devices  32.7 us (19%)
  Pallas kernels  21.5 us (13%)
  blocking collectives  11.2 us (7%)
  matrix products  9.6 us (6%)
  local copies, waits for them, and re-layouts  9.16 us (5%)
  other arithmetic  8.75 us (5%)
    ppermute x7, waiting for transfers between devices, dense(): right = back(right)  22.7 us
    pallas_call x5, Pallas kernels, serve(): pl.pallas_call(functools.partial(serve_body, columns, len(ins)), out_shap...  21.5 us
    ppermute x3, waiting for transfers between devices, dense(): top = ahead((to_ahead + top.astype(jnp.float32)).astype(jnp.bfloat16))  21.1 us
    all_to_all x1, blocking collectives, dense(): lax.all_to_all(spread.T, 'dp', split_axis=0, concat_axis=0, tiled=True)  11.2 us
    ppermute x7, starting transfers between devices, dense(): right = back(right)  10.7 us
    ppermute x1, waiting for transfers between devices, dense(): cross(theirs).astype(jnp.float32)  9.61 us
    dot_general x9, matrix products, term(): jnp.dot(act[offset % chips][:, low:high], weight, preferred_element_type=...  9.6 us
    ppermute x1, waiting for transfers between devices, dense(): act = jnp.concatenate([kept, cross(given)], axis=0)  5.27 us
  transfers between devices with their start and end apart: 43, of which 19 were waited for; matrix products, arithmetic and copies ran while one was open for 8% of the time, Pallas kernels for 13%

profile of v1, /device:TPU:0, one launch (start us, length us, event | category | flops | bytes accessed | tf_op | source)
XLA Modules:
  0.0 168.2 jit_solution(708110304833414825)
XLA Ops:
  0.0 1.1 slice_select_fusion
  1.1 3.0 %collective-permute-start.3 = (bf16[72,2048]{1,0:T(8,128)(2,1)S(1)}, bf16[72,2048]{1,0:T(8,128)(2,1)S(1)}, u32[]{:S(2)}, u32[]{:S(2)}) collective-permute-start(bf16[72,2048]{1,0:T(8,128)(2,1)S(1)} %slice_select_fusion), channel_id=1, source_target_pairs={{0,2},{1,3},{4,0},{5,1},{8,4},{9,5},{12,8},{13,9},{14,12},{15,13},... | collective-permute-start | bytes 884744 | tf_op jit(solution)/shard_map/ppermute | solution.py:192
  4.6 2.6 %fusion.1 = bf16[96,2304]{0,1:T(8,128)(2,1)S(1)} fusion(bf16[96,2304]{0,1:T(8,128)(2,1)S(1)} %copy.36), kind=kLoop, calls=%fused_computation.8 | loop fusion | flops 14598144 | bytes 884736 | tf_op jit(solution)/shard_map/convert_element_type | solution.py:176
  7.4 1.5 collective-permute-done
  9.3 2.0 %collective-permute-start.1 = (bf16[192,8,72]{0,2,1:T(8,128)(2,1)S(1)}, bf16[192,8,72]{0,2,1:T(8,128)(2,1)S(1)}, u32[]{:S(2)}, u32[]{:S(2)}) collective-permute-start(bf16[192,8,72]{0,2,1:T(8,128)(2,1)S(1)} %get-tuple-element.36), channel_id=1, source_target_pairs={{0,16},{16,0},{1,17},{17,1},{2,18},{18,2},{3,19},{19,3},{4,20},{20... | collective-permute-start | bytes 663560 | tf_op jit(solution)/shard_map/ppermute | solution.py:183
  11.3 1.6 collective-permute-start.5
  13.3 5.3 %collective-permute-done.1 = bf16[192,8,72]{0,2,1:T(8,128)(2,1)S(1)} collective-permute-done((bf16[192,8,72]{0,2,1:T(8,128)(2,1)S(1)}, bf16[192,8,72]{0,2,1:T(8,128)(2,1)S(1)}, u32[]{:S(2)}, u32[]{:S(2)}) %collective-permute-start.1) | collective-permute-done | bytes 221216 | tf_op jit(solution)/shard_map/ppermute | solution.py:183
  19.2 0.6 fusion.52
  19.8 0.6 fusion.50
  20.4 0.6 fusion.51
  21.0 1.8 %collective-permute-start.7 = (bf16[72,2048]{1,0:T(8,128)(2,1)S(1)}, bf16[72,2048]{1,0:T(8,128)(2,1)S(1)}, u32[]{:S(2)}, u32[]{:S(2)}) collective-permute-start(bf16[72,2048]{1,0:T(8,128)(2,1)S(1)} %collective-permute-done.5), channel_id=1, source_target_pairs={{0,2},{1,3},{4,0},{5,1},{8,4},{9,5},{12,8},{13,9},{14,12},{15,13},... | collective-permute-start | bytes 884744 | tf_op jit(solution)/shard_map/ppermute | solution.py:192
  22.8 0.6 fusion.48
  23.7 0.6 fusion.49
  24.3 5.1 %collective-permute-done.7 = bf16[72,2048]{1,0:T(8,128)(2,1)S(1)} collective-permute-done((bf16[72,2048]{1,0:T(8,128)(2,1)S(1)}, bf16[72,2048]{1,0:T(8,128)(2,1)S(1)}, u32[]{:S(2)}, u32[]{:S(2)}) %collective-permute-start.7) | collective-permute-done | bytes 294944 | tf_op jit(solution)/shard_map/ppermute | solution.py:192
  29.4 1.6 collective-permute-start.9
  31.4 0.5 collective-permute-start.8
  31.9 0.6 fusion.47
  32.5 2.0 %collective-permute-done.9 = bf16[32,2048]{1,0:T(8,128)(2,1)S(1)} collective-permute-done((bf16[32,2048]{1,0:T(8,128)(2,1)S(1)}, bf16[32,2048]{1,0:T(8,128)(2,1)S(1)}, u32[]{:S(2)}, u32[]{:S(2)}) %collective-permute-start.9) | collective-permute-done | bytes 131104 | tf_op jit(solution)/shard_map/ppermute | solution.py:195
  34.4 0.6 fusion.55
  35.0 1.7 %collective-permute-done.8 = bf16[40,2048]{1,0:T(8,128)(2,1)S(1)} collective-permute-done((bf16[40,2048]{1,0:T(8,128)(2,1)S(1)}, bf16[40,2048]{1,0:T(8,128)(2,1)S(1)}, u32[]{:S(2)}, u32[]{:S(2)}) %collective-permute-start.8) | collective-permute-done | bytes 163872 | tf_op jit(solution)/shard_map/ppermute | solution.py:195
  36.7 2.2 %fusion.53 = f32[384,2048]{1,0:T(8,128)} fusion(bf16[40,2048]{1,0:T(8,128)(2,1)S(1)} %collective-permute-done.8, bf16[384,72]{0,1:T(8,128)(2,1)S(1)} %slice_bitcast_fusion), kind=kOutput, calls=%fused_computation.95 | convolution fusion | flops 62914560 | bytes 3340288 | tf_op jit(solution)/shard_map/dot_general | solution.py:187
  38.9 3.2 %add_add_fusion = f32[384,2048]{1,0:T(8,128)S(1)} fusion(f32[384,2048]{1,0:T(8,128)S(1)} %fusion.55, f32[384,2048]{1,0:T(8,128)} %fusion.53, f32[384,2048]{1,0:T(8,128)S(1)} %fusion.47, f32[384,2048]{1,0:T(8,128)S(1)} %fusion.48, f32[384,2048]{1,0:T(8,128)S(1)} %fusion.49, f32[384,2048]{1,0:T(8,128)S(1)} %fusion.50, f32[384,2048]{1,0:T(8,128)S(1)} %fusion.52, ...), kind=kOutput, calls=%fused_computation | convolution fusion | flops 119537664 | bytes 28661760 | tf_op jit(solution)/shard_map/dot_general | solution.py:187
  42.4 0.5 collective-permute-start.10
  42.9 1.8 %collective-permute-done.11 = f32[96,2048]{1,0:T(8,128)S(1)} collective-permute-done((f32[96,2048]{1,0:T(8,128)S(1)}, f32[96,2048]{1,0:T(8,128)S(1)}, u32[]{:S(2)}, u32[]{:S(2)}) %collective-permute-start.11) | collective-permute-done | bytes 786464 | tf_op jit(solution)/shard_map/ppermute | solution.py:197
  44.8 1.6 collective-permute-start.12
  46.4 9.6 %collective-permute-done.12 = bf16[96,2048]{1,0:T(8,128)(2,1)S(1)} collective-permute-done((bf16[96,2048]{1,0:T(8,128)(2,1)S(1)}, bf16[96,2048]{1,0:T(8,128)(2,1)S(1)}, u32[]{:S(2)}, u32[]{:S(2)}) %collective-permute-start.12) | collective-permute-done | bytes 393248 | tf_op jit(solution)/shard_map/ppermute | solution.py:198
  56.0 1.5 multiply_reduce_fusion
  57.7 1.6 collective-permute-start.16
  59.8 8.4 %collective-permute-done.16.refs_1_ = bf16[96,2048]{1,0:T(8,128)(2,1)} collective-permute-done((bf16[96,2048]{1,0:T(8,128)(2,1)S(1)}, bf16[96,2048]{1,0:T(8,128)(2,1)}, u32[]{:S(2)}, u32[]{:S(2)}) %collective-permute-start.16) | collective-permute-done | bytes 393248 | tf_op jit(solution)/shard_map/ppermute | solution.py:225
  68.2 1.6 collective-permute-start.21
  70.3 11.2 %all_to_all.9 = f32[16,1,96]{2,1,0:T(1,128)S(1)} all-to-all(f32[16,1,96]{2,1,0:T(1,128)S(1)} %bitcast.98), channel_id=1, replica_groups=mesh['groups'=2,'dp'=16] {'dp'}, dimensions={0} | all-to-all | bytes 12288 | tf_op jit(solution)/shard_map/all_to_all | solution.py:206
  81.6 0.6 collective-permute-start.26
  82.2 1.5 collective-permute-start.25
  83.7 0.5 collective-permute-start.17
  84.2 9.2 %collective-permute-done.26.refs_1_ = bf16[96,2048]{1,0:T(8,128)(2,1)} collective-permute-done((bf16[96,2048]{1,0:T(8,128)(2,1)}, bf16[96,2048]{1,0:T(8,128)(2,1)}, u32[]{:S(2)}, u32[]{:S(2)}) %collective-permute-start.26) | collective-permute-done | bytes 393248 | tf_op jit(solution)/shard_map/ppermute | solution.py:225
  93.4 1.6 slice.179
  95.1 0.5 collective-permute-start.31
  95.6 1.6 slice.178
  97.2 1.5 collective-permute-start.30
  98.8 0.7 copy.42
  99.5 1.9 %copy-done.1 = bf16[1,2048,768]{2,1,0:T(8,128)(2,1)S(1)} copy-done((bf16[1,2048,768]{2,1,0:T(8,128)(2,1)S(1)}, bf16[1,2048,768]{2,1,0:T(8,128)(2,1)}, u32[]{:S(2)}) %copy-start.1) | copy-done | bytes 3145752
  101.4 1.9 %copy-done.3 = bf16[1,768,2048]{2,1,0:T(8,128)(2,1)S(1)} copy-done((bf16[1,768,2048]{2,1,0:T(8,128)(2,1)S(1)}, bf16[1,768,2048]{2,1,0:T(8,128)(2,1)}, u32[]{:S(2)}) %copy-start.3) | copy-done | bytes 3145752
  103.3 0.8 copy-done.4
  104.1 3.2 %serve.5 = (bf16[96,2048]{1,0:T(8,128)(2,1)S(1)}, bf16[96,2048]{1,0:T(8,128)(2,1)S(1)}) custom-call(bf16[96,2048]{1,0:T(8,128)(2,1)S(1)} %multiply_convert_fusion.refs_0_, bf16[96,2048]{1,0:T(8,128)(2,1)} %collective-permute-done.13.refs_1_, f32[96,16]{1,0:T(8,128)S(1)} %bitcast.86, bf16[2048,768]{1,0:T(8,128)(2,1)S(1)} %bitcast.71, ...), custom_call_target="tpu_custom_call" | custom-call | flops 1811939328 | bytes 9437184 | tf_op jit(solution)/shard_map/serve/pallas_call | solution.py:125
  108.4 5.2 %serve.6 = (bf16[192,2048]{1,0:T(8,128)(2,1)S(1)}, bf16[192,2048]{1,0:T(8,128)(2,1)S(1)}) custom-call(bf16[96,2048]{1,0:T(8,128)(2,1)} %collective-permute-done.15.refs_0_, bf16[96,2048]{1,0:T(8,128)(2,1)} %collective-permute-done.16.refs_1_, bf16[96,2048]{1,0:T(8,128)(2,1)} %collective-permute-done.17.refs_2_, ...), custom_call_target="tpu_custom_call" | custom-call | flops 3623878656 | bytes 9437184 | tf_op jit(solution)/shard_map/serve/pallas_call | solution.py:125
  114.2 3.0 %serve.9 = (bf16[96,2048]{1,0:T(8,128)(2,1)S(1)}, bf16[96,2048]{1,0:T(8,128)(2,1)S(1)}) custom-call(bf16[48,2048]{1,0:T(8,128)(2,1)} %collective-permute-done.30.refs_0_, bf16[48,2048]{1,0:T(8,128)(2,1)} %collective-permute-done.31.refs_1_, bf16[48,2048]{1,0:T(8,128)(2,1)S(1)} %collective-permute-done.32.refs_2_, ...), custom_call_target="tpu_custom_call" | custom-call | flops 1811939328 | bytes 9437184 | tf_op jit(solution)/shard_map/serve/pallas_call | solution.py:125
  117.8 4.9 %serve.7 = (bf16[192,2048]{1,0:T(8,128)(2,1)S(1)}, bf16[192,2048]{1,0:T(8,128)(2,1)S(1)}) custom-call(bf16[96,2048]{1,0:T(8,128)(2,1)} %collective-permute-done.20.refs_0_, bf16[96,2048]{1,0:T(8,128)(2,1)} %collective-permute-done.21.refs_1_, bf16[96,2048]{1,0:T(8,128)(2,1)S(1)} %collective-permute-done.22.refs_2_, ...), custom_call_target="tpu_custom_call" | custom-call | flops 3623878656 | bytes 9437184 | tf_op jit(solution)/shard_map/serve/pallas_call | solution.py:125
  123.3 5.2 %serve.8 = (bf16[192,2048]{1,0:T(8,128)(2,1)S(1)}, bf16[192,2048]{1,0:T(8,128)(2,1)S(1)}) custom-call(bf16[96,2048]{1,0:T(8,128)(2,1)} %collective-permute-done.25.refs_0_, bf16[96,2048]{1,0:T(8,128)(2,1)} %collective-permute-done.26.refs_1_, bf16[96,2048]{1,0:T(8,128)(2,1)S(1)} %collective-permute-done.27.refs_2_, ...), custom_call_target="tpu_custom_call" | custom-call | flops 3623878656 | bytes 9437184 | tf_op jit(solution)/shard_map/serve/pallas_call | solution.py:125
  128.8 0.6 collective-permute-start.35
  129.3 1.5 collective-permute-done.29
  130.8 0.5 collective-permute-start.39
  131.5 4.5 %collective-permute-done.35 = bf16[48,2048]{1,0:T(8,128)(2,1)S(1)} collective-permute-done((bf16[48,2048]{1,0:T(8,128)(2,1)S(1)}, bf16[48,2048]{1,0:T(8,128)(2,1)S(1)}, u32[]{:S(2)}, u32[]{:S(2)}) %collective-permute-start.35) | collective-permute-done | bytes 196640 | tf_op jit(solution)/shard_map/ppermute | solution.py:229
  136.1 1.7 %collective-permute-done.39 = bf16[48,2048]{1,0:T(8,128)(2,1)S(1)} collective-permute-done((bf16[48,2048]{1,0:T(8,128)(2,1)S(1)}, bf16[48,2048]{1,0:T(8,128)(2,1)S(1)}, u32[]{:S(2)}, u32[]{:S(2)}) %collective-permute-start.39) | collective-permute-done | bytes 196640 | tf_op jit(solution)/shard_map/ppermute | solution.py:229
  137.9 0.6 collective-permute-start.36
  138.5 1.5 collective-permute-start.40
  140.2 8.0 %collective-permute-done.36 = bf16[96,2048]{1,0:T(8,128)(2,1)S(1)} collective-permute-done((bf16[96,2048]{1,0:T(8,128)(2,1)S(1)}, bf16[96,2048]{1,0:T(8,128)(2,1)S(1)}, u32[]{:S(2)}, u32[]{:S(2)}) %collective-permute-start.36) | collective-permute-done | bytes 393248 | tf_op jit(solution)/shard_map/ppermute | solution.py:234
  148.7 0.6 collective-permute-start.37
  149.3 1.4 collective-permute-start.41
  151.0 7.0 %collective-permute-done.37 = bf16[96,2048]{1,0:T(8,128)(2,1)S(1)} collective-permute-done((bf16[96,2048]{1,0:T(8,128)(2,1)S(1)}, bf16[96,2048]{1,0:T(8,128)(2,1)S(1)}, u32[]{:S(2)}, u32[]{:S(2)}) %collective-permute-start.37) | collective-permute-done | bytes 393248 | tf_op jit(solution)/shard_map/ppermute | solution.py:234
  158.4 1.1 collective-permute-start.38
  159.5 1.0 collective-permute-start.42
  160.5 6.1 %collective-permute-done.38 = bf16[96,2048]{1,0:T(8,128)(2,1)S(1)} collective-permute-done((bf16[96,2048]{1,0:T(8,128)(2,1)S(1)}, bf16[96,2048]{1,0:T(8,128)(2,1)S(1)}, u32[]{:S(2)}, u32[]{:S(2)}) %collective-permute-start.38) | collective-permute-done | bytes 393248 | tf_op jit(solution)/shard_map/ppermute | solution.py:234
  166.6 0.7 collective-permute-done.42
  167.2 1.0 add_convert_fusion
  (103 shorter events, 8.9 us)
Async XLA Ops:
  0.0 4.3 %copy-start.9 = (bf16[96,2304]{1,0:T(8,128)(2,1)S(1)}, bf16[96,2304]{1,0:T(8,128)(2,1)}, u32[]{:S(2)}) copy-start(bf16[96,2304]{1,0:T(8,128)(2,1)} %param.9) | copy-start | bytes 1327108
  1.1 10.1 %collective-permute-start.3 = (bf16[72,2048]{1,0:T(8,128)(2,1)S(1)}, bf16[72,2048]{1,0:T(8,128)(2,1)S(1)}, u32[]{:S(2)}, u32[]{:S(2)}) collective-permute-start(bf16[72,2048]{1,0:T(8,128)(2,1)S(1)} %slice_select_fusion), channel_id=1, source_target_pairs={{0,2},{1,3},{4,0},{5,1},{8,4},{9,5},{12,8},{13,9},{14,12},{15,13},... | collective-permute-start | bytes 884744 | tf_op jit(solution)/shard_map/ppermute | solution.py:192
  4.2 8.8 %collective-permute-start.2 = (bf16[72,2048]{1,0:T(8,128)(2,1)S(1)}, bf16[72,2048]{1,0:T(8,128)(2,1)S(1)}, u32[]{:S(2)}, u32[]{:S(2)}) collective-permute-start(bf16[72,2048]{1,0:T(8,128)(2,1)S(1)} %slice_select_fusion), channel_id=1, source_target_pairs={{0,4},{1,5},{4,8},{5,9},{8,12},{9,13},{12,14},{13,15},{14,10},{15,... | collective-permute-start | bytes 884744 | tf_op jit(solution)/shard_map/ppermute | solution.py:191
  7.3 1.6 collective-permute-start
  9.3 9.3 %collective-permute-start.1 = (bf16[192,8,72]{0,2,1:T(8,128)(2,1)S(1)}, bf16[192,8,72]{0,2,1:T(8,128)(2,1)S(1)}, u32[]{:S(2)}, u32[]{:S(2)}) collective-permute-start(bf16[192,8,72]{0,2,1:T(8,128)(2,1)S(1)} %get-tuple-element.36), channel_id=1, source_target_pairs={{0,16},{16,0},{1,17},{17,1},{2,18},{18,2},{3,19},{19,3},{4,20},{20... | collective-permute-start | bytes 663560 | tf_op jit(solution)/shard_map/ppermute | solution.py:183
  11.3 9.7 %collective-permute-start.5 = (bf16[72,2048]{1,0:T(8,128)(2,1)S(1)}, bf16[72,2048]{1,0:T(8,128)(2,1)S(1)}, u32[]{:S(2)}, u32[]{:S(2)}) collective-permute-start(bf16[72,2048]{1,0:T(8,128)(2,1)S(1)} %collective-permute-done.3), channel_id=1, source_target_pairs={{0,2},{1,3},{4,0},{5,1},{8,4},{9,5},{12,8},{13,9},{14,12},{15,13},... | collective-permute-start | bytes 884744 | tf_op jit(solution)/shard_map/ppermute | solution.py:192
  12.9 10.5 %collective-permute-start.4 = (bf16[72,2048]{1,0:T(8,128)(2,1)S(1)}, bf16[72,2048]{1,0:T(8,128)(2,1)S(1)}, u32[]{:S(2)}, u32[]{:S(2)}) collective-permute-start(bf16[72,2048]{1,0:T(8,128)(2,1)S(1)} %collective-permute-done.2), channel_id=1, source_target_pairs={{0,4},{1,5},{4,8},{5,9},{8,12},{9,13},{12,14},{13,15},{14,10},{15,... | collective-permute-start | bytes 884744 | tf_op jit(solution)/shard_map/ppermute | solution.py:191
  21.0 8.4 %collective-permute-start.7 = (bf16[72,2048]{1,0:T(8,128)(2,1)S(1)}, bf16[72,2048]{1,0:T(8,128)(2,1)S(1)}, u32[]{:S(2)}, u32[]{:S(2)}) collective-permute-start(bf16[72,2048]{1,0:T(8,128)(2,1)S(1)} %collective-permute-done.5), channel_id=1, source_target_pairs={{0,2},{1,3},{4,0},{5,1},{8,4},{9,5},{12,8},{13,9},{14,12},{15,13},... | collective-permute-start | bytes 884744 | tf_op jit(solution)/shard_map/ppermute | solution.py:192
  23.4 8.0 %collective-permute-start.6 = (bf16[72,2048]{1,0:T(8,128)(2,1)S(1)}, bf16[72,2048]{1,0:T(8,128)(2,1)S(1)}, u32[]{:S(2)}, u32[]{:S(2)}) collective-permute-start(bf16[72,2048]{1,0:T(8,128)(2,1)S(1)} %collective-permute-done.4), channel_id=1, source_target_pairs={{0,4},{1,5},{4,8},{5,9},{8,12},{9,13},{12,14},{13,15},{14,10},{15,... | collective-permute-start | bytes 884744 | tf_op jit(solution)/shard_map/ppermute | solution.py:191
  29.4 5.0 %collective-permute-start.9 = (bf16[32,2048]{1,0:T(8,128)(2,1)S(1)}, bf16[32,2048]{1,0:T(8,128)(2,1)S(1)}, u32[]{:S(2)}, u32[]{:S(2)}) collective-permute-start(bf16[32,2048]{1,0:T(8,128)(2,1)S(1)} %slice.170), channel_id=1, source_target_pairs={{0,2},{1,3},{4,0},{5,1},{8,4},{9,5},{12,8},{13,9},{14,12},{15,13},... | collective-permute-start | bytes 393224 | tf_op jit(solution)/shard_map/ppermute | solution.py:195
  31.4 5.4 %collective-permute-start.8 = (bf16[40,2048]{1,0:T(8,128)(2,1)S(1)}, bf16[40,2048]{1,0:T(8,128)(2,1)S(1)}, u32[]{:S(2)}, u32[]{:S(2)}) collective-permute-start(bf16[40,2048]{1,0:T(8,128)(2,1)S(1)} %slice.168), channel_id=1, source_target_pairs={{0,4},{1,5},{4,8},{5,9},{8,12},{9,13},{12,14},{13,15},{14,10},{15,... | collective-permute-start | bytes 491528 | tf_op jit(solution)/shard_map/ppermute | solution.py:195
  42.2 4.2 %copy-start.6 = (f32[384,2048]{1,0:T(8,128)}, f32[384,2048]{1,0:T(8,128)S(1)}, u32[]{:S(2)}) copy-start(f32[384,2048]{1,0:T(8,128)S(1)} %add_add_fusion) | copy-start | bytes 9437188
  42.3 13.7 %copy-start.11 = (f32[2048]{0:T(1024)S(1)}, f32[2048]{0:T(1024)}, u32[]{:S(2)}) copy-start(f32[2048]{0:T(1024)} %param.11) | copy-start | bytes 24580
  42.3 2.4 %collective-permute-start.11 = (f32[96,2048]{1,0:T(8,128)S(1)}, f32[96,2048]{1,0:T(8,128)S(1)}, u32[]{:S(2)}, u32[]{:S(2)}) collective-permute-start(f32[96,2048]{1,0:T(8,128)S(1)} %get-tuple-element.28), channel_id=1, source_target_pairs={{0,1},{1,0},{2,3},{3,2},{4,5},{5,4},{6,7},{7,6},{8,9},{9,8},{10,11... | collective-permute-start | bytes 2359304 | tf_op jit(solution)/shard_map/ppermute | solution.py:197
  42.4 4.0 %collective-permute-start.10 = (f32[96,2048]{1,0:T(8,128)S(1)}, f32[96,2048]{1,0:T(8,128)S(1)}, u32[]{:S(2)}, u32[]{:S(2)}) collective-permute-start(f32[96,2048]{1,0:T(8,128)S(1)} %get-tuple-element.27), channel_id=1, source_target_pairs={{0,1},{1,0},{2,3},{3,2},{4,5},{5,4},{6,7},{7,6},{8,9},{9,8},{10,11... | collective-permute-start | bytes 2359304 | tf_op jit(solution)/shard_map/ppermute | solution.py:198
  44.7 12.8 %copy-start.12 = (f32[2048]{0:T(1024)S(1)}, f32[2048]{0:T(1024)}, u32[]{:S(2)}) copy-start(f32[2048]{0:T(1024)} %param.12) | copy-start | bytes 24580
  44.8 11.2 %collective-permute-start.12 = (bf16[96,2048]{1,0:T(8,128)(2,1)S(1)}, bf16[96,2048]{1,0:T(8,128)(2,1)S(1)}, u32[]{:S(2)}, u32[]{:S(2)}) collective-permute-start(bf16[96,2048]{1,0:T(8,128)(2,1)S(1)} %fusion.37), channel_id=1, source_target_pairs={{0,16},{16,0},{1,17},{17,1},{2,18},{18,2},{3,19},{19,3},{4,20},{20... | collective-permute-start | bytes 1179656 | tf_op jit(solution)/shard_map/ppermute | solution.py:198
  56.0 43.5 %copy-start = (bf16[1,2048,768]{2,1,0:T(8,128)(2,1)S(1)}, bf16[1,2048,768]{2,1,0:T(8,128)(2,1)}, u32[]{:S(2)}) copy-start(bf16[1,2048,768]{2,1,0:T(8,128)(2,1)} %param.13) | copy-start | bytes 9437188
  57.5 12.2 %copy-start.7 = (f32[96,2048]{1,0:T(8,128)}, f32[96,2048]{1,0:T(8,128)S(1)}, u32[]{:S(2)}) copy-start(f32[96,2048]{1,0:T(8,128)S(1)} %get-tuple-element.26) | copy-start | bytes 2359300
  57.5 12.7 %copy-start.10 = (s32[96,8]{0,1:T(8,128)S(1)}, s32[96,8]{0,1:T(8,128)}, u32[]{:S(2)}) copy-start(s32[96,8]{0,1:T(8,128)} %param.17) | copy-start | bytes 9220
  57.5 12.7 %copy-start.13 = (s32[96,8]{0,1:T(8,128)S(1)}, s32[96,8]{0,1:T(8,128)}, u32[]{:S(2)}) copy-start(s32[96,8]{0,1:T(8,128)} %param.16) | copy-start | bytes 9220
  57.7 10.5 %collective-permute-start.16 = (bf16[96,2048]{1,0:T(8,128)(2,1)S(1)}, bf16[96,2048]{1,0:T(8,128)(2,1)}, u32[]{:S(2)}, u32[]{:S(2)}) collective-permute-start(bf16[96,2048]{1,0:T(8,128)(2,1)S(1)} %multiply_convert_fusion.refs_0_), channel_id=1, source_target_pairs={{0,2},{1,3},{4,0},{5,1},{8,4},{9,5},{12,8},{13,9},{14,12},{15,13},... | collective-permute-start | bytes 1179656 | tf_op jit(solution)/shard_map/ppermute | solution.py:225
  59.4 10.4 %collective-permute-start.15 = (bf16[96,2048]{1,0:T(8,128)(2,1)S(1)}, bf16[96,2048]{1,0:T(8,128)(2,1)}, u32[]{:S(2)}, u32[]{:S(2)}) collective-permute-start(bf16[96,2048]{1,0:T(8,128)(2,1)S(1)} %multiply_convert_fusion.refs_0_), channel_id=1, source_target_pairs={{0,4},{1,5},{4,8},{5,9},{8,12},{9,13},{12,14},{13,15},{14,10},{15,... | collective-permute-start | bytes 1179656 | tf_op jit(solution)/shard_map/ppermute | solution.py:224
  68.2 13.4 %collective-permute-start.21 = (bf16[96,2048]{1,0:T(8,128)(2,1)}, bf16[96,2048]{1,0:T(8,128)(2,1)}, u32[]{:S(2)}, u32[]{:S(2)}) collective-permute-start(bf16[96,2048]{1,0:T(8,128)(2,1)} %collective-permute-done.16.refs_1_), channel_id=1, source_target_pairs={{0,2},{1,3},{4,0},{5,1},{8,4},{9,5},{12,8},{13,9},{14,12},{15,13},... | collective-permute-start | bytes 1179656 | tf_op jit(solution)/shard_map/ppermute | solution.py:225
  69.8 12.4 %collective-permute-start.20 = (bf16[96,2048]{1,0:T(8,128)(2,1)}, bf16[96,2048]{1,0:T(8,128)(2,1)}, u32[]{:S(2)}, u32[]{:S(2)}) collective-permute-start(bf16[96,2048]{1,0:T(8,128)(2,1)} %collective-permute-done.15.refs_0_), channel_id=1, source_target_pairs={{0,4},{1,5},{4,8},{5,9},{8,12},{9,13},{12,14},{13,15},{14,10},{15,... | collective-permute-start | bytes 1179656 | tf_op jit(solution)/shard_map/ppermute | solution.py:224
  81.5 18.0 %collective-permute-start.13 = (bf16[96,2048]{1,0:T(8,128)(2,1)S(1)}, bf16[96,2048]{1,0:T(8,128)(2,1)}, u32[]{:S(2)}, u32[]{:S(2)}) collective-permute-start(bf16[96,2048]{1,0:T(8,128)(2,1)S(1)} %multiply_convert_fusion.refs_0_), channel_id=1, source_target_pairs={{0,1},{1,0},{2,3},{3,2},{4,5},{5,4},{6,7},{7,6},{8,9},{9,8},{10,11... | collective-permute-start | bytes 1179656 | tf_op jit(solution)/shard_map/ppermute | solution.py:214
  81.6 11.8 %collective-permute-start.26 = (bf16[96,2048]{1,0:T(8,128)(2,1)}, bf16[96,2048]{1,0:T(8,128)(2,1)}, u32[]{:S(2)}, u32[]{:S(2)}) collective-permute-start(bf16[96,2048]{1,0:T(8,128)(2,1)} %collective-permute-done.21.refs_1_), channel_id=1, source_target_pairs={{0,2},{1,3},{4,0},{5,1},{8,4},{9,5},{12,8},{13,9},{14,12},{15,13},... | collective-permute-start | bytes 1179656 | tf_op jit(solution)/shard_map/ppermute | solution.py:225
  82.2 13.4 %collective-permute-start.25 = (bf16[96,2048]{1,0:T(8,128)(2,1)}, bf16[96,2048]{1,0:T(8,128)(2,1)}, u32[]{:S(2)}, u32[]{:S(2)}) collective-permute-start(bf16[96,2048]{1,0:T(8,128)(2,1)} %collective-permute-done.20.refs_0_), channel_id=1, source_target_pairs={{0,4},{1,5},{4,8},{5,9},{8,12},{9,13},{12,14},{13,15},{14,10},{15,... | collective-permute-start | bytes 1179656 | tf_op jit(solution)/shard_map/ppermute | solution.py:224
  83.7 23.6 %collective-permute-start.18 = (bf16[96,2048]{1,0:T(8,128)(2,1)}, bf16[96,2048]{1,0:T(8,128)(2,1)}, u32[]{:S(2)}, u32[]{:S(2)}) collective-permute-start(bf16[96,2048]{1,0:T(8,128)(2,1)} %collective-permute-done.16.refs_1_), channel_id=1, source_target_pairs={{0,1},{1,0},{2,3},{3,2},{4,5},{5,4},{6,7},{7,6},{8,9},{9,8},{10,11... | collective-permute-start | bytes 1179656 | tf_op jit(solution)/shard_map/ppermute | solution.py:226
  83.7 24.1 %collective-permute-start.17 = (bf16[96,2048]{1,0:T(8,128)(2,1)}, bf16[96,2048]{1,0:T(8,128)(2,1)}, u32[]{:S(2)}, u32[]{:S(2)}) collective-permute-start(bf16[96,2048]{1,0:T(8,128)(2,1)} %collective-permute-done.15.refs_0_), channel_id=1, source_target_pairs={{0,1},{1,0},{2,3},{3,2},{4,5},{5,4},{6,7},{7,6},{8,9},{9,8},{10,11... | collective-permute-start | bytes 1179656 | tf_op jit(solution)/shard_map/ppermute | solution.py:226
  95.1 12.8 %collective-permute-start.31 = (bf16[48,2048]{1,0:T(8,128)(2,1)}, bf16[48,2048]{1,0:T(8,128)(2,1)}, u32[]{:S(2)}, u32[]{:S(2)}) collective-permute-start(bf16[48,2048]{1,0:T(8,128)(2,1)} %slice.179), channel_id=1, source_target_pairs={{0,2},{1,3},{4,0},{5,1},{8,4},{9,5},{12,8},{13,9},{14,12},{15,13},... | collective-permute-start | bytes 589832 | tf_op jit(solution)/shard_map/ppermute | solution.py:225
  97.2 11.1 %collective-permute-start.30 = (bf16[48,2048]{1,0:T(8,128)(2,1)}, bf16[48,2048]{1,0:T(8,128)(2,1)}, u32[]{:S(2)}, u32[]{:S(2)}) collective-permute-start(bf16[48,2048]{1,0:T(8,128)(2,1)} %slice.178), channel_id=1, source_target_pairs={{0,4},{1,5},{4,8},{5,9},{8,12},{9,13},{12,14},{13,15},{14,10},{15,... | collective-permute-start | bytes 589832 | tf_op jit(solution)/shard_map/ppermute | solution.py:224
  99.5 1.9 %copy-start.1 = (bf16[1,2048,768]{2,1,0:T(8,128)(2,1)S(1)}, bf16[1,2048,768]{2,1,0:T(8,128)(2,1)}, u32[]{:S(2)}) copy-start(bf16[1,2048,768]{2,1,0:T(8,128)(2,1)} %param.14) | copy-start | bytes 9437188
  101.4 1.9 %copy-start.3 = (bf16[1,768,2048]{2,1,0:T(8,128)(2,1)S(1)}, bf16[1,768,2048]{2,1,0:T(8,128)(2,1)}, u32[]{:S(2)}) copy-start(bf16[1,768,2048]{2,1,0:T(8,128)(2,1)} %param.15) | copy-start | bytes 9437188
  103.3 0.8 copy-start.4
  104.1 4.4 %copy-start.2 = (bf16[1,2048,768]{2,1,0:T(8,128)(2,1)S(1)}, bf16[1,2048,768]{2,1,0:T(8,128)(2,1)}, u32[]{:S(2)}) copy-start(bf16[1,2048,768]{2,1,0:T(8,128)(2,1)} %param.14) | copy-start | bytes 9437188
  104.1 4.4 %copy-start.5 = (f32[16,96]{0,1:T(8,128)S(1)}, f32[16,96]{0,1:T(8,128)}, u32[]{:S(2)}) copy-start(f32[16,96]{0,1:T(8,128)} %copy.42) | copy-start | bytes 18436
  107.2 53.2 %collective-permute-start.14 = (bf16[96,2048]{1,0:T(8,128)(2,1)S(1)}, bf16[96,2048]{1,0:T(8,128)(2,1)S(1)}, u32[]{:S(2)}, u32[]{:S(2)}) collective-permute-start(bf16[96,2048]{1,0:T(8,128)(2,1)S(1)} %get-tuple-element.16), channel_id=1, source_target_pairs={{0,1},{1,0},{2,3},{3,2},{4,5},{5,4},{6,7},{7,6},{8,9},{9,8},{10,11... | collective-permute-start | bytes 1179656 | tf_op jit(solution)/shard_map/ppermute | solution.py:228
  107.3 9.9 %collective-permute-start.23 = (bf16[96,2048]{1,0:T(8,128)(2,1)}, bf16[96,2048]{1,0:T(8,128)(2,1)S(1)}, u32[]{:S(2)}, u32[]{:S(2)}) collective-permute-start(bf16[96,2048]{1,0:T(8,128)(2,1)} %collective-permute-done.21.refs_1_), channel_id=1, source_target_pairs={{0,1},{1,0},{2,3},{3,2},{4,5},{5,4},{6,7},{7,6},{8,9},{9,8},{10,11... | collective-permute-start | bytes 1179656 | tf_op jit(solution)/shard_map/ppermute | solution.py:226
  107.8 9.9 %collective-permute-start.22 = (bf16[96,2048]{1,0:T(8,128)(2,1)}, bf16[96,2048]{1,0:T(8,128)(2,1)S(1)}, u32[]{:S(2)}, u32[]{:S(2)}) collective-permute-start(bf16[96,2048]{1,0:T(8,128)(2,1)} %collective-permute-done.20.refs_0_), channel_id=1, source_target_pairs={{0,1},{1,0},{2,3},{3,2},{4,5},{5,4},{6,7},{7,6},{8,9},{9,8},{10,11... | collective-permute-start | bytes 1179656 | tf_op jit(solution)/shard_map/ppermute | solution.py:226
  107.9 5.7 %collective-permute-start.33 = (bf16[48,2048]{1,0:T(8,128)(2,1)}, bf16[48,2048]{1,0:T(8,128)(2,1)S(1)}, u32[]{:S(2)}, u32[]{:S(2)}) collective-permute-start(bf16[48,2048]{1,0:T(8,128)(2,1)} %collective-permute-done.31.refs_1_), channel_id=1, source_target_pairs={{0,1},{1,0},{2,3},{3,2},{4,5},{5,4},{6,7},{7,6},{8,9},{9,8},{10,11... | collective-permute-start | bytes 589832 | tf_op jit(solution)/shard_map/ppermute | solution.py:226
  108.3 5.8 %collective-permute-start.32 = (bf16[48,2048]{1,0:T(8,128)(2,1)}, bf16[48,2048]{1,0:T(8,128)(2,1)S(1)}, u32[]{:S(2)}, u32[]{:S(2)}) collective-permute-start(bf16[48,2048]{1,0:T(8,128)(2,1)} %collective-permute-done.30.refs_0_), channel_id=1, source_target_pairs={{0,1},{1,0},{2,3},{3,2},{4,5},{5,4},{6,7},{7,6},{8,9},{9,8},{10,11... | collective-permute-start | bytes 589832 | tf_op jit(solution)/shard_map/ppermute | solution.py:226
  113.6 9.2 %collective-permute-start.28 = (bf16[96,2048]{1,0:T(8,128)(2,1)}, bf16[96,2048]{1,0:T(8,128)(2,1)S(1)}, u32[]{:S(2)}, u32[]{:S(2)}) collective-permute-start(bf16[96,2048]{1,0:T(8,128)(2,1)} %collective-permute-done.26.refs_1_), channel_id=1, source_target_pairs={{0,1},{1,0},{2,3},{3,2},{4,5},{5,4},{6,7},{7,6},{8,9},{9,8},{10,11... | collective-permute-start | bytes 1179656 | tf_op jit(solution)/shard_map/ppermute | solution.py:226
  114.1 9.2 %collective-permute-start.27 = (bf16[96,2048]{1,0:T(8,128)(2,1)}, bf16[96,2048]{1,0:T(8,128)(2,1)S(1)}, u32[]{:S(2)}, u32[]{:S(2)}) collective-permute-start(bf16[96,2048]{1,0:T(8,128)(2,1)} %collective-permute-done.25.refs_0_), channel_id=1, source_target_pairs={{0,1},{1,0},{2,3},{3,2},{4,5},{5,4},{6,7},{7,6},{8,9},{9,8},{10,11... | collective-permute-start | bytes 1179656 | tf_op jit(solution)/shard_map/ppermute | solution.py:226
  117.3 33.5 %collective-permute-start.19 = (bf16[192,2048]{1,0:T(8,128)(2,1)S(1)}, bf16[192,2048]{1,0:T(8,128)(2,1)S(1)}, u32[]{:S(2)}, u32[]{:S(2)}) collective-permute-start(bf16[192,2048]{1,0:T(8,128)(2,1)S(1)} %get-tuple-element.18), channel_id=1, source_target_pairs={{0,1},{1,0},{2,3},{3,2},{4,5},{5,4},{6,7},{7,6},{8,9},{9,8},{10,11... | collective-permute-start | bytes 2359304 | tf_op jit(solution)/shard_map/ppermute | solution.py:228
  117.7 10.9 %collective-permute-start.34 = (bf16[96,2048]{1,0:T(8,128)(2,1)S(1)}, bf16[96,2048]{1,0:T(8,128)(2,1)S(1)}, u32[]{:S(2)}, u32[]{:S(2)}) collective-permute-start(bf16[96,2048]{1,0:T(8,128)(2,1)S(1)} %get-tuple-element.24), channel_id=1, source_target_pairs={{0,1},{1,0},{2,3},{3,2},{4,5},{5,4},{6,7},{7,6},{8,9},{9,8},{10,11... | collective-permute-start | bytes 1179656 | tf_op jit(solution)/shard_map/ppermute | solution.py:228
  122.8 17.2 %collective-permute-start.24 = (bf16[192,2048]{1,0:T(8,128)(2,1)S(1)}, bf16[192,2048]{1,0:T(8,128)(2,1)S(1)}, u32[]{:S(2)}, u32[]{:S(2)}) collective-permute-start(bf16[192,2048]{1,0:T(8,128)(2,1)S(1)} %get-tuple-element.20), channel_id=1, source_target_pairs={{0,1},{1,0},{2,3},{3,2},{4,5},{5,4},{6,7},{7,6},{8,9},{9,8},{10,11... | collective-permute-start | bytes 2359304 | tf_op jit(solution)/shard_map/ppermute | solution.py:228
  128.5 2.4 %collective-permute-start.29 = (bf16[192,2048]{1,0:T(8,128)(2,1)S(1)}, bf16[192,2048]{1,0:T(8,128)(2,1)S(1)}, u32[]{:S(2)}, u32[]{:S(2)}) collective-permute-start(bf16[192,2048]{1,0:T(8,128)(2,1)S(1)} %get-tuple-element.22), channel_id=1, source_target_pairs={{0,1},{1,0},{2,3},{3,2},{4,5},{5,4},{6,7},{7,6},{8,9},{9,8},{10,11... | collective-permute-start | bytes 2359304 | tf_op jit(solution)/shard_map/ppermute | solution.py:228
  128.8 7.3 %collective-permute-start.35 = (bf16[48,2048]{1,0:T(8,128)(2,1)S(1)}, bf16[48,2048]{1,0:T(8,128)(2,1)S(1)}, u32[]{:S(2)}, u32[]{:S(2)}) collective-permute-start(bf16[48,2048]{1,0:T(8,128)(2,1)S(1)} %get-tuple-element.39), channel_id=1, source_target_pairs={{0,4},{1,5},{4,8},{5,9},{8,12},{9,13},{12,14},{13,15},{14,10},{15,... | collective-permute-start | bytes 589832 | tf_op jit(solution)/shard_map/ppermute | solution.py:229
  130.8 6.9 %collective-permute-start.39 = (bf16[48,2048]{1,0:T(8,128)(2,1)S(1)}, bf16[48,2048]{1,0:T(8,128)(2,1)S(1)}, u32[]{:S(2)}, u32[]{:S(2)}) collective-permute-start(bf16[48,2048]{1,0:T(8,128)(2,1)S(1)} %get-tuple-element.40), channel_id=1, source_target_pairs={{0,2},{1,3},{4,0},{5,1},{8,4},{9,5},{12,8},{13,9},{14,12},{15,13},... | collective-permute-start | bytes 589832 | tf_op jit(solution)/shard_map/ppermute | solution.py:229
  137.9 10.4 %collective-permute-start.36 = (bf16[96,2048]{1,0:T(8,128)(2,1)S(1)}, bf16[96,2048]{1,0:T(8,128)(2,1)S(1)}, u32[]{:S(2)}, u32[]{:S(2)}) collective-permute-start(bf16[96,2048]{1,0:T(8,128)(2,1)S(1)} %get-tuple-element.33), channel_id=1, source_target_pairs={{0,4},{1,5},{4,8},{5,9},{8,12},{9,13},{12,14},{13,15},{14,10},{15,... | collective-permute-start | bytes 1179656 | tf_op jit(solution)/shard_map/ppermute | solution.py:234
  138.5 10.0 %collective-permute-start.40 = (bf16[96,2048]{1,0:T(8,128)(2,1)S(1)}, bf16[96,2048]{1,0:T(8,128)(2,1)S(1)}, u32[]{:S(2)}, u32[]{:S(2)}) collective-permute-start(bf16[96,2048]{1,0:T(8,128)(2,1)S(1)} %get-tuple-element.34), channel_id=1, source_target_pairs={{0,2},{1,3},{4,0},{5,1},{8,4},{9,5},{12,8},{13,9},{14,12},{15,13},... | collective-permute-start | bytes 1179656 | tf_op jit(solution)/shard_map/ppermute | solution.py:235
  148.7 9.3 %collective-permute-start.37 = (bf16[96,2048]{1,0:T(8,128)(2,1)S(1)}, bf16[96,2048]{1,0:T(8,128)(2,1)S(1)}, u32[]{:S(2)}, u32[]{:S(2)}) collective-permute-start(bf16[96,2048]{1,0:T(8,128)(2,1)S(1)} %get-tuple-element.31), channel_id=1, source_target_pairs={{0,4},{1,5},{4,8},{5,9},{8,12},{9,13},{12,14},{13,15},{14,10},{15,... | collective-permute-start | bytes 1179656 | tf_op jit(solution)/shard_map/ppermute | solution.py:234
  149.3 8.9 %collective-permute-start.41 = (bf16[96,2048]{1,0:T(8,128)(2,1)S(1)}, bf16[96,2048]{1,0:T(8,128)(2,1)S(1)}, u32[]{:S(2)}, u32[]{:S(2)}) collective-permute-start(bf16[96,2048]{1,0:T(8,128)(2,1)S(1)} %get-tuple-element.32), channel_id=1, source_target_pairs={{0,2},{1,3},{4,0},{5,1},{8,4},{9,5},{12,8},{13,9},{14,12},{15,13},... | collective-permute-start | bytes 1179656 | tf_op jit(solution)/shard_map/ppermute | solution.py:235
  151.0 16.3 %copy-start.8 = (f32[96,2048]{1,0:T(8,128)S(1)}, f32[96,2048]{1,0:T(8,128)}, u32[]{:S(2)}) copy-start(f32[96,2048]{1,0:T(8,128)} %copy-done.7) | copy-start | bytes 2359300
  158.4 8.2 %collective-permute-start.38 = (bf16[96,2048]{1,0:T(8,128)(2,1)S(1)}, bf16[96,2048]{1,0:T(8,128)(2,1)S(1)}, u32[]{:S(2)}, u32[]{:S(2)}) collective-permute-start(bf16[96,2048]{1,0:T(8,128)(2,1)S(1)} %get-tuple-element.29), channel_id=1, source_target_pairs={{0,4},{1,5},{4,8},{5,9},{8,12},{9,13},{12,14},{13,15},{14,10},{15,... | collective-permute-start | bytes 1179656 | tf_op jit(solution)/shard_map/ppermute | solution.py:234
  159.5 7.8 %collective-permute-start.42 = (bf16[96,2048]{1,0:T(8,128)(2,1)S(1)}, bf16[96,2048]{1,0:T(8,128)(2,1)S(1)}, u32[]{:S(2)}, u32[]{:S(2)}) collective-permute-start(bf16[96,2048]{1,0:T(8,128)(2,1)S(1)} %get-tuple-element.30), channel_id=1, source_target_pairs={{0,2},{1,3},{4,0},{5,1},{8,4},{9,5},{12,8},{13,9},{14,12},{15,13},... | collective-permute-start | bytes 1179656 | tf_op jit(solution)/shard_map/ppermute | solution.py:235

commit v2 on v1

--- a/solution.py
+++ b/solution.py
@@ -92,16 +92,19 @@
     return max(t for t in range(LANES, most + 1, LANES) if extent % t == 0)
 
 
-def serve_body(columns, blocks, *refs):
-    ins, share_ref = refs[:blocks], refs[blocks]
-    gate_ref, up_ref, down_ref, own_ref, other_ref, x_ref, h_ref = refs[blocks + 1 :]
+def serve_body(blocks, expert_ref, *refs):
+    ins = refs[:blocks]
+    gate_ref, up_ref, down_ref, own_ref, other_ref, x_ref, h_ref = refs[blocks:]
     width, wide = gate_ref.shape
     start = 0
     share = []
-    for ref, (column, low, high) in zip(ins, columns):
+    for ref in ins:
         size = ref.shape[0]
-        x_ref[start : start + size, :] = ref[...]
-        share.append(share_ref[low:high, column : column + 1])
+        x_ref[start : start + size, :] = ref[:, :width]
+        tags = ref[:, width:].astype(jnp.float32)
+        mine = lax.broadcasted_iota(jnp.int32, tags.shape, 1) == expert_ref[0]
+        chosen = jnp.sum(jnp.where(mine, tags, 0.0), axis=1, keepdims=True)
+        share.append(chosen / jnp.sum(tags, axis=1, keepdims=True))
         start += size
     share = jnp.concatenate(share, axis=0)
     tile = tile_of(wide, 256)
@@ -118,25 +121,163 @@
         other_ref[:, at : at + tile] = out[half:].astype(jnp.bfloat16)
 
 
-def serve(ins, columns, share, experts):
+VMEM = pl.BlockSpec(memory_space=pltpu.VMEM)
+
+
+def serve(ins, expert, experts):
     rows = sum(x.shape[0] for x in ins)
     width, wide = experts[0].shape
-    vmem = pl.BlockSpec(memory_space=pltpu.VMEM)
-    return pl.pallas_call(
-        functools.partial(serve_body, columns, len(ins)),
+    return pl.pallas_call(
+        functools.partial(serve_body, len(ins)),
         out_shape=[jax.ShapeDtypeStruct((rows // 2, width), jnp.bfloat16)] * 2,
-        in_specs=[vmem] * (len(ins) + 4),
-        out_specs=[vmem, vmem],
+        in_specs=[pl.BlockSpec(memory_space=pltpu.SMEM)] + [VMEM] * (len(ins) + 3),
+        out_specs=[VMEM, VMEM],
         scratch_shapes=[pltpu.VMEM((rows, width), jnp.bfloat16), pltpu.VMEM((rows, wide), jnp.bfloat16)],
         compiler_params=pltpu.CompilerParams(vmem_limit_bytes=VMEM_LIMIT),
         cost_estimate=pl.CostEstimate(
             flops=6 * rows * width * wide, bytes_accessed=6 * width * wide, transcendentals=rows * wide
         ),
         name="serve",
-    )(*ins, share, *experts)
+    )(expert, *ins, *experts)
+
+
+def bulk_body(offsets, act_ref, *refs):
+    pieces, out_ref = refs[:-1], refs[-1]
+    width = out_ref.shape[1]
+    tile = tile_of(width, 512)
+    for at in range(0, width, tile):
+        total = None
+        for offset, piece in zip(offsets, pieces):
+            part = jnp.dot(act_ref[offset], piece[:, at : at + tile], preferred_element_type=jnp.float32)
+            total = part if total is None else total + part
+        out_ref[:, at : at + tile] = total
+
+
+def bulk(act, offsets, pieces):
+    shape = (act.shape[1], pieces[0].shape[1])
+    depth = sum(piece.shape[0] for piece in pieces)
+    return pl.pallas_call(
+        functools.partial(bulk_body, offsets),
+        out_shape=jax.ShapeDtypeStruct(shape, jnp.float32),
+        in_specs=[VMEM] * (len(pieces) + 1),
+        out_specs=VMEM,
+        compiler_params=pltpu.CompilerParams(vmem_limit_bytes=VMEM_LIMIT),
+        cost_estimate=pl.CostEstimate(
+            flops=2 * shape[0] * shape[1] * depth, bytes_accessed=4 * shape[0] * shape[1], transcendentals=0
+        ),
+        name="bulk",
+    )(act, *pieces)
+
+
+def last_body(far, act_ref, total_ref, top_ref, bottom_ref, *outs):
+    width = total_ref.shape[1]
+    mid = top_ref.shape[0]
+    rows = outs[0].shape[0]
+    tile = tile_of(width, 512)
+    for at in range(0, width, tile):
+        to = at + tile
+        total = total_ref[:, at:to]
+        total += jnp.dot(act_ref[far][:, :mid], top_ref[:, at:to], preferred_element_type=jnp.float32)
+        total += jnp.dot(act_ref[far][:, mid:], bottom_ref[:, at:to], preferred_element_type=jnp.float32)
+        for index, out in enumerate(outs):
+            out[:, at:to] = total[index * rows : (index + 1) * rows]
+
+
+def last(act, far, total, top, bottom):
+    rows, width = total.shape
+    return pl.pallas_call(
+        functools.partial(last_body, far),
+        out_shape=[jax.ShapeDtypeStruct((rows // 4, width), jnp.float32)] * 4,
+        in_specs=[VMEM] * 4,
+        out_specs=[VMEM] * 4,
+        compiler_params=pltpu.CompilerParams(vmem_limit_bytes=VMEM_LIMIT),
+        cost_estimate=pl.CostEstimate(
+            flops=2 * rows * width * act.shape[2], bytes_accessed=8 * rows * width, transcendentals=0
+        ),
+        name="last",
+    )(act, total, top, bottom)
+
+
+def norm_body(parts, *refs):
+    bias_ref, gain_ref, tags_ref, merged_ref, block_ref = refs[3 * parts :]
+    width = merged_ref.shape[1]
+    at = 0
+    square = 0.0
+    for index in range(parts):
+        own_ref, other_ref, cross_ref = refs[3 * index : 3 * index + 3]
+        to = at + own_ref.shape[1]
+        merged = own_ref[...] + other_ref[...] + bias_ref[:, at:to] + cross_ref[...].astype(jnp.float32)
+        merged_ref[:, at:to] = merged
+        square += jnp.sum(merged * merged, axis=1, keepdims=True)
+        at = to
+    scale = lax.rsqrt(square / width + 1e-06)
+    block_ref[:, :width] = (merged_ref[...] * scale * gain_ref[...]).astype(jnp.bfloat16)
+    block_ref[:, width:] = tags_ref[...]
+
+
+def normalize(parts, bias, gain, tags):
+    rows = tags.shape[0]
+    width = bias.shape[0]
+    flat = [array for part in parts for array in part]
+    return pl.pallas_call(
+        functools.partial(norm_body, len(parts)),
+        out_shape=[
+            jax.ShapeDtypeStruct((rows, width), jnp.float32),
+            jax.ShapeDtypeStruct((rows, width + tags.shape[1]), jnp.bfloat16),
+        ],
+        in_specs=[VMEM] * (len(flat) + 3),
+        out_specs=[VMEM, VMEM],
+        compiler_params=pltpu.CompilerParams(vmem_limit_bytes=VMEM_LIMIT),
+        name="normalize",
+    )(*flat, bias[None], gain[None], tags)
 
 
 VMEM_LIMIT = 24 * 1024 * 1024
+PARTS = 2
+
+
+def add_body(at, own_ref, other_ref, *refs):
+    out_ref = refs[-1]
+    size = out_ref.shape[0]
+    total = own_ref[at : at + size, :].astype(jnp.float32) + other_ref[at : at + size, :].astype(jnp.float32)
+    for ref in refs[:-1]:
+        total += ref[...].astype(jnp.float32)
+    out_ref[...] = total.astype(jnp.bfloat16)
+
+
+def add(own, other, at, size, total):
+    ins = [own, other] + ([] if total is None else [total])
+    return pl.pallas_call(
+        functools.partial(add_body, at),
+        out_shape=jax.ShapeDtypeStruct((size, own.shape[1]), jnp.bfloat16),
+        in_specs=[VMEM] * len(ins),
+        out_specs=VMEM,
+        compiler_params=pltpu.CompilerParams(vmem_limit_bytes=VMEM_LIMIT),
+        name="add",
+    )(*ins)
+
+
+def finish_body(merged_ref, own_ref, other_ref, *refs):
+    out_ref = refs[-1]
+    at = 0
+    for index in range(0, len(refs) - 1, 2):
+        first, second = refs[index], refs[index + 1]
+        to = at + first.shape[0]
+        total = own_ref[at:to, :].astype(jnp.float32) + other_ref[at:to, :].astype(jnp.float32)
+        total += first[...].astype(jnp.float32) + second[...].astype(jnp.float32)
+        out_ref[at:to, :] = (merged_ref[at:to, :] + total).astype(jnp.bfloat16)
+        at = to
+
+
+def finish(merged, *ins):
+    return pl.pallas_call(
+        finish_body,
+        out_shape=jax.ShapeDtypeStruct(merged.shape, jnp.bfloat16),
+        in_specs=[VMEM] * (len(ins) + 1),
+        out_specs=VMEM,
+        compiler_params=pltpu.CompilerParams(vmem_limit_bytes=VMEM_LIMIT),
+        name="finish",
+    )(merged, *ins)
 
 
 def around(array, spot):
@@ -172,7 +313,7 @@
     ahead = functools.partial(lax.ppermute, axis_name="dp", perm=ring_pairs(chips, 1))
     back = functools.partial(lax.ppermute, axis_name="dp", perm=ring_pairs(chips, -1))
 
-    left = right = jnp.where(first_group, merger_weight[:half], merger_weight[half:])
+    weight = jnp.where(first_group, merger_weight[:half], merger_weight[half:])
     act = jax.nn.gelu(merger_input.astype(jnp.float32), approximate=False).astype(jnp.bfloat16)
     act = act.reshape(rows, chips, 2, 2, half)
     kept = jnp.where(first_core, act[:, :, 0], act[:, :, 1])
@@ -183,58 +324,54 @@
     act = jnp.concatenate([kept, cross(given)], axis=0)
     act = around(act.transpose(1, 0, 2), spot)
 
-    def term(offset, weight, low, high):
-        return jnp.dot(act[offset % chips][:, low:high], weight, preferred_element_type=jnp.float32)
-
-    total = term(0, left, 0, half)
-    for step in range(1, far):
+    lanes = jnp.arange(-(-n // LANES) * LANES, dtype=jnp.int32)
+    named = expert_ids[:, :, None] == lanes[None, None, :]
+    tags = jnp.sum(jnp.where(named, combine_ints[:, :, None], 0), axis=1).astype(jnp.bfloat16)
+
+    mid = (half + 15) // 16 * 8
+    streams = []
+    for part in range(PARTS):
+        left = right = weight[:, part * width // PARTS : (part + 1) * width // PARTS]
+        offsets, pieces = [0], [left]
+        for step in range(1, far):
+            left = ahead(left)
+            right = back(right)
+            offsets += [chips - step, step]
+            pieces += [left, right]
+        top = ahead(left[:mid])
+        bottom = back(right[mid:])
+        total = bulk(act, offsets, pieces)
+        own, own_other, theirs, theirs_other = last(act, far, total, top, bottom)
+        theirs = (theirs + swap(theirs_other)).astype(jnp.bfloat16)
+        streams.append((own, swap(own_other), cross(theirs)))
+    merged, block = normalize(streams, merger_bias, norm_gain, tags)
+
+    experts = [w[0] for w in (gate_weight, up_weight, down_weight)]
+    expert = me.astype(jnp.int32)[None]
+    cut = rows // 2
+    left = right = block
+    other = swap(block)
+    outs = [serve([block, other], expert, experts)]
+    for step in range(1, far + 1):
+        if step == far:
+            left, right = left[:cut], right[cut:]
         left = ahead(left)
         right = back(right)
-        total = total + term(-step, left, 0, half) + term(step, right, 0, half)
-    mid = (half + 15) // 16 * 8
-    total = total + term(far, ahead(left[:mid]), 0, mid) + term(far, back(right[mid:]), mid, half)
-    total = total.reshape(4, rows, width)
-    theirs = (total[2] + swap(total[3])).astype(jnp.bfloat16)
-    merged = total[0] + swap(total[1]) + merger_bias + cross(theirs).astype(jnp.float32)
-    scale = lax.rsqrt(jnp.mean(merged * merged, axis=1, keepdims=True) + 1e-06)
-    normed = (merged * scale * norm_gain).astype(jnp.bfloat16)
-
-    counts = combine_ints.astype(jnp.float32)
-    weights = counts / jnp.sum(counts, axis=1, keepdims=True)
-    named = expert_ids[:, :, None] == jnp.arange(n, dtype=jnp.int32)[None, None, :]
-    spread = jnp.sum(jnp.where(named, weights[:, :, None], 0.0), axis=1)
-    share = lax.all_to_all(spread.T, "dp", split_axis=0, concat_axis=0, tiled=True)
-    share = share.reshape(chips, 2, rows)
-    share = jnp.where(first_core, share, share[:, ::-1])
-    share = around(share, spot).reshape(n, rows).T
-
-    experts = [w[0] for w in (gate_weight, up_weight, down_weight)]
-    cut = rows // 2
-    left = right = normed
-    other = swap(normed)
-    outs = [serve([normed, other], [(0, 0, rows), (1, 0, rows)], share, experts)]
-    for step in range(1, far + 1):
-        if step < far:
-            lo, hi = 2 * (chips - step), 2 * step
-            columns = [(lo, 0, rows), (hi, 0, rows), (lo + 1, 0, rows), (hi + 1, 0, rows)]
-        else:
-            left, right = left[:cut], right[cut:]
-            lo = 2 * far
-            columns = [(lo, 0, cut), (lo, cut, rows), (lo + 1, 0, cut), (lo + 1, cut, rows)]
-        left = ahead(left)
-        right = back(right)
-        left_other, right_other = swap(left), swap(right)
-        outs.append(serve([left, right, left_other, right_other], columns, share, experts))
-    sums = [own.astype(jnp.float32) + swap(other).astype(jnp.float32) for own, other in outs]
-    top, bottom = ahead(sums[far][:cut].astype(jnp.bfloat16)), back(sums[far][cut:].astype(jnp.bfloat16))
-    top = jnp.pad(top, ((0, rows - cut), (0, 0)))
-    bottom = jnp.pad(bottom, ((cut, 0), (0, 0)))
-    for step in reversed(range(1, far)):
-        to_back, to_ahead = sums[step][:rows], sums[step][rows:]
-        top = ahead((to_ahead + top.astype(jnp.float32)).astype(jnp.bfloat16))
-        bottom = back((to_back + bottom.astype(jnp.float32)).astype(jnp.bfloat16))
-    combined = sums[0] + top.astype(jnp.float32) + bottom.astype(jnp.float32)
-    return (merged + combined).astype(jnp.bfloat16)
+        others = swap(left), swap(right)
+        outs.append(serve([left, right, *others], expert, experts))
+    outs = [(own, swap(other)) for own, other in outs]
+
+    def home(way, at, low, total):
+        for step in reversed(range(1, far)):
+            total = add(*outs[step], at + low, cut, total)
+            total = way(total)
+        return total
+
+    ahead_high = home(ahead, rows, cut, None)
+    back_low = home(back, 0, 0, None)
+    ahead_low = home(ahead, rows, 0, ahead(add(*outs[far], 0, cut, None)))
+    back_high = home(back, 0, cut, back(add(*outs[far], cut, cut, None)))
+    return finish(merged, *outs[0], ahead_low, back_low, ahead_high, back_high)
 
 
 def shards(*arrays):

time: 169 us -> 166 us (0.982)
  starting transfers between devices: 32.7 us -> 48.9 us
  blocking collectives: 11.2 us -> 0 us
  matrix products: 9.6 us -> 0 us
  Pallas kernels: 21.5 us -> 27.9 us
  waiting for transfers between devices: 74.9 us -> 69 us
  local copies, waits for them, and re-layouts: 9.16 us -> 12.7 us
  other arithmetic: 8.75 us -> 6.36 us
    ppermute x7 -> x10, waiting for transfers between devices: 0.33 us -> 35.6 us  [dense(): left = ahead(left)]
    ppermute x7 -> x10, waiting for transfers between devices: 22.7 us -> 1.53 us  [dense(): right = back(right)]
    ppermute x27 -> x38, waiting for transfers between devices: 45.1 us -> 31.8 us  [the longest x12 12.7 us: home(): total = way(total)]
    ppermute x7 -> x10, starting transfers between devices: 4.84 us -> 17.3 us  [dense(): left = ahead(left)]
    all_to_all x1 -> x0, blocking collectives: 11.2 us -> none  [dense(): lax.all_to_all(spread.T, 'dp', split_axis=0, concat_axis=0, tiled=True)]
    ppermute x27 -> x38, starting transfers between devices: 15.1 us -> 24.9 us  [the longest x12 12.9 us: home(): total = way(total)]
    dot_general x9 -> x0, matrix products: 9.6 us -> none  [term(): jnp.dot(act[offset % chips][:, low:high], weight, preferred_element_type=...]
    ppermute x7 -> x10, starting transfers between devices: 10.7 us -> 4.18 us  [dense(): right = back(right)]
  transfers between devices with their start and end apart: 43 -> 60, of which waited for: 19 -> 21; matrix products, arithmetic and copies ran while one was open for 8% -> 5% of each run, Pallas kernels for 13% -> 15%
where the time goes in v2:
time: 166 us; the launch traced here: 165 us
  waiting for transfers between devices  69 us (42%)
  starting transfers between devices  48.9 us (29%)
  Pallas kernels  27.9 us (17%)
  local copies, waits for them, and re-layouts  12.7 us (8%)
  other arithmetic  6.36 us (4%)
    ppermute x10, waiting for transfers between devices, dense(): left = ahead(left)  35.6 us
    pallas_call x5, Pallas kernels, serve(): pl.pallas_call(functools.partial(serve_body, len(ins)), out_shape=[jax.Sh...  18.9 us
    ppermute x10, starting transfers between devices, dense(): left = ahead(left)  17.3 us
    ppermute x12, starting transfers between devices, home(): total = way(total)  12.9 us
    ppermute x12, waiting for transfers between devices, home(): total = way(total)  12.7 us
    unnamed x41, local copies, waits for them, and re-layouts  10.6 us
    ppermute x1, waiting for transfers between devices, dense(): ahead_low = home(ahead, rows, 0, ahead(add(*outs[far], 0, cut, None)))  5.35 us
    ppermute x1, waiting for transfers between devices, dense(): back_high = home(back, 0, cut, back(add(*outs[far], cut, cut, None)))  4.99 us
  transfers between devices with their start and end apart: 60, of which 21 were waited for; matrix products, arithmetic and copies ran while one was open for 5% of the time, Pallas kernels for 15%

profile of v2, /device:TPU:0, one launch (start us, length us, event | category | flops | bytes accessed | tf_op | source)
XLA Modules:
  0.0 165.3 jit_solution(5659337111157338700)
XLA Ops:
  0.0 1.3 copy.17
  1.3 2.6 %fusion.1 = bf16[96,2304]{0,1:T(8,128)(2,1)S(1)} fusion(bf16[96,2304]{0,1:T(8,128)(2,1)S(1)} %copy.17), kind=kLoop, calls=%fused_computation.8 | loop fusion | flops 14598144 | bytes 884736 | tf_op jit(solution)/shard_map/convert_element_type | solution.py:317
  5.4 3.1 %collective-permute-start.2 = (bf16[72,1024]{1,0:T(8,128)(2,1)S(1)}, bf16[72,1024]{1,0:T(8,128)(2,1)S(1)}, u32[]{:S(2)}, u32[]{:S(2)}) collective-permute-start(bf16[72,1024]{1,0:T(8,128)(2,1)S(1)} %get-tuple-element.54.refs_0_), channel_id=1, source_target_pairs={{0,4},{1,5},{4,8},{5,9},{8,12},{9,13},{12,14},{13,15},{14,10},{15,... | collective-permute-start | bytes 442376 | tf_op jit(solution)/shard_map/ppermute | solution.py:337
  8.7 2.0 %collective-permute-start.1 = (bf16[192,8,72]{2,0,1:T(8,128)(2,1)S(1)}, bf16[192,8,72]{2,0,1:T(8,128)(2,1)S(1)}, u32[]{:S(2)}, u32[]{:S(2)}) collective-permute-start(bf16[192,8,72]{2,0,1:T(8,128)(2,1)S(1)} %get-tuple-element.48), channel_id=1, source_target_pairs={{0,16},{16,0},{1,17},{17,1},{2,18},{18,2},{3,19},{19,3},{4,20},{20... | collective-permute-start | bytes 663560 | tf_op jit(solution)/shard_map/ppermute | solution.py:324
  10.7 1.6 collective-permute-start.13
  12.8 1.6 collective-permute-start.4
  14.8 2.7 %collective-permute-done.13.refs_1_ = bf16[72,1024]{1,0:T(8,128)(2,1)S(1)} collective-permute-done((bf16[72,1024]{1,0:T(8,128)(2,1)S(1)}, bf16[72,1024]{1,0:T(8,128)(2,1)S(1)}, u32[]{:S(2)}, u32[]{:S(2)}) %collective-permute-start.13) | collective-permute-done | bytes 147488 | tf_op jit(solution)/shard_map/ppermute | solution.py:337
  17.5 1.6 collective-permute-start.15
  19.5 1.1 collective-permute-done.4.refs_3_
  20.6 1.6 collective-permute-start.6
  22.9 3.0 %collective-permute-done.6.refs_5_ = bf16[72,1024]{1,0:T(8,128)(2,1)S(1)} collective-permute-done((bf16[72,1024]{1,0:T(8,128)(2,1)S(1)}, bf16[72,1024]{1,0:T(8,128)(2,1)S(1)}, u32[]{:S(2)}, u32[]{:S(2)}) %collective-permute-start.6) | collective-permute-done | bytes 147488 | tf_op jit(solution)/shard_map/ppermute | solution.py:337
  25.9 1.6 collective-permute-start.8
  28.9 1.6 bulk.2.total_ref
  30.4 1.6 collective-permute-done.9.bottom_ref
  32.0 1.2 last.2
  33.3 1.6 collective-permute-start.17
  35.3 4.2 %collective-permute-done.17.refs_5_ = bf16[72,1024]{1,0:T(8,128)(2,1)S(1)} collective-permute-done((bf16[72,1024]{1,0:T(8,128)(2,1)S(1)}, bf16[72,1024]{1,0:T(8,128)(2,1)S(1)}, u32[]{:S(2)}, u32[]{:S(2)}) %collective-permute-start.17) | collective-permute-done | bytes 147488 | tf_op jit(solution)/shard_map/ppermute | solution.py:337
  39.5 1.6 collective-permute-start.19
  41.6 1.5 bulk.3.total_ref
  43.2 2.3 %collective-permute-done.20.bottom_ref = bf16[32,1024]{1,0:T(8,128)(2,1)S(1)} collective-permute-done((bf16[32,1024]{1,0:T(8,128)(2,1)S(1)}, bf16[32,1024]{1,0:T(8,128)(2,1)S(1)}, u32[]{:S(2)}, u32[]{:S(2)}) %collective-permute-start.20) | collective-permute-done | bytes 65568 | tf_op jit(solution)/shard_map/ppermute | solution.py:342
  45.4 1.2 last.3
  48.0 0.9 collective-permute-start.12
  49.6 1.1 collective-permute-start.23
  50.8 1.5 copy.21
  52.3 1.4 copy.20
  53.7 1.1 select_reduce_fusion
  54.8 1.3 collective-permute-done.12.refs_2_
  56.1 3.7 %collective-permute-done.23.refs_5_ = bf16[96,1024]{1,0:T(8,128)(2,1)} collective-permute-done((bf16[96,1024]{1,0:T(8,128)(2,1)}, bf16[96,1024]{1,0:T(8,128)(2,1)}, u32[]{:S(2)}, u32[]{:S(2)}) %collective-permute-start.23) | collective-permute-done | bytes 196640 | tf_op jit(solution)/shard_map/ppermute | solution.py:346
  59.8 1.0 copy-done.10
  60.8 1.5 normalize.1
  62.4 0.9 copy-done.5
  63.2 1.6 collective-permute-start.26
  65.3 9.1 %collective-permute-done.26.refs_0_ = bf16[96,2176]{1,0:T(8,128)(2,1)S(1)} collective-permute-done((bf16[96,2176]{1,0:T(8,128)(2,1)S(1)}, bf16[96,2176]{1,0:T(8,128)(2,1)S(1)}, u32[]{:S(2)}, u32[]{:S(2)}) %collective-permute-start.26) | collective-permute-done | bytes 417824 | tf_op jit(solution)/shard_map/ppermute | solution.py:358
  74.4 1.6 collective-permute-start.31
  76.5 8.3 %collective-permute-done.31.refs_0_ = bf16[96,2176]{1,0:T(8,128)(2,1)} collective-permute-done((bf16[96,2176]{1,0:T(8,128)(2,1)S(1)}, bf16[96,2176]{1,0:T(8,128)(2,1)}, u32[]{:S(2)}, u32[]{:S(2)}) %collective-permute-start.31) | collective-permute-done | bytes 417824 | tf_op jit(solution)/shard_map/ppermute | solution.py:358
  84.7 1.6 collective-permute-start.36
  87.3 7.2 %collective-permute-done.36.refs_0_ = bf16[96,2176]{1,0:T(8,128)(2,1)} collective-permute-done((bf16[96,2176]{1,0:T(8,128)(2,1)}, bf16[96,2176]{1,0:T(8,128)(2,1)}, u32[]{:S(2)}, u32[]{:S(2)}) %collective-permute-start.36) | collective-permute-done | bytes 417824 | tf_op jit(solution)/shard_map/ppermute | solution.py:358
  94.5 1.3 collective-permute-done.37.refs_1_
  96.3 0.9 slice.78
  97.2 0.9 slice.79
  98.2 1.6 collective-permute-start.41
  100.3 1.9 %copy-done.1 = bf16[1,2048,768]{2,1,0:T(8,128)(2,1)S(1)} copy-done((bf16[1,2048,768]{2,1,0:T(8,128)(2,1)S(1)}, bf16[1,2048,768]{2,1,0:T(8,128)(2,1)}, u32[]{:S(2)}) %copy-start.1) | copy-done | bytes 3145752
  102.2 1.9 %copy-done.3 = bf16[1,768,2048]{2,1,0:T(8,128)(2,1)S(1)} copy-done((bf16[1,768,2048]{2,1,0:T(8,128)(2,1)S(1)}, bf16[1,768,2048]{2,1,0:T(8,128)(2,1)}, u32[]{:S(2)}) %copy-start.3) | copy-done | bytes 3145752
  104.1 5.4 %serve.7 = (bf16[192,2048]{1,0:T(8,128)(2,1)S(1)}, bf16[192,2048]{1,0:T(8,128)(2,1)S(1)}) custom-call(s32[1]{0:T(128)} %bitcast.8.expert_ref, bf16[96,2176]{1,0:T(8,128)(2,1)} %collective-permute-done.31.refs_0_, bf16[96,2176]{1,0:T(8,128)(2,1)} %collective-permute-done.32.refs_1_, bf16[96,2176]{1,0:T(8,128)(2,1)} %collective-permute-done.33.refs_2_, ...), custom_call_target="tpu_custom_call" | custom-call | flops 3623878656 | bytes 9437184 | tf_op jit(solution)/shard_map/serve/pallas_call | solution.py:130
  110.6 5.3 %serve.8 = (bf16[192,2048]{1,0:T(8,128)(2,1)S(1)}, bf16[192,2048]{1,0:T(8,128)(2,1)S(1)}) custom-call(s32[1]{0:T(128)} %bitcast.8.expert_ref, bf16[96,2176]{1,0:T(8,128)(2,1)} %collective-permute-done.36.refs_0_, bf16[96,2176]{1,0:T(8,128)(2,1)} %collective-permute-done.37.refs_1_, bf16[96,2176]{1,0:T(8,128)(2,1)} %collective-permute-done.38.refs_2_, ...), custom_call_target="tpu_custom_call" | custom-call | flops 3623878656 | bytes 9437184 | tf_op jit(solution)/shard_map/serve/pallas_call | solution.py:130
  116.1 2.1 %serve.9 = (bf16[96,2048]{1,0:T(8,128)(2,1)S(1)}, bf16[96,2048]{1,0:T(8,128)(2,1)S(1)}) custom-call(s32[1]{0:T(128)} %bitcast.8.expert_ref, bf16[48,2176]{1,0:T(8,128)(2,1)S(1)} %collective-permute-done.41.refs_0_, bf16[48,2176]{1,0:T(8,128)(2,1)S(1)} %collective-permute-done.42.refs_1_, bf16[48,2176]{1,0:T(8,128)(2,1)S(1)} %collective-permute-done.43.refs_2_, ...), custom_call_target="tpu_custom_call" | custom-call | flops 1811939328 | bytes 9437184 | tf_op jit(solution)/shard_map/serve/pallas_call | solution.py:130
  118.7 4.0 %serve.6 = (bf16[192,2048]{1,0:T(8,128)(2,1)S(1)}, bf16[192,2048]{1,0:T(8,128)(2,1)S(1)}) custom-call(s32[1]{0:T(128)} %bitcast.8.expert_ref, bf16[96,2176]{1,0:T(8,128)(2,1)S(1)} %copy-done.14, bf16[96,2176]{1,0:T(8,128)(2,1)S(1)} %copy-done.16, bf16[96,2176]{1,0:T(8,128)(2,1)S(1)} %collective-permute-done.28.refs_2_, ...), custom_call_target="tpu_custom_call" | custom-call | flops 3623878656 | bytes 9437184 | tf_op jit(solution)/shard_map/serve/pallas_call | solution.py:130
  123.3 1.5 collective-permute-start.46
  124.9 5.4 %collective-permute-done.46.refs_0_ = bf16[48,2048]{1,0:T(8,128)(2,1)S(1)} collective-permute-done((bf16[48,2048]{1,0:T(8,128)(2,1)S(1)}, bf16[48,2048]{1,0:T(8,128)(2,1)S(1)}, u32[]{:S(2)}, u32[]{:S(2)}) %collective-permute-start.46) | collective-permute-done | bytes 196640 | tf_op jit(solution)/shard_map/ppermute | solution.py:372
  130.8 1.6 collective-permute-start.47
  133.1 5.0 %collective-permute-done.56.refs_0_ = bf16[48,2048]{1,0:T(8,128)(2,1)S(1)} collective-permute-done((bf16[48,2048]{1,0:T(8,128)(2,1)S(1)}, bf16[48,2048]{1,0:T(8,128)(2,1)S(1)}, u32[]{:S(2)}, u32[]{:S(2)}) %collective-permute-start.56) | collective-permute-done | bytes 196640 | tf_op jit(solution)/shard_map/ppermute | solution.py:373
  138.1 1.5 collective-permute-start.53
  139.6 0.8 collective-permute-start.57
  140.4 2.1 %serve.5 = (bf16[96,2048]{1,0:T(8,128)(2,1)S(1)}, bf16[96,2048]{1,0:T(8,128)(2,1)S(1)}) custom-call(s32[1]{0:T(128)} %bitcast.8.expert_ref, bf16[96,2176]{1,0:T(8,128)(2,1)S(1)} %copy-done.8, bf16[96,2176]{1,0:T(8,128)(2,1)S(1)} %collective-permute-done.24.refs_1_, bf16[2048,768]{1,0:T(8,128)(2,1)S(1)} %bitcast.21, bf16[2048,768]{1,0:T(8,128)(2,1)S(1)} %bitcast.26, ...), custom_call_target="tpu_custom_call" | custom-call | flops 1811939328 | bytes 9437184 | tf_op jit(solution)/shard_map/serve/pallas_call | solution.py:130
  142.6 1.6 collective-permute-start.48
  144.3 1.3 collective-permute-done.53.refs_0_
  146.2 1.6 collective-permute-start.54
  149.0 1.6 collective-permute-start.49
  150.5 2.8 %collective-permute-done.51.refs_0_ = bf16[48,2048]{1,0:T(8,128)(2,1)S(1)} collective-permute-done((bf16[48,2048]{1,0:T(8,128)(2,1)S(1)}, bf16[48,2048]{1,0:T(8,128)(2,1)S(1)}, u32[]{:S(2)}, u32[]{:S(2)}) %collective-permute-start.51) | collective-permute-done | bytes 196640 | tf_op jit(solution)/shard_map/ppermute | solution.py:367
  154.1 1.6 collective-permute-start.55
  155.7 1.9 %collective-permute-done.58.refs_0_ = bf16[48,2048]{1,0:T(8,128)(2,1)S(1)} collective-permute-done((bf16[48,2048]{1,0:T(8,128)(2,1)S(1)}, bf16[48,2048]{1,0:T(8,128)(2,1)S(1)}, u32[]{:S(2)}, u32[]{:S(2)}) %collective-permute-start.58) | collective-permute-done | bytes 196640 | tf_op jit(solution)/shard_map/ppermute | solution.py:367
  158.2 3.6 %collective-permute-done.52.refs_1_ = bf16[48,2048]{1,0:T(8,128)(2,1)S(1)} collective-permute-done((bf16[48,2048]{1,0:T(8,128)(2,1)S(1)}, bf16[48,2048]{1,0:T(8,128)(2,1)S(1)}, u32[]{:S(2)}, u32[]{:S(2)}) %collective-permute-start.52) | collective-permute-done | bytes 196640 | tf_op jit(solution)/shard_map/ppermute | solution.py:367
  161.8 2.5 %collective-permute-done.59.refs_3_ = bf16[48,2048]{1,0:T(8,128)(2,1)S(1)} collective-permute-done((bf16[48,2048]{1,0:T(8,128)(2,1)S(1)}, bf16[48,2048]{1,0:T(8,128)(2,1)S(1)}, u32[]{:S(2)}, u32[]{:S(2)}) %collective-permute-start.59) | collective-permute-done | bytes 196640 | tf_op jit(solution)/shard_map/ppermute | solution.py:367
  164.3 1.0 finish.1
  (142 shorter events, 18.0 us)
Async XLA Ops:
  4.5 3.9 %collective-permute-start = (bf16[96,8,2,72]{3,0,1,2:T(8,128)(2,1)S(1)}, bf16[96,8,2,72]{3,0,1,2:T(8,128)(2,1)S(1)}, u32[]{:S(2)}, u32[]{:S(2)}) collective-permute-start(bf16[96,8,2,72]{3,0,1,2:T(8,128)(2,1)S(1)} %get-tuple-element.50), channel_id=1, source_target_pairs={{0,1},{1,0},{2,3},{3,2},{4,5},{5,4},{6,7},{7,6},{8,9},{9,8},{10,11... | collective-permute-start | bytes 663560 | tf_op jit(solution)/shard_map/ppermute | solution.py:321
  5.4 7.4 %collective-permute-start.2 = (bf16[72,1024]{1,0:T(8,128)(2,1)S(1)}, bf16[72,1024]{1,0:T(8,128)(2,1)S(1)}, u32[]{:S(2)}, u32[]{:S(2)}) collective-permute-start(bf16[72,1024]{1,0:T(8,128)(2,1)S(1)} %get-tuple-element.54.refs_0_), channel_id=1, source_target_pairs={{0,4},{1,5},{4,8},{5,9},{8,12},{9,13},{12,14},{13,15},{14,10},{15,... | collective-permute-start | bytes 442376 | tf_op jit(solution)/shard_map/ppermute | solution.py:337
  8.5 5.9 %collective-permute-start.3 = (bf16[72,1024]{1,0:T(8,128)(2,1)S(1)}, bf16[72,1024]{1,0:T(8,128)(2,1)S(1)}, u32[]{:S(2)}, u32[]{:S(2)}) collective-permute-start(bf16[72,1024]{1,0:T(8,128)(2,1)S(1)} %get-tuple-element.54.refs_0_), channel_id=1, source_target_pairs={{0,2},{1,3},{4,0},{5,1},{8,4},{9,5},{12,8},{13,9},{14,12},{15,13},... | collective-permute-start | bytes 442376 | tf_op jit(solution)/shard_map/ppermute | solution.py:338
  8.7 13.9 %collective-permute-start.1 = (bf16[192,8,72]{2,0,1:T(8,128)(2,1)S(1)}, bf16[192,8,72]{2,0,1:T(8,128)(2,1)S(1)}, u32[]{:S(2)}, u32[]{:S(2)}) collective-permute-start(bf16[192,8,72]{2,0,1:T(8,128)(2,1)S(1)} %get-tuple-element.48), channel_id=1, source_target_pairs={{0,16},{16,0},{1,17},{17,1},{2,18},{18,2},{3,19},{19,3},{4,20},{20... | collective-permute-start | bytes 663560 | tf_op jit(solution)/shard_map/ppermute | solution.py:324
  10.7 6.7 %collective-permute-start.13 = (bf16[72,1024]{1,0:T(8,128)(2,1)S(1)}, bf16[72,1024]{1,0:T(8,128)(2,1)S(1)}, u32[]{:S(2)}, u32[]{:S(2)}) collective-permute-start(bf16[72,1024]{1,0:T(8,128)(2,1)S(1)} %get-tuple-element.53.refs_0_), channel_id=1, source_target_pairs={{0,4},{1,5},{4,8},{5,9},{8,12},{9,13},{12,14},{13,15},{14,10},{15,... | collective-permute-start | bytes 442376 | tf_op jit(solution)/shard_map/ppermute | solution.py:337
  12.3 6.7 %collective-permute-start.14 = (bf16[72,1024]{1,0:T(8,128)(2,1)S(1)}, bf16[72,1024]{1,0:T(8,128)(2,1)S(1)}, u32[]{:S(2)}, u32[]{:S(2)}) collective-permute-start(bf16[72,1024]{1,0:T(8,128)(2,1)S(1)} %get-tuple-element.53.refs_0_), channel_id=1, source_target_pairs={{0,2},{1,3},{4,0},{5,1},{8,4},{9,5},{12,8},{13,9},{14,12},{15,13},... | collective-permute-start | bytes 442376 | tf_op jit(solution)/shard_map/ppermute | solution.py:338
  12.8 7.9 %collective-permute-start.4 = (bf16[72,1024]{1,0:T(8,128)(2,1)S(1)}, bf16[72,1024]{1,0:T(8,128)(2,1)S(1)}, u32[]{:S(2)}, u32[]{:S(2)}) collective-permute-start(bf16[72,1024]{1,0:T(8,128)(2,1)S(1)} %collective-permute-done.2.refs_1_), channel_id=1, source_target_pairs={{0,4},{1,5},{4,8},{5,9},{8,12},{9,13},{12,14},{13,15},{14,10},{15,... | collective-permute-start | bytes 442376 | tf_op jit(solution)/shard_map/ppermute | solution.py:337
  14.4 7.8 %collective-permute-start.5 = (bf16[72,1024]{1,0:T(8,128)(2,1)S(1)}, bf16[72,1024]{1,0:T(8,128)(2,1)S(1)}, u32[]{:S(2)}, u32[]{:S(2)}) collective-permute-start(bf16[72,1024]{1,0:T(8,128)(2,1)S(1)} %collective-permute-done.3.refs_2_), channel_id=1, source_target_pairs={{0,2},{1,3},{4,0},{5,1},{8,4},{9,5},{12,8},{13,9},{14,12},{15,13},... | collective-permute-start | bytes 442376 | tf_op jit(solution)/shard_map/ppermute | solution.py:338
  17.5 15.8 %collective-permute-start.15 = (bf16[72,1024]{1,0:T(8,128)(2,1)S(1)}, bf16[72,1024]{1,0:T(8,128)(2,1)S(1)}, u32[]{:S(2)}, u32[]{:S(2)}) collective-permute-start(bf16[72,1024]{1,0:T(8,128)(2,1)S(1)} %collective-permute-done.13.refs_1_), channel_id=1, source_target_pairs={{0,4},{1,5},{4,8},{5,9},{8,12},{9,13},{12,14},{13,15},{14,10},{15,... | collective-permute-start | bytes 442376 | tf_op jit(solution)/shard_map/ppermute | solution.py:337
  19.0 15.8 %collective-permute-start.16 = (bf16[72,1024]{1,0:T(8,128)(2,1)S(1)}, bf16[72,1024]{1,0:T(8,128)(2,1)S(1)}, u32[]{:S(2)}, u32[]{:S(2)}) collective-permute-start(bf16[72,1024]{1,0:T(8,128)(2,1)S(1)} %collective-permute-done.14.refs_2_), channel_id=1, source_target_pairs={{0,2},{1,3},{4,0},{5,1},{8,4},{9,5},{12,8},{13,9},{14,12},{15,13},... | collective-permute-start | bytes 442376 | tf_op jit(solution)/shard_map/ppermute | solution.py:338
  20.6 5.3 %collective-permute-start.6 = (bf16[72,1024]{1,0:T(8,128)(2,1)S(1)}, bf16[72,1024]{1,0:T(8,128)(2,1)S(1)}, u32[]{:S(2)}, u32[]{:S(2)}) collective-permute-start(bf16[72,1024]{1,0:T(8,128)(2,1)S(1)} %collective-permute-done.4.refs_3_), channel_id=1, source_target_pairs={{0,4},{1,5},{4,8},{5,9},{8,12},{9,13},{12,14},{13,15},{14,10},{15,... | collective-permute-start | bytes 442376 | tf_op jit(solution)/shard_map/ppermute | solution.py:337
  22.2 5.5 %collective-permute-start.7 = (bf16[72,1024]{1,0:T(8,128)(2,1)S(1)}, bf16[72,1024]{1,0:T(8,128)(2,1)S(1)}, u32[]{:S(2)}, u32[]{:S(2)}) collective-permute-start(bf16[72,1024]{1,0:T(8,128)(2,1)S(1)} %collective-permute-done.5.refs_4_), channel_id=1, source_target_pairs={{0,2},{1,3},{4,0},{5,1},{8,4},{9,5},{12,8},{13,9},{14,12},{15,13},... | collective-permute-start | bytes 442376 | tf_op jit(solution)/shard_map/ppermute | solution.py:338
  25.9 6.1 %collective-permute-start.8 = (bf16[40,1024]{1,0:T(8,128)(2,1)S(1)}, bf16[40,1024]{1,0:T(8,128)(2,1)S(1)}, u32[]{:S(2)}, u32[]{:S(2)}) collective-permute-start(bf16[40,1024]{1,0:T(8,128)(2,1)S(1)} %slice.73), channel_id=1, source_target_pairs={{0,4},{1,5},{4,8},{5,9},{8,12},{9,13},{12,14},{13,15},{14,10},{15,... | collective-permute-start | bytes 245768 | tf_op jit(solution)/shard_map/ppermute | solution.py:341
  27.8 4.3 %collective-permute-start.9 = (bf16[32,1024]{1,0:T(8,128)(2,1)S(1)}, bf16[32,1024]{1,0:T(8,128)(2,1)S(1)}, u32[]{:S(2)}, u32[]{:S(2)}) collective-permute-start(bf16[32,1024]{1,0:T(8,128)(2,1)S(1)} %slice.74), channel_id=1, source_target_pairs={{0,2},{1,3},{4,0},{5,1},{8,4},{9,5},{12,8},{13,9},{14,12},{15,13},... | collective-permute-start | bytes 196616 | tf_op jit(solution)/shard_map/ppermute | solution.py:342
  33.3 14.0 %collective-permute-start.11 = (f32[96,1024]{1,0:T(8,128)S(1)}, f32[96,1024]{1,0:T(8,128)S(1)}, u32[]{:S(2)}, u32[]{:S(2)}) collective-permute-start(f32[96,1024]{1,0:T(8,128)S(1)} %get-tuple-element.28), channel_id=1, source_target_pairs={{0,1},{1,0},{2,3},{3,2},{4,5},{5,4},{6,7},{7,6},{8,9},{9,8},{10,11... | collective-permute-start | bytes 1179656 | tf_op jit(solution)/shard_map/ppermute | solution.py:345
  33.3 6.3 %collective-permute-start.17 = (bf16[72,1024]{1,0:T(8,128)(2,1)S(1)}, bf16[72,1024]{1,0:T(8,128)(2,1)S(1)}, u32[]{:S(2)}, u32[]{:S(2)}) collective-permute-start(bf16[72,1024]{1,0:T(8,128)(2,1)S(1)} %collective-permute-done.15.refs_3_), channel_id=1, source_target_pairs={{0,4},{1,5},{4,8},{5,9},{8,12},{9,13},{12,14},{13,15},{14,10},{15,... | collective-permute-start | bytes 442376 | tf_op jit(solution)/shard_map/ppermute | solution.py:337
  34.9 6.3 %collective-permute-start.18 = (bf16[72,1024]{1,0:T(8,128)(2,1)S(1)}, bf16[72,1024]{1,0:T(8,128)(2,1)S(1)}, u32[]{:S(2)}, u32[]{:S(2)}) collective-permute-start(bf16[72,1024]{1,0:T(8,128)(2,1)S(1)} %collective-permute-done.16.refs_4_), channel_id=1, source_target_pairs={{0,2},{1,3},{4,0},{5,1},{8,4},{9,5},{12,8},{13,9},{14,12},{15,13},... | collective-permute-start | bytes 442376 | tf_op jit(solution)/shard_map/ppermute | solution.py:338
  39.5 5.9 %collective-permute-start.19 = (bf16[40,1024]{1,0:T(8,128)(2,1)S(1)}, bf16[40,1024]{1,0:T(8,128)(2,1)S(1)}, u32[]{:S(2)}, u32[]{:S(2)}) collective-permute-start(bf16[40,1024]{1,0:T(8,128)(2,1)S(1)} %slice.76), channel_id=1, source_target_pairs={{0,4},{1,5},{4,8},{5,9},{8,12},{9,13},{12,14},{13,15},{14,10},{15,... | collective-permute-start | bytes 245768 | tf_op jit(solution)/shard_map/ppermute | solution.py:341
  41.1 4.3 %collective-permute-start.20 = (bf16[32,1024]{1,0:T(8,128)(2,1)S(1)}, bf16[32,1024]{1,0:T(8,128)(2,1)S(1)}, u32[]{:S(2)}, u32[]{:S(2)}) collective-permute-start(bf16[32,1024]{1,0:T(8,128)(2,1)S(1)} %slice.77), channel_id=1, source_target_pairs={{0,2},{1,3},{4,0},{5,1},{8,4},{9,5},{12,8},{13,9},{14,12},{15,13},... | collective-permute-start | bytes 196616 | tf_op jit(solution)/shard_map/ppermute | solution.py:342
  46.7 13.1 %copy-start.11 = (f32[2048]{0:T(1024)S(1)}, f32[2048]{0:T(1024)}, u32[]{:S(2)}) copy-start(f32[2048]{0:T(1024)} %param.11) | copy-start | bytes 24580
  46.7 13.1 %copy-start.12 = (f32[2048]{0:T(1024)S(1)}, f32[2048]{0:T(1024)}, u32[]{:S(2)}) copy-start(f32[2048]{0:T(1024)} %param.12) | copy-start | bytes 24580
  46.7 2.2 %collective-permute-start.22 = (f32[96,1024]{1,0:T(8,128)S(1)}, f32[96,1024]{1,0:T(8,128)S(1)}, u32[]{:S(2)}, u32[]{:S(2)}) collective-permute-start(f32[96,1024]{1,0:T(8,128)S(1)} %get-tuple-element.32), channel_id=1, source_target_pairs={{0,1},{1,0},{2,3},{3,2},{4,5},{5,4},{6,7},{7,6},{8,9},{9,8},{10,11... | collective-permute-start | bytes 1179656 | tf_op jit(solution)/shard_map/ppermute | solution.py:345
  46.7 8.1 %collective-permute-start.10 = (f32[96,1024]{1,0:T(8,128)}, f32[96,1024]{1,0:T(8,128)}, u32[]{:S(2)}, u32[]{:S(2)}) collective-permute-start(f32[96,1024]{1,0:T(8,128)} %get-tuple-element.26), channel_id=1, source_target_pairs={{0,1},{1,0},{2,3},{3,2},{4,5},{5,4},{6,7},{7,6},{8,9},{9,8},{10,11... | collective-permute-start | bytes 1179656 | tf_op jit(solution)/shard_map/ppermute | solution.py:346
  47.2 7.6 %collective-permute-start.21 = (f32[96,1024]{1,0:T(8,128)}, f32[96,1024]{1,0:T(8,128)}, u32[]{:S(2)}, u32[]{:S(2)}) collective-permute-start(f32[96,1024]{1,0:T(8,128)} %get-tuple-element.30), channel_id=1, source_target_pairs={{0,1},{1,0},{2,3},{3,2},{4,5},{5,4},{6,7},{7,6},{8,9},{9,8},{10,11... | collective-permute-start | bytes 1179656 | tf_op jit(solution)/shard_map/ppermute | solution.py:346
  48.0 8.1 %collective-permute-start.12 = (bf16[96,1024]{1,0:T(8,128)(2,1)}, bf16[96,1024]{1,0:T(8,128)(2,1)}, u32[]{:S(2)}, u32[]{:S(2)}) collective-permute-start(bf16[96,1024]{1,0:T(8,128)(2,1)} %add_convert_fusion.1), channel_id=1, source_target_pairs={{0,16},{16,0},{1,17},{17,1},{2,18},{18,2},{3,19},{19,3},{4,20},{20... | collective-permute-start | bytes 589832 | tf_op jit(solution)/shard_map/ppermute | solution.py:346
  49.6 10.2 %collective-permute-start.23 = (bf16[96,1024]{1,0:T(8,128)(2,1)}, bf16[96,1024]{1,0:T(8,128)(2,1)}, u32[]{:S(2)}, u32[]{:S(2)}) collective-permute-start(bf16[96,1024]{1,0:T(8,128)(2,1)} %add_convert_fusion), channel_id=1, source_target_pairs={{0,16},{16,0},{1,17},{17,1},{2,18},{18,2},{3,19},{19,3},{4,20},{20... | collective-permute-start | bytes 589832 | tf_op jit(solution)/shard_map/ppermute | solution.py:346
  50.8 49.5 %copy-start = (bf16[1,2048,768]{2,1,0:T(8,128)(2,1)S(1)}, bf16[1,2048,768]{2,1,0:T(8,128)(2,1)}, u32[]{:S(2)}) copy-start(bf16[1,2048,768]{2,1,0:T(8,128)(2,1)} %param.13) | copy-start | bytes 9437188
  63.2 11.1 %collective-permute-start.26 = (bf16[96,2176]{1,0:T(8,128)(2,1)S(1)}, bf16[96,2176]{1,0:T(8,128)(2,1)S(1)}, u32[]{:S(2)}, u32[]{:S(2)}) collective-permute-start(bf16[96,2176]{1,0:T(8,128)(2,1)S(1)} %get-tuple-element.34.refs_0_), channel_id=1, source_target_pairs={{0,4},{1,5},{4,8},{5,9},{8,12},{9,13},{12,14},{13,15},{14,10},{15,... | collective-permute-start | bytes 1253384 | tf_op jit(solution)/shard_map/ppermute | solution.py:358
  64.8 11.1 %collective-permute-start.27 = (bf16[96,2176]{1,0:T(8,128)(2,1)S(1)}, bf16[96,2176]{1,0:T(8,128)(2,1)S(1)}, u32[]{:S(2)}, u32[]{:S(2)}) collective-permute-start(bf16[96,2176]{1,0:T(8,128)(2,1)S(1)} %get-tuple-element.34.refs_0_), channel_id=1, source_target_pairs={{0,2},{1,3},{4,0},{5,1},{8,4},{9,5},{12,8},{13,9},{14,12},{15,13},... | collective-permute-start | bytes 1253384 | tf_op jit(solution)/shard_map/ppermute | solution.py:359
  74.4 10.4 %collective-permute-start.31 = (bf16[96,2176]{1,0:T(8,128)(2,1)S(1)}, bf16[96,2176]{1,0:T(8,128)(2,1)}, u32[]{:S(2)}, u32[]{:S(2)}) collective-permute-start(bf16[96,2176]{1,0:T(8,128)(2,1)S(1)} %collective-permute-done.26.refs_0_), channel_id=1, source_target_pairs={{0,4},{1,5},{4,8},{5,9},{8,12},{9,13},{12,14},{13,15},{14,10},{15,... | collective-permute-start | bytes 1253384 | tf_op jit(solution)/shard_map/ppermute | solution.py:358
  76.0 10.4 %collective-permute-start.32 = (bf16[96,2176]{1,0:T(8,128)(2,1)S(1)}, bf16[96,2176]{1,0:T(8,128)(2,1)}, u32[]{:S(2)}, u32[]{:S(2)}) collective-permute-start(bf16[96,2176]{1,0:T(8,128)(2,1)S(1)} %collective-permute-done.27.refs_1_), channel_id=1, source_target_pairs={{0,2},{1,3},{4,0},{5,1},{8,4},{9,5},{12,8},{13,9},{14,12},{15,13},... | collective-permute-start | bytes 1253384 | tf_op jit(solution)/shard_map/ppermute | solution.py:359
  84.7 9.7 %collective-permute-start.36 = (bf16[96,2176]{1,0:T(8,128)(2,1)}, bf16[96,2176]{1,0:T(8,128)(2,1)}, u32[]{:S(2)}, u32[]{:S(2)}) collective-permute-start(bf16[96,2176]{1,0:T(8,128)(2,1)} %collective-permute-done.31.refs_0_), channel_id=1, source_target_pairs={{0,4},{1,5},{4,8},{5,9},{8,12},{9,13},{12,14},{13,15},{14,10},{15,... | collective-permute-start | bytes 1253384 | tf_op jit(solution)/shard_map/ppermute | solution.py:358
  86.3 9.4 %collective-permute-start.37 = (bf16[96,2176]{1,0:T(8,128)(2,1)}, bf16[96,2176]{1,0:T(8,128)(2,1)}, u32[]{:S(2)}, u32[]{:S(2)}) collective-permute-start(bf16[96,2176]{1,0:T(8,128)(2,1)} %collective-permute-done.32.refs_1_), channel_id=1, source_target_pairs={{0,2},{1,3},{4,0},{5,1},{8,4},{9,5},{12,8},{13,9},{14,12},{15,13},... | collective-permute-start | bytes 1253384 | tf_op jit(solution)/shard_map/ppermute | solution.py:359
  86.8 11.4 %collective-permute-start.33 = (bf16[96,2176]{1,0:T(8,128)(2,1)}, bf16[96,2176]{1,0:T(8,128)(2,1)}, u32[]{:S(2)}, u32[]{:S(2)}) collective-permute-start(bf16[96,2176]{1,0:T(8,128)(2,1)} %collective-permute-done.31.refs_0_), channel_id=1, source_target_pairs={{0,1},{1,0},{2,3},{3,2},{4,5},{5,4},{6,7},{7,6},{8,9},{9,8},{10,11... | collective-permute-start | bytes 1253384 | tf_op jit(solution)/shard_map/ppermute | solution.py:360
  86.8 13.0 %collective-permute-start.34 = (bf16[96,2176]{1,0:T(8,128)(2,1)}, bf16[96,2176]{1,0:T(8,128)(2,1)}, u32[]{:S(2)}, u32[]{:S(2)}) collective-permute-start(bf16[96,2176]{1,0:T(8,128)(2,1)} %collective-permute-done.32.refs_1_), channel_id=1, source_target_pairs={{0,1},{1,0},{2,3},{3,2},{4,5},{5,4},{6,7},{7,6},{8,9},{9,8},{10,11... | collective-permute-start | bytes 1253384 | tf_op jit(solution)/shard_map/ppermute | solution.py:360
  94.5 15.6 %collective-permute-start.38 = (bf16[96,2176]{1,0:T(8,128)(2,1)}, bf16[96,2176]{1,0:T(8,128)(2,1)}, u32[]{:S(2)}, u32[]{:S(2)}) collective-permute-start(bf16[96,2176]{1,0:T(8,128)(2,1)} %collective-permute-done.36.refs_0_), channel_id=1, source_target_pairs={{0,1},{1,0},{2,3},{3,2},{4,5},{5,4},{6,7},{7,6},{8,9},{9,8},{10,11... | collective-permute-start | bytes 1253384 | tf_op jit(solution)/shard_map/ppermute | solution.py:360
  95.8 14.4 %collective-permute-start.39 = (bf16[96,2176]{1,0:T(8,128)(2,1)}, bf16[96,2176]{1,0:T(8,128)(2,1)}, u32[]{:S(2)}, u32[]{:S(2)}) collective-permute-start(bf16[96,2176]{1,0:T(8,128)(2,1)} %collective-permute-done.37.refs_1_), channel_id=1, source_target_pairs={{0,1},{1,0},{2,3},{3,2},{4,5},{5,4},{6,7},{7,6},{8,9},{9,8},{10,11... | collective-permute-start | bytes 1253384 | tf_op jit(solution)/shard_map/ppermute | solution.py:360
  95.8 23.0 %collective-permute-start.28 = (bf16[96,2176]{1,0:T(8,128)(2,1)}, bf16[96,2176]{1,0:T(8,128)(2,1)S(1)}, u32[]{:S(2)}, u32[]{:S(2)}) collective-permute-start(bf16[96,2176]{1,0:T(8,128)(2,1)} %copy-done.13), channel_id=1, source_target_pairs={{0,1},{1,0},{2,3},{3,2},{4,5},{5,4},{6,7},{7,6},{8,9},{9,8},{10,11... | collective-permute-start | bytes 1253384 | tf_op jit(solution)/shard_map/ppermute | solution.py:360
  98.2 11.3 %collective-permute-start.41 = (bf16[48,2176]{1,0:T(8,128)(2,1)S(1)}, bf16[48,2176]{1,0:T(8,128)(2,1)S(1)}, u32[]{:S(2)}, u32[]{:S(2)}) collective-permute-start(bf16[48,2176]{1,0:T(8,128)(2,1)S(1)} %slice.78), channel_id=1, source_target_pairs={{0,4},{1,5},{4,8},{5,9},{8,12},{9,13},{12,14},{13,15},{14,10},{15,... | collective-permute-start | bytes 626696 | tf_op jit(solution)/shard_map/ppermute | solution.py:358
  99.8 9.8 %collective-permute-start.42 = (bf16[48,2176]{1,0:T(8,128)(2,1)S(1)}, bf16[48,2176]{1,0:T(8,128)(2,1)S(1)}, u32[]{:S(2)}, u32[]{:S(2)}) collective-permute-start(bf16[48,2176]{1,0:T(8,128)(2,1)S(1)} %slice.79), channel_id=1, source_target_pairs={{0,2},{1,3},{4,0},{5,1},{8,4},{9,5},{12,8},{13,9},{14,12},{15,13},... | collective-permute-start | bytes 626696 | tf_op jit(solution)/shard_map/ppermute | solution.py:359
  109.5 9.3 %collective-permute-start.29 = (bf16[96,2176]{1,0:T(8,128)(2,1)S(1)}, bf16[96,2176]{1,0:T(8,128)(2,1)S(1)}, u32[]{:S(2)}, u32[]{:S(2)}) collective-permute-start(bf16[96,2176]{1,0:T(8,128)(2,1)S(1)} %copy-done.16), channel_id=1, source_target_pairs={{0,1},{1,0},{2,3},{3,2},{4,5},{5,4},{6,7},{7,6},{8,9},{9,8},{10,11... | collective-permute-start | bytes 1253384 | tf_op jit(solution)/shard_map/ppermute | solution.py:360
  109.6 30.1 %collective-permute-start.35 = (bf16[192,2048]{1,0:T(8,128)(2,1)S(1)}, bf16[192,2048]{1,0:T(8,128)(2,1)S(1)}, u32[]{:S(2)}, u32[]{:S(2)}) collective-permute-start(bf16[192,2048]{1,0:T(8,128)(2,1)S(1)} %get-tuple-element.40), channel_id=1, source_target_pairs={{0,1},{1,0},{2,3},{3,2},{4,5},{5,4},{6,7},{7,6},{8,9},{9,8},{10,11... | collective-permute-start | bytes 2359304 | tf_op jit(solution)/shard_map/ppermute | solution.py:362
  110.1 5.9 %collective-permute-start.43 = (bf16[48,2176]{1,0:T(8,128)(2,1)S(1)}, bf16[48,2176]{1,0:T(8,128)(2,1)S(1)}, u32[]{:S(2)}, u32[]{:S(2)}) collective-permute-start(bf16[48,2176]{1,0:T(8,128)(2,1)S(1)} %collective-permute-done.41.refs_0_), channel_id=1, source_target_pairs={{0,1},{1,0},{2,3},{3,2},{4,5},{5,4},{6,7},{7,6},{8,9},{9,8},{10,11... | collective-permute-start | bytes 626696 | tf_op jit(solution)/shard_map/ppermute | solution.py:360
  110.1 5.9 %collective-permute-start.44 = (bf16[48,2176]{1,0:T(8,128)(2,1)S(1)}, bf16[48,2176]{1,0:T(8,128)(2,1)S(1)}, u32[]{:S(2)}, u32[]{:S(2)}) collective-permute-start(bf16[48,2176]{1,0:T(8,128)(2,1)S(1)} %collective-permute-done.42.refs_1_), channel_id=1, source_target_pairs={{0,1},{1,0},{2,3},{3,2},{4,5},{5,4},{6,7},{7,6},{8,9},{9,8},{10,11... | collective-permute-start | bytes 626696 | tf_op jit(solution)/shard_map/ppermute | solution.py:360
  115.9 14.8 %collective-permute-start.40 = (bf16[192,2048]{1,0:T(8,128)(2,1)S(1)}, bf16[192,2048]{1,0:T(8,128)(2,1)S(1)}, u32[]{:S(2)}, u32[]{:S(2)}) collective-permute-start(bf16[192,2048]{1,0:T(8,128)(2,1)S(1)} %get-tuple-element.42), channel_id=1, source_target_pairs={{0,1},{1,0},{2,3},{3,2},{4,5},{5,4},{6,7},{7,6},{8,9},{9,8},{10,11... | collective-permute-start | bytes 2359304 | tf_op jit(solution)/shard_map/ppermute | solution.py:362
  118.2 5.1 %collective-permute-start.45 = (bf16[96,2048]{1,0:T(8,128)(2,1)S(1)}, bf16[96,2048]{1,0:T(8,128)(2,1)S(1)}, u32[]{:S(2)}, u32[]{:S(2)}) collective-permute-start(bf16[96,2048]{1,0:T(8,128)(2,1)S(1)} %get-tuple-element.44), channel_id=1, source_target_pairs={{0,1},{1,0},{2,3},{3,2},{4,5},{5,4},{6,7},{7,6},{8,9},{9,8},{10,11... | collective-permute-start | bytes 1179656 | tf_op jit(solution)/shard_map/ppermute | solution.py:362
  122.7 25.1 %collective-permute-start.30 = (bf16[192,2048]{1,0:T(8,128)(2,1)S(1)}, bf16[192,2048]{1,0:T(8,128)(2,1)S(1)}, u32[]{:S(2)}, u32[]{:S(2)}) collective-permute-start(bf16[192,2048]{1,0:T(8,128)(2,1)S(1)} %get-tuple-element.38), channel_id=1, source_target_pairs={{0,1},{1,0},{2,3},{3,2},{4,5},{5,4},{6,7},{7,6},{8,9},{9,8},{10,11... | collective-permute-start | bytes 2359304 | tf_op jit(solution)/shard_map/ppermute | solution.py:362
  122.8 9.7 %collective-permute-start.24 = (bf16[96,2176]{1,0:T(8,128)(2,1)S(1)}, bf16[96,2176]{1,0:T(8,128)(2,1)S(1)}, u32[]{:S(2)}, u32[]{:S(2)}) collective-permute-start(bf16[96,2176]{1,0:T(8,128)(2,1)S(1)} %copy-done.8), channel_id=1, source_target_pairs={{0,1},{1,0},{2,3},{3,2},{4,5},{5,4},{6,7},{7,6},{8,9},{9,8},{10,11... | collective-permute-start | bytes 1253384 | tf_op jit(solution)/shard_map/ppermute | solution.py:353
  123.3 6.9 %collective-permute-start.46 = (bf16[48,2048]{1,0:T(8,128)(2,1)S(1)}, bf16[48,2048]{1,0:T(8,128)(2,1)S(1)}, u32[]{:S(2)}, u32[]{:S(2)}) collective-permute-start(bf16[48,2048]{1,0:T(8,128)(2,1)S(1)} %add.24), channel_id=1, source_target_pairs={{0,4},{1,5},{4,8},{5,9},{8,12},{9,13},{12,14},{13,15},{14,10},{15,... | collective-permute-start | bytes 589832 | tf_op jit(solution)/shard_map/ppermute | solution.py:372
  130.3 7.8 %collective-permute-start.56 = (bf16[48,2048]{1,0:T(8,128)(2,1)S(1)}, bf16[48,2048]{1,0:T(8,128)(2,1)S(1)}, u32[]{:S(2)}, u32[]{:S(2)}) collective-permute-start(bf16[48,2048]{1,0:T(8,128)(2,1)S(1)} %add.34), channel_id=1, source_target_pairs={{0,2},{1,3},{4,0},{5,1},{8,4},{9,5},{12,8},{13,9},{14,12},{15,13},... | collective-permute-start | bytes 589832 | tf_op jit(solution)/shard_map/ppermute | solution.py:373
  130.8 11.7 %collective-permute-start.47 = (bf16[48,2048]{1,0:T(8,128)(2,1)S(1)}, bf16[48,2048]{1,0:T(8,128)(2,1)S(1)}, u32[]{:S(2)}, u32[]{:S(2)}) collective-permute-start(bf16[48,2048]{1,0:T(8,128)(2,1)S(1)} %add.25), channel_id=1, source_target_pairs={{0,4},{1,5},{4,8},{5,9},{8,12},{9,13},{12,14},{13,15},{14,10},{15,... | collective-permute-start | bytes 589832 | tf_op jit(solution)/shard_map/ppermute | solution.py:367
  132.5 11.7 %collective-permute-start.50 = (bf16[48,2048]{1,0:T(8,128)(2,1)S(1)}, bf16[48,2048]{1,0:T(8,128)(2,1)S(1)}, u32[]{:S(2)}, u32[]{:S(2)}) collective-permute-start(bf16[48,2048]{1,0:T(8,128)(2,1)S(1)} %add.28), channel_id=1, source_target_pairs={{0,2},{1,3},{4,0},{5,1},{8,4},{9,5},{12,8},{13,9},{14,12},{15,13},... | collective-permute-start | bytes 589832 | tf_op jit(solution)/shard_map/ppermute | solution.py:367
  138.1 7.5 %collective-permute-start.53 = (bf16[48,2048]{1,0:T(8,128)(2,1)S(1)}, bf16[48,2048]{1,0:T(8,128)(2,1)S(1)}, u32[]{:S(2)}, u32[]{:S(2)}) collective-permute-start(bf16[48,2048]{1,0:T(8,128)(2,1)S(1)} %add.31), channel_id=1, source_target_pairs={{0,4},{1,5},{4,8},{5,9},{8,12},{9,13},{12,14},{13,15},{14,10},{15,... | collective-permute-start | bytes 589832 | tf_op jit(solution)/shard_map/ppermute | solution.py:367
  139.6 6.5 %collective-permute-start.57 = (bf16[48,2048]{1,0:T(8,128)(2,1)S(1)}, bf16[48,2048]{1,0:T(8,128)(2,1)S(1)}, u32[]{:S(2)}, u32[]{:S(2)}) collective-permute-start(bf16[48,2048]{1,0:T(8,128)(2,1)S(1)} %add.35), channel_id=1, source_target_pairs={{0,2},{1,3},{4,0},{5,1},{8,4},{9,5},{12,8},{13,9},{14,12},{15,13},... | collective-permute-start | bytes 589832 | tf_op jit(solution)/shard_map/ppermute | solution.py:367
  142.6 6.3 %collective-permute-start.48 = (bf16[48,2048]{1,0:T(8,128)(2,1)S(1)}, bf16[48,2048]{1,0:T(8,128)(2,1)S(1)}, u32[]{:S(2)}, u32[]{:S(2)}) collective-permute-start(bf16[48,2048]{1,0:T(8,128)(2,1)S(1)} %add.26), channel_id=1, source_target_pairs={{0,4},{1,5},{4,8},{5,9},{8,12},{9,13},{12,14},{13,15},{14,10},{15,... | collective-permute-start | bytes 589832 | tf_op jit(solution)/shard_map/ppermute | solution.py:367
  144.2 14.0 %collective-permute-start.25 = (bf16[96,2048]{1,0:T(8,128)(2,1)S(1)}, bf16[96,2048]{1,0:T(8,128)(2,1)S(1)}, u32[]{:S(2)}, u32[]{:S(2)}) collective-permute-start(bf16[96,2048]{1,0:T(8,128)(2,1)S(1)} %get-tuple-element.36), channel_id=1, source_target_pairs={{0,1},{1,0},{2,3},{3,2},{4,5},{5,4},{6,7},{7,6},{8,9},{9,8},{10,11... | collective-permute-start | bytes 1179656 | tf_op jit(solution)/shard_map/ppermute | solution.py:362
  145.6 7.8 %collective-permute-start.51 = (bf16[48,2048]{1,0:T(8,128)(2,1)S(1)}, bf16[48,2048]{1,0:T(8,128)(2,1)S(1)}, u32[]{:S(2)}, u32[]{:S(2)}) collective-permute-start(bf16[48,2048]{1,0:T(8,128)(2,1)S(1)} %add.29), channel_id=1, source_target_pairs={{0,2},{1,3},{4,0},{5,1},{8,4},{9,5},{12,8},{13,9},{14,12},{15,13},... | collective-permute-start | bytes 589832 | tf_op jit(solution)/shard_map/ppermute | solution.py:367
  146.2 7.8 %collective-permute-start.54 = (bf16[48,2048]{1,0:T(8,128)(2,1)S(1)}, bf16[48,2048]{1,0:T(8,128)(2,1)S(1)}, u32[]{:S(2)}, u32[]{:S(2)}) collective-permute-start(bf16[48,2048]{1,0:T(8,128)(2,1)S(1)} %add.32), channel_id=1, source_target_pairs={{0,4},{1,5},{4,8},{5,9},{8,12},{9,13},{12,14},{13,15},{14,10},{15,... | collective-permute-start | bytes 589832 | tf_op jit(solution)/shard_map/ppermute | solution.py:367
  147.8 9.7 %collective-permute-start.58 = (bf16[48,2048]{1,0:T(8,128)(2,1)S(1)}, bf16[48,2048]{1,0:T(8,128)(2,1)S(1)}, u32[]{:S(2)}, u32[]{:S(2)}) collective-permute-start(bf16[48,2048]{1,0:T(8,128)(2,1)S(1)} %add.36), channel_id=1, source_target_pairs={{0,2},{1,3},{4,0},{5,1},{8,4},{9,5},{12,8},{13,9},{14,12},{15,13},... | collective-permute-start | bytes 589832 | tf_op jit(solution)/shard_map/ppermute | solution.py:367
  149.0 9.2 %collective-permute-start.49 = (bf16[48,2048]{1,0:T(8,128)(2,1)S(1)}, bf16[48,2048]{1,0:T(8,128)(2,1)S(1)}, u32[]{:S(2)}, u32[]{:S(2)}) collective-permute-start(bf16[48,2048]{1,0:T(8,128)(2,1)S(1)} %add.27), channel_id=1, source_target_pairs={{0,4},{1,5},{4,8},{5,9},{8,12},{9,13},{12,14},{13,15},{14,10},{15,... | collective-permute-start | bytes 589832 | tf_op jit(solution)/shard_map/ppermute | solution.py:367
  153.4 8.3 %collective-permute-start.52 = (bf16[48,2048]{1,0:T(8,128)(2,1)S(1)}, bf16[48,2048]{1,0:T(8,128)(2,1)S(1)}, u32[]{:S(2)}, u32[]{:S(2)}) collective-permute-start(bf16[48,2048]{1,0:T(8,128)(2,1)S(1)} %add.30), channel_id=1, source_target_pairs={{0,2},{1,3},{4,0},{5,1},{8,4},{9,5},{12,8},{13,9},{14,12},{15,13},... | collective-permute-start | bytes 589832 | tf_op jit(solution)/shard_map/ppermute | solution.py:367
  154.1 10.2 %copy-start.6 = (f32[96,2048]{1,0:T(8,128)S(1)}, f32[96,2048]{1,0:T(8,128)}, u32[]{:S(2)}) copy-start(f32[96,2048]{1,0:T(8,128)} %copy-done.5) | copy-start | bytes 2359300
  154.1 7.7 %collective-permute-start.55 = (bf16[48,2048]{1,0:T(8,128)(2,1)S(1)}, bf16[48,2048]{1,0:T(8,128)(2,1)S(1)}, u32[]{:S(2)}, u32[]{:S(2)}) collective-permute-start(bf16[48,2048]{1,0:T(8,128)(2,1)S(1)} %add.33), channel_id=1, source_target_pairs={{0,4},{1,5},{4,8},{5,9},{8,12},{9,13},{12,14},{13,15},{14,10},{15,... | collective-permute-start | bytes 589832 | tf_op jit(solution)/shard_map/ppermute | solution.py:367
  157.6 6.7 %collective-permute-start.59 = (bf16[48,2048]{1,0:T(8,128)(2,1)S(1)}, bf16[48,2048]{1,0:T(8,128)(2,1)S(1)}, u32[]{:S(2)}, u32[]{:S(2)}) collective-permute-start(bf16[48,2048]{1,0:T(8,128)(2,1)S(1)} %add.37), channel_id=1, source_target_pairs={{0,2},{1,3},{4,0},{5,1},{8,4},{9,5},{12,8},{13,9},{14,12},{15,13},... | collective-permute-start | bytes 589832 | tf_op jit(solution)/shard_map/ppermute | solution.py:367
  (14 other events, 51.6 us)

commit v3 on v2

--- a/solution.py
+++ b/solution.py
@@ -92,20 +92,17 @@
     return max(t for t in range(LANES, most + 1, LANES) if extent % t == 0)
 
 
-def serve_body(blocks, expert_ref, *refs):
+def serve_body(columns, share_ref, *refs):
+    blocks = len(columns)
     ins = refs[:blocks]
     gate_ref, up_ref, down_ref, own_ref, other_ref, x_ref, h_ref = refs[blocks:]
     width, wide = gate_ref.shape
     start = 0
     share = []
-    for ref in ins:
-        size = ref.shape[0]
-        x_ref[start : start + size, :] = ref[:, :width]
-        tags = ref[:, width:].astype(jnp.float32)
-        mine = lax.broadcasted_iota(jnp.int32, tags.shape, 1) == expert_ref[0]
-        chosen = jnp.sum(jnp.where(mine, tags, 0.0), axis=1, keepdims=True)
-        share.append(chosen / jnp.sum(tags, axis=1, keepdims=True))
-        start += size
+    for ref, (column, low, high) in zip(ins, columns):
+        x_ref[start : start + high - low, :] = ref[...]
+        share.append(share_ref[low:high, column : column + 1])
+        start += high - low
     share = jnp.concatenate(share, axis=0)
     tile = tile_of(wide, 256)
     for at in range(0, wide, tile):
@@ -124,13 +121,13 @@
 VMEM = pl.BlockSpec(memory_space=pltpu.VMEM)
 
 
-def serve(ins, expert, experts):
+def serve(ins, columns, share, experts):
     rows = sum(x.shape[0] for x in ins)
     width, wide = experts[0].shape
     return pl.pallas_call(
-        functools.partial(serve_body, len(ins)),
+        functools.partial(serve_body, columns),
         out_shape=[jax.ShapeDtypeStruct((rows // 2, width), jnp.bfloat16)] * 2,
-        in_specs=[pl.BlockSpec(memory_space=pltpu.SMEM)] + [VMEM] * (len(ins) + 3),
+        in_specs=[VMEM] * (len(ins) + 4),
         out_specs=[VMEM, VMEM],
         scratch_shapes=[pltpu.VMEM((rows, width), jnp.bfloat16), pltpu.VMEM((rows, wide), jnp.bfloat16)],
         compiler_params=pltpu.CompilerParams(vmem_limit_bytes=VMEM_LIMIT),
@@ -138,7 +135,7 @@
             flops=6 * rows * width * wide, bytes_accessed=6 * width * wide, transcendentals=rows * wide
         ),
         name="serve",
-    )(expert, *ins, *experts)
+    )(share, *ins, *experts)
 
 
 def bulk_body(offsets, act_ref, *refs):
@@ -199,8 +196,9 @@
 
 
 def norm_body(parts, *refs):
-    bias_ref, gain_ref, tags_ref, merged_ref, block_ref = refs[3 * parts :]
+    bias_ref, gain_ref, merged_ref, low_ref, high_ref = refs[3 * parts :]
     width = merged_ref.shape[1]
+    cut = low_ref.shape[0]
     at = 0
     square = 0.0
     for index in range(parts):
@@ -211,25 +209,23 @@
         square += jnp.sum(merged * merged, axis=1, keepdims=True)
         at = to
     scale = lax.rsqrt(square / width + 1e-06)
-    block_ref[:, :width] = (merged_ref[...] * scale * gain_ref[...]).astype(jnp.bfloat16)
-    block_ref[:, width:] = tags_ref[...]
-
-
-def normalize(parts, bias, gain, tags):
-    rows = tags.shape[0]
+    low_ref[...] = (merged_ref[:cut, :] * scale[:cut] * gain_ref[...]).astype(jnp.bfloat16)
+    high_ref[...] = (merged_ref[cut:, :] * scale[cut:] * gain_ref[...]).astype(jnp.bfloat16)
+
+
+def normalize(parts, bias, gain):
+    rows = parts[0][0].shape[0]
     width = bias.shape[0]
     flat = [array for part in parts for array in part]
+    half = jax.ShapeDtypeStruct((rows // 2, width), jnp.bfloat16)
     return pl.pallas_call(
         functools.partial(norm_body, len(parts)),
-        out_shape=[
-            jax.ShapeDtypeStruct((rows, width), jnp.float32),
-            jax.ShapeDtypeStruct((rows, width + tags.shape[1]), jnp.bfloat16),
-        ],
-        in_specs=[VMEM] * (len(flat) + 3),
-        out_specs=[VMEM, VMEM],
+        out_shape=[jax.ShapeDtypeStruct((rows, width), jnp.float32), half, half],
+        in_specs=[VMEM] * (len(flat) + 2),
+        out_specs=[VMEM] * 3,
         compiler_params=pltpu.CompilerParams(vmem_limit_bytes=VMEM_LIMIT),
         name="normalize",
-    )(*flat, bias[None], gain[None], tags)
+    )(*flat, bias[None], gain[None])
 
 
 VMEM_LIMIT = 24 * 1024 * 1024
@@ -257,14 +253,13 @@
     )(*ins)
 
 
-def finish_body(merged_ref, own_ref, other_ref, *refs):
+def finish_body(merged_ref, *refs):
     out_ref = refs[-1]
     at = 0
-    for index in range(0, len(refs) - 1, 2):
-        first, second = refs[index], refs[index + 1]
-        to = at + first.shape[0]
-        total = own_ref[at:to, :].astype(jnp.float32) + other_ref[at:to, :].astype(jnp.float32)
-        total += first[...].astype(jnp.float32) + second[...].astype(jnp.float32)
+    for index in range(0, len(refs) - 1, 4):
+        ins = refs[index : index + 4]
+        to = at + ins[0].shape[0]
+        total = sum(ref[...].astype(jnp.float32) for ref in ins)
         out_ref[at:to, :] = (merged_ref[at:to, :] + total).astype(jnp.bfloat16)
         at = to
 
@@ -324,10 +319,6 @@
     act = jnp.concatenate([kept, cross(given)], axis=0)
     act = around(act.transpose(1, 0, 2), spot)
 
-    lanes = jnp.arange(-(-n // LANES) * LANES, dtype=jnp.int32)
-    named = expert_ids[:, :, None] == lanes[None, None, :]
-    tags = jnp.sum(jnp.where(named, combine_ints[:, :, None], 0), axis=1).astype(jnp.bfloat16)
-
     mid = (half + 15) // 16 * 8
     streams = []
     for part in range(PARTS):
@@ -343,35 +334,52 @@
         total = bulk(act, offsets, pieces)
         own, own_other, theirs, theirs_other = last(act, far, total, top, bottom)
         theirs = (theirs + swap(theirs_other)).astype(jnp.bfloat16)
-        streams.append((own, swap(own_other), cross(theirs)))
-    merged, block = normalize(streams, merger_bias, norm_gain, tags)
+        theirs = cross(theirs)
+        streams.append((own, swap(own_other), theirs))
+    merged, *block = normalize(streams, merger_bias, norm_gain)
+
+    counts = combine_ints.astype(jnp.float32)
+    weights = counts / jnp.sum(counts, axis=1, keepdims=True)
+    named = expert_ids[:, :, None] == jnp.arange(n, dtype=jnp.int32)[None, None, :]
+    spread = jnp.sum(jnp.where(named, weights[:, :, None], 0.0), axis=1)
+    share = lax.all_to_all(spread.T, "dp", split_axis=0, concat_axis=0, tiled=True)
+    share = share.reshape(chips, 2, rows)
+    share = jnp.where(first_core, share, share[:, ::-1])
+    share = around(share, spot).reshape(n, rows).T
 
     experts = [w[0] for w in (gate_weight, up_weight, down_weight)]
-    expert = me.astype(jnp.int32)[None]
     cut = rows // 2
-    left = right = block
-    other = swap(block)
-    outs = [serve([block, other], expert, experts)]
-    for step in range(1, far + 1):
-        if step == far:
-            left, right = left[:cut], right[cut:]
-        left = ahead(left)
-        right = back(right)
-        others = swap(left), swap(right)
-        outs.append(serve([left, right, *others], expert, experts))
-    outs = [(own, swap(other)) for own, other in outs]
-
-    def home(way, at, low, total):
+    spans = [(0, cut), (cut, rows)]
+    outs = []
+    left, right = list(block), list(block)
+    for half, span in enumerate(spans):
+        outs.append([serve([block[half], swap(block[half])], [(0, *span), (1, *span)], share, experts)])
+    for step in range(1, far):
+        lo, hi = 2 * (chips - step), 2 * step
+        for half, span in enumerate(spans):
+            left[half] = ahead(left[half])
+            right[half] = back(right[half])
+            others = swap(left[half]), swap(right[half])
+            columns = [(lo, *span), (hi, *span), (lo + 1, *span), (hi + 1, *span)]
+            outs[half].append(serve([left[half], right[half], *others], columns, share, experts))
+    top = ahead(left[0])
+    bottom = back(right[1])
+    columns = [(2 * far + side, *span) for side in (0, 1) for span in spans]
+    distant = serve([top, bottom, swap(top), swap(bottom)], columns, share, experts)
+    distant = (distant[0], swap(distant[1]))
+    outs = [[(own, swap(other)) for own, other in pairs] for pairs in outs]
+
+    def home(way, half, at, total):
         for step in reversed(range(1, far)):
-            total = add(*outs[step], at + low, cut, total)
+            total = add(*outs[half][step], at, cut, total)
             total = way(total)
         return total
 
-    ahead_high = home(ahead, rows, cut, None)
+    ahead_high = home(ahead, 1, cut, None)
     back_low = home(back, 0, 0, None)
-    ahead_low = home(ahead, rows, 0, ahead(add(*outs[far], 0, cut, None)))
-    back_high = home(back, 0, cut, back(add(*outs[far], cut, cut, None)))
-    return finish(merged, *outs[0], ahead_low, back_low, ahead_high, back_high)
+    ahead_low = home(ahead, 0, cut, ahead(add(*distant, 0, cut, None)))
+    back_high = home(back, 1, 0, back(add(*distant, cut, cut, None)))
+    return finish(merged, *outs[0][0], ahead_low, back_low, *outs[1][0], ahead_high, back_high)
 
 
 def shards(*arrays):

time: 166 us -> 169 us (1.018)
  waiting for transfers between devices: 69 us -> 57 us
  blocking collectives: 0 us -> 10.1 us
  starting transfers between devices: 48.9 us -> 55.9 us
  Pallas kernels: 27.9 us -> 33.3 us
  local copies, waits for them, and re-layouts: 12.7 us -> 7.66 us
  other arithmetic: 6.36 us -> 4 us
    ppermute x10 -> x6, waiting for transfers between devices: 35.6 us -> 10.9 us  [dense(): left = ahead(left)]
    ppermute x20 -> x45, starting transfers between devices: 7.91 us -> 23.2 us  [the longest x6 6.43 us: dense(): left[half] = ahead(left[half])]
    ppermute x20 -> x45, waiting for transfers between devices: 15.3 us -> 30.1 us  [the longest x6 11.9 us: dense(): left[half] = ahead(left[half])]
    all_to_all x0 -> x1, blocking collectives: none -> 10.1 us  [dense(): lax.all_to_all(spread.T, 'dp', split_axis=0, concat_axis=0, tiled=True)]
    pallas_call x5 -> x9, Pallas kernels: 18.9 us -> 26.3 us  [serve(): pl.pallas_call(functools.partial(serve_body, columns), out_shape=[jax.Sha...]
    ppermute x10 -> x6, starting transfers between devices: 17.3 us -> 11 us  [dense(): left = ahead(left)]
    unnamed x41 -> x29, local copies, waits for them, and re-layouts: 10.6 us -> 7.35 us
    ppermute x10 -> x6, starting transfers between devices: 4.18 us -> 2.26 us  [dense(): right = back(right)]
  transfers between devices with their start and end apart: 60 -> 77, of which waited for: 21 -> 26; matrix products, arithmetic and copies ran while one was open for 5% -> 1% of each run, Pallas kernels for 15% -> 19%
where the time goes in v3:
time: 169 us
  waiting for transfers between devices  57 us (34%)
  starting transfers between devices  55.9 us (33%)
  Pallas kernels  33.3 us (20%)
  blocking collectives  10.1 us (6%)
  local copies, waits for them, and re-layouts  7.66 us (5%)
  other arithmetic  4 us (2%)
    pallas_call x9, Pallas kernels, serve(): pl.pallas_call(functools.partial(serve_body, columns), out_shape=[jax.Sha...  26.3 us
    ppermute x12, starting transfers between devices, home(): total = way(total)  12.6 us
    ppermute x6, waiting for transfers between devices, dense(): left[half] = ahead(left[half])  11.9 us
    ppermute x12, waiting for transfers between devices, home(): total = way(total)  11.7 us
    ppermute x6, starting transfers between devices, dense(): left = ahead(left)  11 us
    ppermute x6, waiting for transfers between devices, dense(): left = ahead(left)  10.9 us
    all_to_all x1, blocking collectives, dense(): lax.all_to_all(spread.T, 'dp', split_axis=0, concat_axis=0, tiled=True)  10.1 us
    ppermute x2, waiting for transfers between devices, dense(): theirs = cross(theirs)  9.28 us
  transfers between devices with their start and end apart: 77, of which 26 were waited for; matrix products, arithmetic and copies ran while one was open for 1% of the time, Pallas kernels for 19%

profile of v3, /device:TPU:0, one launch (start us, length us, event | category | flops | bytes accessed | tf_op | source)
XLA Modules:
  0.0 168.5 jit_solution(4181303797805842059)
XLA Ops:
  0.0 1.3 copy.24
  1.3 2.6 %fusion.1 = bf16[96,2304]{0,1:T(8,128)(2,1)S(1)} fusion(bf16[96,2304]{0,1:T(8,128)(2,1)S(1)} %copy.24), kind=kLoop, calls=%fused_computation.8 | loop fusion | flops 14598144 | bytes 884736 | tf_op jit(solution)/shard_map/convert_element_type | solution.py:312
  5.4 3.1 %collective-permute-start.2 = (bf16[72,1024]{1,0:T(8,128)(2,1)S(1)}, bf16[72,1024]{1,0:T(8,128)(2,1)S(1)}, u32[]{:S(2)}, u32[]{:S(2)}) collective-permute-start(bf16[72,1024]{1,0:T(8,128)(2,1)S(1)} %get-tuple-element.72.refs_0_), channel_id=1, source_target_pairs={{0,4},{1,5},{4,8},{5,9},{8,12},{9,13},{12,14},{13,15},{14,10},{15,... | collective-permute-start | bytes 442376 | tf_op jit(solution)/shard_map/ppermute | solution.py:328
  8.7 2.0 %collective-permute-start.1 = (bf16[192,8,72]{2,0,1:T(8,128)(2,1)S(1)}, bf16[192,8,72]{2,0,1:T(8,128)(2,1)S(1)}, u32[]{:S(2)}, u32[]{:S(2)}) collective-permute-start(bf16[192,8,72]{2,0,1:T(8,128)(2,1)S(1)} %get-tuple-element.66), channel_id=1, source_target_pairs={{0,16},{16,0},{1,17},{17,1},{2,18},{18,2},{3,19},{19,3},{4,20},{20... | collective-permute-start | bytes 663560 | tf_op jit(solution)/shard_map/ppermute | solution.py:319
  10.7 1.6 collective-permute-start.13
  12.8 1.6 collective-permute-start.4
  14.8 2.7 %collective-permute-done.13.refs_1_ = bf16[72,1024]{1,0:T(8,128)(2,1)S(1)} collective-permute-done((bf16[72,1024]{1,0:T(8,128)(2,1)S(1)}, bf16[72,1024]{1,0:T(8,128)(2,1)S(1)}, u32[]{:S(2)}, u32[]{:S(2)}) %collective-permute-start.13) | collective-permute-done | bytes 147488 | tf_op jit(solution)/shard_map/ppermute | solution.py:328
  17.5 1.6 collective-permute-start.15
  19.5 1.1 collective-permute-done.4.refs_3_
  20.6 1.6 collective-permute-start.6
  22.9 3.0 %collective-permute-done.6.refs_5_ = bf16[72,1024]{1,0:T(8,128)(2,1)S(1)} collective-permute-done((bf16[72,1024]{1,0:T(8,128)(2,1)S(1)}, bf16[72,1024]{1,0:T(8,128)(2,1)S(1)}, u32[]{:S(2)}, u32[]{:S(2)}) %collective-permute-start.6) | collective-permute-done | bytes 147488 | tf_op jit(solution)/shard_map/ppermute | solution.py:328
  25.9 1.6 collective-permute-start.8
  28.2 0.7 fusion.33.act_ref
  28.9 1.6 bulk.2.total_ref
  30.4 1.6 collective-permute-done.9.bottom_ref
  32.7 1.6 collective-permute-start.17
  34.7 4.2 %collective-permute-done.17.refs_5_ = bf16[72,1024]{1,0:T(8,128)(2,1)S(1)} collective-permute-done((bf16[72,1024]{1,0:T(8,128)(2,1)S(1)}, bf16[72,1024]{1,0:T(8,128)(2,1)S(1)}, u32[]{:S(2)}, u32[]{:S(2)}) %collective-permute-start.17) | collective-permute-done | bytes 147488 | tf_op jit(solution)/shard_map/ppermute | solution.py:328
  38.9 1.6 collective-permute-start.19
  41.0 1.5 bulk.3.total_ref
  42.5 2.3 %collective-permute-done.20.bottom_ref = bf16[32,1024]{1,0:T(8,128)(2,1)S(1)} collective-permute-done((bf16[32,1024]{1,0:T(8,128)(2,1)S(1)}, bf16[32,1024]{1,0:T(8,128)(2,1)S(1)}, u32[]{:S(2)}, u32[]{:S(2)}) %collective-permute-start.20) | collective-permute-done | bytes 65568 | tf_op jit(solution)/shard_map/ppermute | solution.py:333
  46.1 1.0 collective-permute-start.12
  47.2 1.1 collective-permute-start.23
  48.3 5.6 %collective-permute-done.12.refs_2_ = bf16[96,1024]{1,0:T(8,128)(2,1)S(1)} collective-permute-done((bf16[96,1024]{1,0:T(8,128)(2,1)S(1)}, bf16[96,1024]{1,0:T(8,128)(2,1)S(1)}, u32[]{:S(2)}, u32[]{:S(2)}) %collective-permute-start.12) | collective-permute-done | bytes 196640 | tf_op jit(solution)/shard_map/ppermute | solution.py:337
  53.9 3.7 %collective-permute-done.23.refs_5_ = bf16[96,1024]{1,0:T(8,128)(2,1)S(1)} collective-permute-done((bf16[96,1024]{1,0:T(8,128)(2,1)S(1)}, bf16[96,1024]{1,0:T(8,128)(2,1)S(1)}, u32[]{:S(2)}, u32[]{:S(2)}) %collective-permute-start.23) | collective-permute-done | bytes 196640 | tf_op jit(solution)/shard_map/ppermute | solution.py:337
  57.6 0.9 normalize.1
  58.5 0.9 copy-done.4
  59.4 1.6 collective-permute-start.26
  62.0 1.6 collective-permute-start.58
  63.6 3.4 %collective-permute-done.26.refs_0_ = bf16[48,2048]{1,0:T(8,128)(2,1)} collective-permute-done((bf16[48,2048]{1,0:T(8,128)(2,1)}, bf16[48,2048]{1,0:T(8,128)(2,1)}, u32[]{:S(2)}, u32[]{:S(2)}) %collective-permute-start.26) | collective-permute-done | bytes 196640 | tf_op jit(solution)/shard_map/ppermute | solution.py:360
  67.0 1.6 collective-permute-start.31
  69.5 3.8 %collective-permute-done.42.refs_1_ = bf16[48,2048]{1,0:T(8,128)(2,1)} collective-permute-done((bf16[48,2048]{1,0:T(8,128)(2,1)S(1)}, bf16[48,2048]{1,0:T(8,128)(2,1)}, u32[]{:S(2)}, u32[]{:S(2)}) %collective-permute-start.42) | collective-permute-done | bytes 196640 | tf_op jit(solution)/shard_map/ppermute | solution.py:361
  73.8 10.1 %all_to_all.9 = f32[16,1,96]{2,1,0:T(1,128)S(1)} all-to-all(f32[16,1,96]{2,1,0:T(1,128)S(1)} %bitcast.71), channel_id=1, replica_groups=mesh['groups'=2,'dp'=16] {'dp'}, dimensions={0} | all-to-all | bytes 12288 | tf_op jit(solution)/shard_map/all_to_all | solution.py:345
  85.2 1.5 collective-permute-start.37
  86.6 1.5 collective-permute-start.44
  88.1 4.0 %collective-permute-done.62.refs_0_ = bf16[48,2048]{1,0:T(8,128)(2,1)} collective-permute-done((bf16[48,2048]{1,0:T(8,128)(2,1)}, bf16[48,2048]{1,0:T(8,128)(2,1)}, u32[]{:S(2)}, u32[]{:S(2)}) %collective-permute-start.62) | collective-permute-done | bytes 196640 | tf_op jit(solution)/shard_map/ppermute | solution.py:360
  92.7 3.7 %collective-permute-done.36.refs_0_ = bf16[48,2048]{1,0:T(8,128)(2,1)} collective-permute-done((bf16[48,2048]{1,0:T(8,128)(2,1)}, bf16[48,2048]{1,0:T(8,128)(2,1)}, u32[]{:S(2)}, u32[]{:S(2)}) %collective-permute-start.36) | collective-permute-done | bytes 196640 | tf_op jit(solution)/shard_map/ppermute | solution.py:360
  97.8 1.5 collective-permute-start.45
  99.3 0.7 collective-permute-done.66.refs_0_
  100.7 4.0 %collective-permute-done.41.refs_0_ = bf16[48,2048]{1,0:T(8,128)(2,1)} collective-permute-done((bf16[48,2048]{1,0:T(8,128)(2,1)}, bf16[48,2048]{1,0:T(8,128)(2,1)}, u32[]{:S(2)}, u32[]{:S(2)}) %collective-permute-start.41) | collective-permute-done | bytes 196640 | tf_op jit(solution)/shard_map/ppermute | solution.py:365
  105.4 1.9 %copy-done.1 = bf16[1,2048,768]{2,1,0:T(8,128)(2,1)S(1)} copy-done((bf16[1,2048,768]{2,1,0:T(8,128)(2,1)S(1)}, bf16[1,2048,768]{2,1,0:T(8,128)(2,1)}, u32[]{:S(2)}) %copy-start.1) | copy-done | bytes 3145752
  107.3 1.9 %copy-done.3 = bf16[1,768,2048]{2,1,0:T(8,128)(2,1)S(1)} copy-done((bf16[1,768,2048]{2,1,0:T(8,128)(2,1)S(1)}, bf16[1,768,2048]{2,1,0:T(8,128)(2,1)}, u32[]{:S(2)}) %copy-start.3) | copy-done | bytes 3145752
  109.2 3.2 %serve.12 = (bf16[96,2048]{1,0:T(8,128)(2,1)S(1)}, bf16[96,2048]{1,0:T(8,128)(2,1)S(1)}) custom-call(f32[96,16]{1,0:T(8,128)S(1)} %bitcast.54, bf16[48,2048]{1,0:T(8,128)(2,1)} %collective-permute-done.36.refs_0_, bf16[48,2048]{1,0:T(8,128)(2,1)} %collective-permute-done.37.refs_1_, bf16[48,2048]{1,0:T(8,128)(2,1)} %collective-permute-done.38.refs_2_, ...), custom_call_target="tpu_custom_call" | custom-call | flops 1811939328 | bytes 9437184 | tf_op jit(solution)/shard_map/serve/pallas_call | solution.py:127
  113.6 3.2 %serve.17 = (bf16[96,2048]{1,0:T(8,128)(2,1)S(1)}, bf16[96,2048]{1,0:T(8,128)(2,1)S(1)}) custom-call(f32[96,16]{1,0:T(8,128)S(1)} %bitcast.55, bf16[48,2048]{1,0:T(8,128)(2,1)} %collective-permute-done.66.refs_0_, bf16[48,2048]{1,0:T(8,128)(2,1)} %collective-permute-done.44.refs_1_, bf16[48,2048]{1,0:T(8,128)(2,1)} %collective-permute-done.67.refs_2_, ...), custom_call_target="tpu_custom_call" | custom-call | flops 1811939328 | bytes 9437184 | tf_op jit(solution)/shard_map/serve/pallas_call | solution.py:127
  117.2 3.1 %serve.13 = (bf16[96,2048]{1,0:T(8,128)(2,1)S(1)}, bf16[96,2048]{1,0:T(8,128)(2,1)S(1)}) custom-call(f32[96,16]{1,0:T(8,128)S(1)} %bitcast.56, bf16[48,2048]{1,0:T(8,128)(2,1)} %collective-permute-done.41.refs_0_, bf16[48,2048]{1,0:T(8,128)(2,1)} %collective-permute-done.45.refs_1_, bf16[48,2048]{1,0:T(8,128)(2,1)} %collective-permute-done.46.refs_2_, ...), custom_call_target="tpu_custom_call" | custom-call | flops 1811939328 | bytes 9437184 | tf_op jit(solution)/shard_map/serve/pallas_call | solution.py:127
  121.4 3.0 %serve.11 = (bf16[96,2048]{1,0:T(8,128)(2,1)S(1)}, bf16[96,2048]{1,0:T(8,128)(2,1)S(1)}) custom-call(f32[96,16]{1,0:T(8,128)S(1)} %bitcast.57, bf16[48,2048]{1,0:T(8,128)(2,1)} %collective-permute-done.31.refs_0_, bf16[48,2048]{1,0:T(8,128)(2,1)} %collective-permute-done.32.refs_1_, bf16[48,2048]{1,0:T(8,128)(2,1)S(1)} %collective-permute-done.33.refs_2_, ...), custom_call_target="tpu_custom_call" | custom-call | flops 1811939328 | bytes 9437184 | tf_op jit(solution)/shard_map/serve/pallas_call | solution.py:127
  124.7 3.2 %serve.16 = (bf16[96,2048]{1,0:T(8,128)(2,1)S(1)}, bf16[96,2048]{1,0:T(8,128)(2,1)S(1)}) custom-call(f32[96,16]{1,0:T(8,128)S(1)} %bitcast.58, bf16[48,2048]{1,0:T(8,128)(2,1)} %collective-permute-done.62.refs_0_, bf16[48,2048]{1,0:T(8,128)(2,1)} %collective-permute-done.43.refs_1_, bf16[48,2048]{1,0:T(8,128)(2,1)S(1)} %collective-permute-done.63.refs_2_, ...), custom_call_target="tpu_custom_call" | custom-call | flops 1811939328 | bytes 9437184 | tf_op jit(solution)/shard_map/serve/pallas_call | solution.py:127
  129.2 1.6 collective-permute-start.73
  130.8 3.1 %serve.10 = (bf16[96,2048]{1,0:T(8,128)(2,1)S(1)}, bf16[96,2048]{1,0:T(8,128)(2,1)S(1)}) custom-call(f32[96,16]{1,0:T(8,128)S(1)} %bitcast.59, bf16[48,2048]{1,0:T(8,128)(2,1)} %collective-permute-done.26.refs_0_, bf16[48,2048]{1,0:T(8,128)(2,1)} %collective-permute-done.27.refs_1_, bf16[48,2048]{1,0:T(8,128)(2,1)} %collective-permute-done.28.refs_2_, ...), custom_call_target="tpu_custom_call" | custom-call | flops 1811939328 | bytes 9437184 | tf_op jit(solution)/shard_map/serve/pallas_call | solution.py:127
  134.0 1.4 collective-permute-start.53
  137.1 3.0 %serve.15 = (bf16[96,2048]{1,0:T(8,128)(2,1)S(1)}, bf16[96,2048]{1,0:T(8,128)(2,1)S(1)}) custom-call(f32[96,16]{1,0:T(8,128)S(1)} %bitcast.60, bf16[48,2048]{1,0:T(8,128)(2,1)} %collective-permute-done.58.refs_0_, bf16[48,2048]{1,0:T(8,128)(2,1)} %collective-permute-done.42.refs_1_, bf16[48,2048]{1,0:T(8,128)(2,1)S(1)} %collective-permute-done.59.refs_2_, ...), custom_call_target="tpu_custom_call" | custom-call | flops 1811939328 | bytes 9437184 | tf_op jit(solution)/shard_map/serve/pallas_call | solution.py:127
  140.6 1.5 collective-permute-start.74
  142.2 1.3 collective-permute-done.70.refs_0_
  143.6 1.5 collective-permute-start.54
  145.1 1.9 %collective-permute-done.50.refs_0_ = bf16[48,2048]{1,0:T(8,128)(2,1)S(1)} collective-permute-done((bf16[48,2048]{1,0:T(8,128)(2,1)S(1)}, bf16[48,2048]{1,0:T(8,128)(2,1)S(1)}, u32[]{:S(2)}, u32[]{:S(2)}) %collective-permute-start.50) | collective-permute-done | bytes 196640 | tf_op jit(solution)/shard_map/ppermute | solution.py:375
  147.7 2.7 %serve.9 = (bf16[48,2048]{1,0:T(8,128)(2,1)S(1)}, bf16[48,2048]{1,0:T(8,128)(2,1)S(1)}) custom-call(f32[96,16]{1,0:T(8,128)S(1)} %bitcast.61, bf16[48,2048]{1,0:T(8,128)(2,1)} %get-tuple-element.43.refs_0_, bf16[48,2048]{1,0:T(8,128)(2,1)} %collective-permute-done.24.refs_1_, bf16[2048,768]{1,0:T(8,128)(2,1)S(1)} %bitcast.34, ...), custom_call_target="tpu_custom_call" | custom-call | flops 905969664 | bytes 9437184 | tf_op jit(solution)/shard_map/serve/pallas_call | solution.py:127
  151.1 1.6 collective-permute-start.75
  152.7 1.7 serve.14
  155.0 1.4 collective-permute-start.55
  156.5 0.9 collective-permute-done.51.refs_0_
  158.8 1.6 collective-permute-start.76
  160.4 2.4 %collective-permute-done.55.refs_3_ = bf16[48,2048]{1,0:T(8,128)(2,1)S(1)} collective-permute-done((bf16[48,2048]{1,0:T(8,128)(2,1)S(1)}, bf16[48,2048]{1,0:T(8,128)(2,1)S(1)}, u32[]{:S(2)}, u32[]{:S(2)}) %collective-permute-start.55) | collective-permute-done | bytes 196640 | tf_op jit(solution)/shard_map/ppermute | solution.py:375
  162.8 2.4 %collective-permute-done.72.refs_6_ = bf16[48,2048]{1,0:T(8,128)(2,1)S(1)} collective-permute-done((bf16[48,2048]{1,0:T(8,128)(2,1)S(1)}, bf16[48,2048]{1,0:T(8,128)(2,1)S(1)}, u32[]{:S(2)}, u32[]{:S(2)}) %collective-permute-start.72) | collective-permute-done | bytes 196640 | tf_op jit(solution)/shard_map/ppermute | solution.py:375
  165.2 2.3 %collective-permute-done.52.refs_2_ = bf16[48,2048]{1,0:T(8,128)(2,1)S(1)} collective-permute-done((bf16[48,2048]{1,0:T(8,128)(2,1)S(1)}, bf16[48,2048]{1,0:T(8,128)(2,1)S(1)}, u32[]{:S(2)}, u32[]{:S(2)}) %collective-permute-start.52) | collective-permute-done | bytes 196640 | tf_op jit(solution)/shard_map/ppermute | solution.py:375
  167.5 1.0 finish.1
  (174 shorter events, 24.0 us)
Async XLA Ops:
  5.4 7.4 %collective-permute-start.2 = (bf16[72,1024]{1,0:T(8,128)(2,1)S(1)}, bf16[72,1024]{1,0:T(8,128)(2,1)S(1)}, u32[]{:S(2)}, u32[]{:S(2)}) collective-permute-start(bf16[72,1024]{1,0:T(8,128)(2,1)S(1)} %get-tuple-element.72.refs_0_), channel_id=1, source_target_pairs={{0,4},{1,5},{4,8},{5,9},{8,12},{9,13},{12,14},{13,15},{14,10},{15,... | collective-permute-start | bytes 442376 | tf_op jit(solution)/shard_map/ppermute | solution.py:328
  8.7 13.9 %collective-permute-start.1 = (bf16[192,8,72]{2,0,1:T(8,128)(2,1)S(1)}, bf16[192,8,72]{2,0,1:T(8,128)(2,1)S(1)}, u32[]{:S(2)}, u32[]{:S(2)}) collective-permute-start(bf16[192,8,72]{2,0,1:T(8,128)(2,1)S(1)} %get-tuple-element.66), channel_id=1, source_target_pairs={{0,16},{16,0},{1,17},{17,1},{2,18},{18,2},{3,19},{19,3},{4,20},{20... | collective-permute-start | bytes 663560 | tf_op jit(solution)/shard_map/ppermute | solution.py:319
  10.7 6.7 %collective-permute-start.13 = (bf16[72,1024]{1,0:T(8,128)(2,1)S(1)}, bf16[72,1024]{1,0:T(8,128)(2,1)S(1)}, u32[]{:S(2)}, u32[]{:S(2)}) collective-permute-start(bf16[72,1024]{1,0:T(8,128)(2,1)S(1)} %get-tuple-element.71.refs_0_), channel_id=1, source_target_pairs={{0,4},{1,5},{4,8},{5,9},{8,12},{9,13},{12,14},{13,15},{14,10},{15,... | collective-permute-start | bytes 442376 | tf_op jit(solution)/shard_map/ppermute | solution.py:328
  12.3 6.7 %collective-permute-start.14 = (bf16[72,1024]{1,0:T(8,128)(2,1)S(1)}, bf16[72,1024]{1,0:T(8,128)(2,1)S(1)}, u32[]{:S(2)}, u32[]{:S(2)}) collective-permute-start(bf16[72,1024]{1,0:T(8,128)(2,1)S(1)} %get-tuple-element.71.refs_0_), channel_id=1, source_target_pairs={{0,2},{1,3},{4,0},{5,1},{8,4},{9,5},{12,8},{13,9},{14,12},{15,13},... | collective-permute-start | bytes 442376 | tf_op jit(solution)/shard_map/ppermute | solution.py:329
  12.8 7.9 %collective-permute-start.4 = (bf16[72,1024]{1,0:T(8,128)(2,1)S(1)}, bf16[72,1024]{1,0:T(8,128)(2,1)S(1)}, u32[]{:S(2)}, u32[]{:S(2)}) collective-permute-start(bf16[72,1024]{1,0:T(8,128)(2,1)S(1)} %collective-permute-done.2.refs_1_), channel_id=1, source_target_pairs={{0,4},{1,5},{4,8},{5,9},{8,12},{9,13},{12,14},{13,15},{14,10},{15,... | collective-permute-start | bytes 442376 | tf_op jit(solution)/shard_map/ppermute | solution.py:328
  14.4 7.8 %collective-permute-start.5 = (bf16[72,1024]{1,0:T(8,128)(2,1)S(1)}, bf16[72,1024]{1,0:T(8,128)(2,1)S(1)}, u32[]{:S(2)}, u32[]{:S(2)}) collective-permute-start(bf16[72,1024]{1,0:T(8,128)(2,1)S(1)} %collective-permute-done.3.refs_2_), channel_id=1, source_target_pairs={{0,2},{1,3},{4,0},{5,1},{8,4},{9,5},{12,8},{13,9},{14,12},{15,13},... | collective-permute-start | bytes 442376 | tf_op jit(solution)/shard_map/ppermute | solution.py:329
  17.5 15.2 %collective-permute-start.15 = (bf16[72,1024]{1,0:T(8,128)(2,1)S(1)}, bf16[72,1024]{1,0:T(8,128)(2,1)S(1)}, u32[]{:S(2)}, u32[]{:S(2)}) collective-permute-start(bf16[72,1024]{1,0:T(8,128)(2,1)S(1)} %collective-permute-done.13.refs_1_), channel_id=1, source_target_pairs={{0,4},{1,5},{4,8},{5,9},{8,12},{9,13},{12,14},{13,15},{14,10},{15,... | collective-permute-start | bytes 442376 | tf_op jit(solution)/shard_map/ppermute | solution.py:328
  19.0 15.2 %collective-permute-start.16 = (bf16[72,1024]{1,0:T(8,128)(2,1)S(1)}, bf16[72,1024]{1,0:T(8,128)(2,1)S(1)}, u32[]{:S(2)}, u32[]{:S(2)}) collective-permute-start(bf16[72,1024]{1,0:T(8,128)(2,1)S(1)} %collective-permute-done.14.refs_2_), channel_id=1, source_target_pairs={{0,2},{1,3},{4,0},{5,1},{8,4},{9,5},{12,8},{13,9},{14,12},{15,13},... | collective-permute-start | bytes 442376 | tf_op jit(solution)/shard_map/ppermute | solution.py:329
  25.9 6.1 %collective-permute-start.8 = (bf16[40,1024]{1,0:T(8,128)(2,1)S(1)}, bf16[40,1024]{1,0:T(8,128)(2,1)S(1)}, u32[]{:S(2)}, u32[]{:S(2)}) collective-permute-start(bf16[40,1024]{1,0:T(8,128)(2,1)S(1)} %slice.73), channel_id=1, source_target_pairs={{0,4},{1,5},{4,8},{5,9},{8,12},{9,13},{12,14},{13,15},{14,10},{15,... | collective-permute-start | bytes 245768 | tf_op jit(solution)/shard_map/ppermute | solution.py:332
  32.6 13.5 %collective-permute-start.11 = (f32[96,1024]{1,0:T(8,128)S(1)}, f32[96,1024]{1,0:T(8,128)S(1)}, u32[]{:S(2)}, u32[]{:S(2)}) collective-permute-start(f32[96,1024]{1,0:T(8,128)S(1)} %get-tuple-element.37), channel_id=1, source_target_pairs={{0,1},{1,0},{2,3},{3,2},{4,5},{5,4},{6,7},{7,6},{8,9},{9,8},{10,11... | collective-permute-start | bytes 1179656 | tf_op jit(solution)/shard_map/ppermute | solution.py:336
  32.7 6.2 %collective-permute-start.17 = (bf16[72,1024]{1,0:T(8,128)(2,1)S(1)}, bf16[72,1024]{1,0:T(8,128)(2,1)S(1)}, u32[]{:S(2)}, u32[]{:S(2)}) collective-permute-start(bf16[72,1024]{1,0:T(8,128)(2,1)S(1)} %collective-permute-done.15.refs_3_), channel_id=1, source_target_pairs={{0,4},{1,5},{4,8},{5,9},{8,12},{9,13},{12,14},{13,15},{14,10},{15,... | collective-permute-start | bytes 442376 | tf_op jit(solution)/shard_map/ppermute | solution.py:328
  34.3 6.2 %collective-permute-start.18 = (bf16[72,1024]{1,0:T(8,128)(2,1)S(1)}, bf16[72,1024]{1,0:T(8,128)(2,1)S(1)}, u32[]{:S(2)}, u32[]{:S(2)}) collective-permute-start(bf16[72,1024]{1,0:T(8,128)(2,1)S(1)} %collective-permute-done.16.refs_4_), channel_id=1, source_target_pairs={{0,2},{1,3},{4,0},{5,1},{8,4},{9,5},{12,8},{13,9},{14,12},{15,13},... | collective-permute-start | bytes 442376 | tf_op jit(solution)/shard_map/ppermute | solution.py:329
  46.1 7.8 %collective-permute-start.12 = (bf16[96,1024]{1,0:T(8,128)(2,1)S(1)}, bf16[96,1024]{1,0:T(8,128)(2,1)S(1)}, u32[]{:S(2)}, u32[]{:S(2)}) collective-permute-start(bf16[96,1024]{1,0:T(8,128)(2,1)S(1)} %add_convert_fusion.1), channel_id=1, source_target_pairs={{0,16},{16,0},{1,17},{17,1},{2,18},{18,2},{3,19},{19,3},{4,20},{20... | collective-permute-start | bytes 589832 | tf_op jit(solution)/shard_map/ppermute | solution.py:337
  47.2 10.4 %collective-permute-start.23 = (bf16[96,1024]{1,0:T(8,128)(2,1)S(1)}, bf16[96,1024]{1,0:T(8,128)(2,1)S(1)}, u32[]{:S(2)}, u32[]{:S(2)}) collective-permute-start(bf16[96,1024]{1,0:T(8,128)(2,1)S(1)} %add_convert_fusion), channel_id=1, source_target_pairs={{0,16},{16,0},{1,17},{17,1},{2,18},{18,2},{3,19},{19,3},{4,20},{20... | collective-permute-start | bytes 589832 | tf_op jit(solution)/shard_map/ppermute | solution.py:337
  59.4 7.6 %collective-permute-start.26 = (bf16[48,2048]{1,0:T(8,128)(2,1)}, bf16[48,2048]{1,0:T(8,128)(2,1)}, u32[]{:S(2)}, u32[]{:S(2)}) collective-permute-start(bf16[48,2048]{1,0:T(8,128)(2,1)} %get-tuple-element.43.refs_0_), channel_id=1, source_target_pairs={{0,4},{1,5},{4,8},{5,9},{8,12},{9,13},{12,14},{13,15},{14,10},{15,... | collective-permute-start | bytes 589832 | tf_op jit(solution)/shard_map/ppermute | solution.py:360
  61.0 8.1 %collective-permute-start.27 = (bf16[48,2048]{1,0:T(8,128)(2,1)}, bf16[48,2048]{1,0:T(8,128)(2,1)}, u32[]{:S(2)}, u32[]{:S(2)}) collective-permute-start(bf16[48,2048]{1,0:T(8,128)(2,1)} %get-tuple-element.43.refs_0_), channel_id=1, source_target_pairs={{0,2},{1,3},{4,0},{5,1},{8,4},{9,5},{12,8},{13,9},{14,12},{15,13},... | collective-permute-start | bytes 589832 | tf_op jit(solution)/shard_map/ppermute | solution.py:361
  61.4 11.9 %collective-permute-start.42 = (bf16[48,2048]{1,0:T(8,128)(2,1)S(1)}, bf16[48,2048]{1,0:T(8,128)(2,1)}, u32[]{:S(2)}, u32[]{:S(2)}) collective-permute-start(bf16[48,2048]{1,0:T(8,128)(2,1)S(1)} %get-tuple-element.52.refs_0_), channel_id=1, source_target_pairs={{0,2},{1,3},{4,0},{5,1},{8,4},{9,5},{12,8},{13,9},{14,12},{15,13},... | collective-permute-start | bytes 589832 | tf_op jit(solution)/shard_map/ppermute | solution.py:361
  61.9 22.0 %collective-permute-start.24 = (bf16[48,2048]{1,0:T(8,128)(2,1)}, bf16[48,2048]{1,0:T(8,128)(2,1)}, u32[]{:S(2)}, u32[]{:S(2)}) collective-permute-start(bf16[48,2048]{1,0:T(8,128)(2,1)} %get-tuple-element.43.refs_0_), channel_id=1, source_target_pairs={{0,1},{1,0},{2,3},{3,2},{4,5},{5,4},{6,7},{7,6},{8,9},{9,8},{10,11... | collective-permute-start | bytes 589832 | tf_op jit(solution)/shard_map/ppermute | solution.py:356
  62.0 22.0 %collective-permute-start.58 = (bf16[48,2048]{1,0:T(8,128)(2,1)S(1)}, bf16[48,2048]{1,0:T(8,128)(2,1)}, u32[]{:S(2)}, u32[]{:S(2)}) collective-permute-start(bf16[48,2048]{1,0:T(8,128)(2,1)S(1)} %get-tuple-element.52.refs_0_), channel_id=1, source_target_pairs={{0,4},{1,5},{4,8},{5,9},{8,12},{9,13},{12,14},{13,15},{14,10},{15,... | collective-permute-start | bytes 589832 | tf_op jit(solution)/shard_map/ppermute | solution.py:360
  67.0 17.5 %collective-permute-start.31 = (bf16[48,2048]{1,0:T(8,128)(2,1)}, bf16[48,2048]{1,0:T(8,128)(2,1)}, u32[]{:S(2)}, u32[]{:S(2)}) collective-permute-start(bf16[48,2048]{1,0:T(8,128)(2,1)} %collective-permute-done.26.refs_0_), channel_id=1, source_target_pairs={{0,4},{1,5},{4,8},{5,9},{8,12},{9,13},{12,14},{13,15},{14,10},{15,... | collective-permute-start | bytes 589832 | tf_op jit(solution)/shard_map/ppermute | solution.py:360
  69.1 16.1 %collective-permute-start.32 = (bf16[48,2048]{1,0:T(8,128)(2,1)}, bf16[48,2048]{1,0:T(8,128)(2,1)}, u32[]{:S(2)}, u32[]{:S(2)}) collective-permute-start(bf16[48,2048]{1,0:T(8,128)(2,1)} %collective-permute-done.27.refs_1_), channel_id=1, source_target_pairs={{0,2},{1,3},{4,0},{5,1},{8,4},{9,5},{12,8},{13,9},{14,12},{15,13},... | collective-permute-start | bytes 589832 | tf_op jit(solution)/shard_map/ppermute | solution.py:361
  73.3 13.3 %collective-permute-start.43 = (bf16[48,2048]{1,0:T(8,128)(2,1)}, bf16[48,2048]{1,0:T(8,128)(2,1)}, u32[]{:S(2)}, u32[]{:S(2)}) collective-permute-start(bf16[48,2048]{1,0:T(8,128)(2,1)} %collective-permute-done.42.refs_1_), channel_id=1, source_target_pairs={{0,2},{1,3},{4,0},{5,1},{8,4},{9,5},{12,8},{13,9},{14,12},{15,13},... | collective-permute-start | bytes 589832 | tf_op jit(solution)/shard_map/ppermute | solution.py:361
  83.9 12.4 %collective-permute-start.56 = (bf16[48,2048]{1,0:T(8,128)(2,1)S(1)}, bf16[48,2048]{1,0:T(8,128)(2,1)S(1)}, u32[]{:S(2)}, u32[]{:S(2)}) collective-permute-start(bf16[48,2048]{1,0:T(8,128)(2,1)S(1)} %get-tuple-element.52.refs_0_), channel_id=1, source_target_pairs={{0,1},{1,0},{2,3},{3,2},{4,5},{5,4},{6,7},{7,6},{8,9},{9,8},{10,11... | collective-permute-start | bytes 589832 | tf_op jit(solution)/shard_map/ppermute | solution.py:356
  84.0 8.1 %collective-permute-start.62 = (bf16[48,2048]{1,0:T(8,128)(2,1)}, bf16[48,2048]{1,0:T(8,128)(2,1)}, u32[]{:S(2)}, u32[]{:S(2)}) collective-permute-start(bf16[48,2048]{1,0:T(8,128)(2,1)} %collective-permute-done.58.refs_0_), channel_id=1, source_target_pairs={{0,4},{1,5},{4,8},{5,9},{8,12},{9,13},{12,14},{13,15},{14,10},{15,... | collective-permute-start | bytes 589832 | tf_op jit(solution)/shard_map/ppermute | solution.py:360
  84.6 11.8 %collective-permute-start.36 = (bf16[48,2048]{1,0:T(8,128)(2,1)}, bf16[48,2048]{1,0:T(8,128)(2,1)}, u32[]{:S(2)}, u32[]{:S(2)}) collective-permute-start(bf16[48,2048]{1,0:T(8,128)(2,1)} %collective-permute-done.31.refs_0_), channel_id=1, source_target_pairs={{0,4},{1,5},{4,8},{5,9},{8,12},{9,13},{12,14},{13,15},{14,10},{15,... | collective-permute-start | bytes 589832 | tf_op jit(solution)/shard_map/ppermute | solution.py:360
  85.2 12.4 %collective-permute-start.37 = (bf16[48,2048]{1,0:T(8,128)(2,1)}, bf16[48,2048]{1,0:T(8,128)(2,1)}, u32[]{:S(2)}, u32[]{:S(2)}) collective-permute-start(bf16[48,2048]{1,0:T(8,128)(2,1)} %collective-permute-done.32.refs_1_), channel_id=1, source_target_pairs={{0,2},{1,3},{4,0},{5,1},{8,4},{9,5},{12,8},{13,9},{14,12},{15,13},... | collective-permute-start | bytes 589832 | tf_op jit(solution)/shard_map/ppermute | solution.py:361
  86.6 11.2 %collective-permute-start.44 = (bf16[48,2048]{1,0:T(8,128)(2,1)}, bf16[48,2048]{1,0:T(8,128)(2,1)}, u32[]{:S(2)}, u32[]{:S(2)}) collective-permute-start(bf16[48,2048]{1,0:T(8,128)(2,1)} %collective-permute-done.43.refs_1_), channel_id=1, source_target_pairs={{0,2},{1,3},{4,0},{5,1},{8,4},{9,5},{12,8},{13,9},{14,12},{15,13},... | collective-permute-start | bytes 589832 | tf_op jit(solution)/shard_map/ppermute | solution.py:361
  92.2 7.9 %collective-permute-start.66 = (bf16[48,2048]{1,0:T(8,128)(2,1)}, bf16[48,2048]{1,0:T(8,128)(2,1)}, u32[]{:S(2)}, u32[]{:S(2)}) collective-permute-start(bf16[48,2048]{1,0:T(8,128)(2,1)} %collective-permute-done.62.refs_0_), channel_id=1, source_target_pairs={{0,4},{1,5},{4,8},{5,9},{8,12},{9,13},{12,14},{13,15},{14,10},{15,... | collective-permute-start | bytes 589832 | tf_op jit(solution)/shard_map/ppermute | solution.py:360
  97.1 7.6 %collective-permute-start.41 = (bf16[48,2048]{1,0:T(8,128)(2,1)}, bf16[48,2048]{1,0:T(8,128)(2,1)}, u32[]{:S(2)}, u32[]{:S(2)}) collective-permute-start(bf16[48,2048]{1,0:T(8,128)(2,1)} %collective-permute-done.36.refs_0_), channel_id=1, source_target_pairs={{0,4},{1,5},{4,8},{5,9},{8,12},{9,13},{12,14},{13,15},{14,10},{15,... | collective-permute-start | bytes 589832 | tf_op jit(solution)/shard_map/ppermute | solution.py:365
  97.8 7.4 %collective-permute-start.45 = (bf16[48,2048]{1,0:T(8,128)(2,1)}, bf16[48,2048]{1,0:T(8,128)(2,1)}, u32[]{:S(2)}, u32[]{:S(2)}) collective-permute-start(bf16[48,2048]{1,0:T(8,128)(2,1)} %collective-permute-done.44.refs_1_), channel_id=1, source_target_pairs={{0,2},{1,3},{4,0},{5,1},{8,4},{9,5},{12,8},{13,9},{14,12},{15,13},... | collective-permute-start | bytes 589832 | tf_op jit(solution)/shard_map/ppermute | solution.py:366
  100.1 12.4 %collective-permute-start.28 = (bf16[48,2048]{1,0:T(8,128)(2,1)}, bf16[48,2048]{1,0:T(8,128)(2,1)}, u32[]{:S(2)}, u32[]{:S(2)}) collective-permute-start(bf16[48,2048]{1,0:T(8,128)(2,1)} %collective-permute-done.26.refs_0_), channel_id=1, source_target_pairs={{0,1},{1,0},{2,3},{3,2},{4,5},{5,4},{6,7},{7,6},{8,9},{9,8},{10,11... | collective-permute-start | bytes 589832 | tf_op jit(solution)/shard_map/ppermute | solution.py:362
  100.1 13.0 %collective-permute-start.68 = (bf16[48,2048]{1,0:T(8,128)(2,1)}, bf16[48,2048]{1,0:T(8,128)(2,1)}, u32[]{:S(2)}, u32[]{:S(2)}) collective-permute-start(bf16[48,2048]{1,0:T(8,128)(2,1)} %collective-permute-done.44.refs_1_), channel_id=1, source_target_pairs={{0,1},{1,0},{2,3},{3,2},{4,5},{5,4},{6,7},{7,6},{8,9},{9,8},{10,11... | collective-permute-start | bytes 589832 | tf_op jit(solution)/shard_map/ppermute | solution.py:362
  100.6 12.2 %collective-permute-start.67 = (bf16[48,2048]{1,0:T(8,128)(2,1)}, bf16[48,2048]{1,0:T(8,128)(2,1)}, u32[]{:S(2)}, u32[]{:S(2)}) collective-permute-start(bf16[48,2048]{1,0:T(8,128)(2,1)} %collective-permute-done.66.refs_0_), channel_id=1, source_target_pairs={{0,1},{1,0},{2,3},{3,2},{4,5},{5,4},{6,7},{7,6},{8,9},{9,8},{10,11... | collective-permute-start | bytes 589832 | tf_op jit(solution)/shard_map/ppermute | solution.py:362
  104.7 8.7 %collective-permute-start.46 = (bf16[48,2048]{1,0:T(8,128)(2,1)}, bf16[48,2048]{1,0:T(8,128)(2,1)}, u32[]{:S(2)}, u32[]{:S(2)}) collective-permute-start(bf16[48,2048]{1,0:T(8,128)(2,1)} %collective-permute-done.41.refs_0_), channel_id=1, source_target_pairs={{0,1},{1,0},{2,3},{3,2},{4,5},{5,4},{6,7},{7,6},{8,9},{9,8},{10,11... | collective-permute-start | bytes 589832 | tf_op jit(solution)/shard_map/ppermute | solution.py:368
  105.2 11.6 %collective-permute-start.47 = (bf16[48,2048]{1,0:T(8,128)(2,1)}, bf16[48,2048]{1,0:T(8,128)(2,1)S(1)}, u32[]{:S(2)}, u32[]{:S(2)}) collective-permute-start(bf16[48,2048]{1,0:T(8,128)(2,1)} %collective-permute-done.45.refs_1_), channel_id=1, source_target_pairs={{0,1},{1,0},{2,3},{3,2},{4,5},{5,4},{6,7},{7,6},{8,9},{9,8},{10,11... | collective-permute-start | bytes 589832 | tf_op jit(solution)/shard_map/ppermute | solution.py:368
  112.5 7.9 %collective-permute-start.29 = (bf16[48,2048]{1,0:T(8,128)(2,1)}, bf16[48,2048]{1,0:T(8,128)(2,1)S(1)}, u32[]{:S(2)}, u32[]{:S(2)}) collective-permute-start(bf16[48,2048]{1,0:T(8,128)(2,1)} %collective-permute-done.27.refs_1_), channel_id=1, source_target_pairs={{0,1},{1,0},{2,3},{3,2},{4,5},{5,4},{6,7},{7,6},{8,9},{9,8},{10,11... | collective-permute-start | bytes 589832 | tf_op jit(solution)/shard_map/ppermute | solution.py:362
  112.8 7.8 %collective-permute-start.33 = (bf16[48,2048]{1,0:T(8,128)(2,1)}, bf16[48,2048]{1,0:T(8,128)(2,1)S(1)}, u32[]{:S(2)}, u32[]{:S(2)}) collective-permute-start(bf16[48,2048]{1,0:T(8,128)(2,1)} %collective-permute-done.31.refs_0_), channel_id=1, source_target_pairs={{0,1},{1,0},{2,3},{3,2},{4,5},{5,4},{6,7},{7,6},{8,9},{9,8},{10,11... | collective-permute-start | bytes 589832 | tf_op jit(solution)/shard_map/ppermute | solution.py:362
  113.0 7.9 %collective-permute-start.34 = (bf16[48,2048]{1,0:T(8,128)(2,1)}, bf16[48,2048]{1,0:T(8,128)(2,1)S(1)}, u32[]{:S(2)}, u32[]{:S(2)}) collective-permute-start(bf16[48,2048]{1,0:T(8,128)(2,1)} %collective-permute-done.32.refs_1_), channel_id=1, source_target_pairs={{0,1},{1,0},{2,3},{3,2},{4,5},{5,4},{6,7},{7,6},{8,9},{9,8},{10,11... | collective-permute-start | bytes 589832 | tf_op jit(solution)/shard_map/ppermute | solution.py:362
  113.3 7.8 %collective-permute-start.63 = (bf16[48,2048]{1,0:T(8,128)(2,1)}, bf16[48,2048]{1,0:T(8,128)(2,1)S(1)}, u32[]{:S(2)}, u32[]{:S(2)}) collective-permute-start(bf16[48,2048]{1,0:T(8,128)(2,1)} %collective-permute-done.62.refs_0_), channel_id=1, source_target_pairs={{0,1},{1,0},{2,3},{3,2},{4,5},{5,4},{6,7},{7,6},{8,9},{9,8},{10,11... | collective-permute-start | bytes 589832 | tf_op jit(solution)/shard_map/ppermute | solution.py:362
  116.8 7.7 %collective-permute-start.64 = (bf16[48,2048]{1,0:T(8,128)(2,1)}, bf16[48,2048]{1,0:T(8,128)(2,1)S(1)}, u32[]{:S(2)}, u32[]{:S(2)}) collective-permute-start(bf16[48,2048]{1,0:T(8,128)(2,1)} %collective-permute-done.43.refs_1_), channel_id=1, source_target_pairs={{0,1},{1,0},{2,3},{3,2},{4,5},{5,4},{6,7},{7,6},{8,9},{9,8},{10,11... | collective-permute-start | bytes 589832 | tf_op jit(solution)/shard_map/ppermute | solution.py:362
  120.3 7.6 %collective-permute-start.59 = (bf16[48,2048]{1,0:T(8,128)(2,1)}, bf16[48,2048]{1,0:T(8,128)(2,1)S(1)}, u32[]{:S(2)}, u32[]{:S(2)}) collective-permute-start(bf16[48,2048]{1,0:T(8,128)(2,1)} %collective-permute-done.58.refs_0_), channel_id=1, source_target_pairs={{0,1},{1,0},{2,3},{3,2},{4,5},{5,4},{6,7},{7,6},{8,9},{9,8},{10,11... | collective-permute-start | bytes 589832 | tf_op jit(solution)/shard_map/ppermute | solution.py:362
  120.6 8.0 %collective-permute-start.40 = (bf16[96,2048]{1,0:T(8,128)(2,1)S(1)}, bf16[96,2048]{1,0:T(8,128)(2,1)S(1)}, u32[]{:S(2)}, u32[]{:S(2)}) collective-permute-start(bf16[96,2048]{1,0:T(8,128)(2,1)S(1)} %get-tuple-element.51), channel_id=1, source_target_pairs={{0,1},{1,0},{2,3},{3,2},{4,5},{5,4},{6,7},{7,6},{8,9},{9,8},{10,11... | collective-permute-start | bytes 1179656 | tf_op jit(solution)/shard_map/ppermute | solution.py:370
  120.9 8.3 %collective-permute-start.69 = (bf16[96,2048]{1,0:T(8,128)(2,1)S(1)}, bf16[96,2048]{1,0:T(8,128)(2,1)S(1)}, u32[]{:S(2)}, u32[]{:S(2)}) collective-permute-start(bf16[96,2048]{1,0:T(8,128)(2,1)S(1)} %get-tuple-element.62), channel_id=1, source_target_pairs={{0,1},{1,0},{2,3},{3,2},{4,5},{5,4},{6,7},{7,6},{8,9},{9,8},{10,11... | collective-permute-start | bytes 1179656 | tf_op jit(solution)/shard_map/ppermute | solution.py:370
  121.1 7.2 %collective-permute-start.48 = (bf16[96,2048]{1,0:T(8,128)(2,1)S(1)}, bf16[96,2048]{1,0:T(8,128)(2,1)S(1)}, u32[]{:S(2)}, u32[]{:S(2)}) collective-permute-start(bf16[96,2048]{1,0:T(8,128)(2,1)S(1)} %get-tuple-element.54), channel_id=1, source_target_pairs={{0,1},{1,0},{2,3},{3,2},{4,5},{5,4},{6,7},{7,6},{8,9},{9,8},{10,11... | collective-permute-start | bytes 1179656 | tf_op jit(solution)/shard_map/ppermute | solution.py:369
  124.5 11.0 %collective-permute-start.35 = (bf16[96,2048]{1,0:T(8,128)(2,1)S(1)}, bf16[96,2048]{1,0:T(8,128)(2,1)S(1)}, u32[]{:S(2)}, u32[]{:S(2)}) collective-permute-start(bf16[96,2048]{1,0:T(8,128)(2,1)S(1)} %get-tuple-element.49), channel_id=1, source_target_pairs={{0,1},{1,0},{2,3},{3,2},{4,5},{5,4},{6,7},{7,6},{8,9},{9,8},{10,11... | collective-permute-start | bytes 1179656 | tf_op jit(solution)/shard_map/ppermute | solution.py:370
  128.0 8.5 %collective-permute-start.65 = (bf16[96,2048]{1,0:T(8,128)(2,1)S(1)}, bf16[96,2048]{1,0:T(8,128)(2,1)S(1)}, u32[]{:S(2)}, u32[]{:S(2)}) collective-permute-start(bf16[96,2048]{1,0:T(8,128)(2,1)S(1)} %get-tuple-element.60), channel_id=1, source_target_pairs={{0,1},{1,0},{2,3},{3,2},{4,5},{5,4},{6,7},{7,6},{8,9},{9,8},{10,11... | collective-permute-start | bytes 1179656 | tf_op jit(solution)/shard_map/ppermute | solution.py:370
  128.6 7.2 %collective-permute-start.49 = (bf16[48,2048]{1,0:T(8,128)(2,1)S(1)}, bf16[48,2048]{1,0:T(8,128)(2,1)S(1)}, u32[]{:S(2)}, u32[]{:S(2)}) collective-permute-start(bf16[48,2048]{1,0:T(8,128)(2,1)S(1)} %add.24), channel_id=1, source_target_pairs={{0,4},{1,5},{4,8},{5,9},{8,12},{9,13},{12,14},{13,15},{14,10},{15,... | collective-permute-start | bytes 589832 | tf_op jit(solution)/shard_map/ppermute | solution.py:380
  129.2 10.9 %collective-permute-start.73 = (bf16[48,2048]{1,0:T(8,128)(2,1)S(1)}, bf16[48,2048]{1,0:T(8,128)(2,1)S(1)}, u32[]{:S(2)}, u32[]{:S(2)}) collective-permute-start(bf16[48,2048]{1,0:T(8,128)(2,1)S(1)} %add.34), channel_id=1, source_target_pairs={{0,2},{1,3},{4,0},{5,1},{8,4},{9,5},{12,8},{13,9},{14,12},{15,13},... | collective-permute-start | bytes 589832 | tf_op jit(solution)/shard_map/ppermute | solution.py:381
  134.0 6.6 %collective-permute-start.53 = (bf16[48,2048]{1,0:T(8,128)(2,1)S(1)}, bf16[48,2048]{1,0:T(8,128)(2,1)S(1)}, u32[]{:S(2)}, u32[]{:S(2)}) collective-permute-start(bf16[48,2048]{1,0:T(8,128)(2,1)S(1)} %add.28), channel_id=1, source_target_pairs={{0,2},{1,3},{4,0},{5,1},{8,4},{9,5},{12,8},{13,9},{14,12},{15,13},... | collective-permute-start | bytes 589832 | tf_op jit(solution)/shard_map/ppermute | solution.py:375
  135.5 15.6 %collective-permute-start.30 = (bf16[96,2048]{1,0:T(8,128)(2,1)S(1)}, bf16[96,2048]{1,0:T(8,128)(2,1)S(1)}, u32[]{:S(2)}, u32[]{:S(2)}) collective-permute-start(bf16[96,2048]{1,0:T(8,128)(2,1)S(1)} %get-tuple-element.47), channel_id=1, source_target_pairs={{0,1},{1,0},{2,3},{3,2},{4,5},{5,4},{6,7},{7,6},{8,9},{9,8},{10,11... | collective-permute-start | bytes 1179656 | tf_op jit(solution)/shard_map/ppermute | solution.py:370
  135.8 7.8 %collective-permute-start.70 = (bf16[48,2048]{1,0:T(8,128)(2,1)S(1)}, bf16[48,2048]{1,0:T(8,128)(2,1)S(1)}, u32[]{:S(2)}, u32[]{:S(2)}) collective-permute-start(bf16[48,2048]{1,0:T(8,128)(2,1)S(1)} %add.31), channel_id=1, source_target_pairs={{0,4},{1,5},{4,8},{5,9},{8,12},{9,13},{12,14},{13,15},{14,10},{15,... | collective-permute-start | bytes 589832 | tf_op jit(solution)/shard_map/ppermute | solution.py:375
  136.5 10.5 %collective-permute-start.50 = (bf16[48,2048]{1,0:T(8,128)(2,1)S(1)}, bf16[48,2048]{1,0:T(8,128)(2,1)S(1)}, u32[]{:S(2)}, u32[]{:S(2)}) collective-permute-start(bf16[48,2048]{1,0:T(8,128)(2,1)S(1)} %add.25), channel_id=1, source_target_pairs={{0,4},{1,5},{4,8},{5,9},{8,12},{9,13},{12,14},{13,15},{14,10},{15,... | collective-permute-start | bytes 589832 | tf_op jit(solution)/shard_map/ppermute | solution.py:375
  140.1 14.3 %collective-permute-start.61 = (bf16[96,2048]{1,0:T(8,128)(2,1)S(1)}, bf16[96,2048]{1,0:T(8,128)(2,1)S(1)}, u32[]{:S(2)}, u32[]{:S(2)}) collective-permute-start(bf16[96,2048]{1,0:T(8,128)(2,1)S(1)} %get-tuple-element.58), channel_id=1, source_target_pairs={{0,1},{1,0},{2,3},{3,2},{4,5},{5,4},{6,7},{7,6},{8,9},{9,8},{10,11... | collective-permute-start | bytes 1179656 | tf_op jit(solution)/shard_map/ppermute | solution.py:370
  140.6 9.8 %collective-permute-start.74 = (bf16[48,2048]{1,0:T(8,128)(2,1)S(1)}, bf16[48,2048]{1,0:T(8,128)(2,1)S(1)}, u32[]{:S(2)}, u32[]{:S(2)}) collective-permute-start(bf16[48,2048]{1,0:T(8,128)(2,1)S(1)} %add.35), channel_id=1, source_target_pairs={{0,2},{1,3},{4,0},{5,1},{8,4},{9,5},{12,8},{13,9},{14,12},{15,13},... | collective-permute-start | bytes 589832 | tf_op jit(solution)/shard_map/ppermute | solution.py:375
  143.6 9.1 %collective-permute-start.54 = (bf16[48,2048]{1,0:T(8,128)(2,1)S(1)}, bf16[48,2048]{1,0:T(8,128)(2,1)S(1)}, u32[]{:S(2)}, u32[]{:S(2)}) collective-permute-start(bf16[48,2048]{1,0:T(8,128)(2,1)S(1)} %add.29), channel_id=1, source_target_pairs={{0,2},{1,3},{4,0},{5,1},{8,4},{9,5},{12,8},{13,9},{14,12},{15,13},... | collective-permute-start | bytes 589832 | tf_op jit(solution)/shard_map/ppermute | solution.py:375
  147.0 8.0 %collective-permute-start.71 = (bf16[48,2048]{1,0:T(8,128)(2,1)S(1)}, bf16[48,2048]{1,0:T(8,128)(2,1)S(1)}, u32[]{:S(2)}, u32[]{:S(2)}) collective-permute-start(bf16[48,2048]{1,0:T(8,128)(2,1)S(1)} %add.32), channel_id=1, source_target_pairs={{0,4},{1,5},{4,8},{5,9},{8,12},{9,13},{12,14},{13,15},{14,10},{15,... | collective-permute-start | bytes 589832 | tf_op jit(solution)/shard_map/ppermute | solution.py:375
  150.4 7.0 %collective-permute-start.51 = (bf16[48,2048]{1,0:T(8,128)(2,1)S(1)}, bf16[48,2048]{1,0:T(8,128)(2,1)S(1)}, u32[]{:S(2)}, u32[]{:S(2)}) collective-permute-start(bf16[48,2048]{1,0:T(8,128)(2,1)S(1)} %add.26), channel_id=1, source_target_pairs={{0,4},{1,5},{4,8},{5,9},{8,12},{9,13},{12,14},{13,15},{14,10},{15,... | collective-permute-start | bytes 589832 | tf_op jit(solution)/shard_map/ppermute | solution.py:375
  151.1 7.0 %collective-permute-start.75 = (bf16[48,2048]{1,0:T(8,128)(2,1)S(1)}, bf16[48,2048]{1,0:T(8,128)(2,1)S(1)}, u32[]{:S(2)}, u32[]{:S(2)}) collective-permute-start(bf16[48,2048]{1,0:T(8,128)(2,1)S(1)} %add.36), channel_id=1, source_target_pairs={{0,2},{1,3},{4,0},{5,1},{8,4},{9,5},{12,8},{13,9},{14,12},{15,13},... | collective-permute-start | bytes 589832 | tf_op jit(solution)/shard_map/ppermute | solution.py:375
  152.7 6.1 %collective-permute-start.25 = (bf16[48,2048]{1,0:T(8,128)(2,1)S(1)}, bf16[48,2048]{1,0:T(8,128)(2,1)S(1)}, u32[]{:S(2)}, u32[]{:S(2)}) collective-permute-start(bf16[48,2048]{1,0:T(8,128)(2,1)S(1)} %get-tuple-element.45), channel_id=1, source_target_pairs={{0,1},{1,0},{2,3},{3,2},{4,5},{5,4},{6,7},{7,6},{8,9},{9,8},{10,11... | collective-permute-start | bytes 589832 | tf_op jit(solution)/shard_map/ppermute | solution.py:370
  154.4 5.9 %collective-permute-start.57 = (bf16[48,2048]{1,0:T(8,128)(2,1)S(1)}, bf16[48,2048]{1,0:T(8,128)(2,1)S(1)}, u32[]{:S(2)}, u32[]{:S(2)}) collective-permute-start(bf16[48,2048]{1,0:T(8,128)(2,1)S(1)} %get-tuple-element.56), channel_id=1, source_target_pairs={{0,1},{1,0},{2,3},{3,2},{4,5},{5,4},{6,7},{7,6},{8,9},{9,8},{10,11... | collective-permute-start | bytes 589832 | tf_op jit(solution)/shard_map/ppermute | solution.py:370
  155.0 7.8 %collective-permute-start.55 = (bf16[48,2048]{1,0:T(8,128)(2,1)S(1)}, bf16[48,2048]{1,0:T(8,128)(2,1)S(1)}, u32[]{:S(2)}, u32[]{:S(2)}) collective-permute-start(bf16[48,2048]{1,0:T(8,128)(2,1)S(1)} %add.30), channel_id=1, source_target_pairs={{0,2},{1,3},{4,0},{5,1},{8,4},{9,5},{12,8},{13,9},{14,12},{15,13},... | collective-permute-start | bytes 589832 | tf_op jit(solution)/shard_map/ppermute | solution.py:375
  157.4 7.8 %collective-permute-start.72 = (bf16[48,2048]{1,0:T(8,128)(2,1)S(1)}, bf16[48,2048]{1,0:T(8,128)(2,1)S(1)}, u32[]{:S(2)}, u32[]{:S(2)}) collective-permute-start(bf16[48,2048]{1,0:T(8,128)(2,1)S(1)} %add.33), channel_id=1, source_target_pairs={{0,4},{1,5},{4,8},{5,9},{8,12},{9,13},{12,14},{13,15},{14,10},{15,... | collective-permute-start | bytes 589832 | tf_op jit(solution)/shard_map/ppermute | solution.py:375
  158.1 9.4 %collective-permute-start.52 = (bf16[48,2048]{1,0:T(8,128)(2,1)S(1)}, bf16[48,2048]{1,0:T(8,128)(2,1)S(1)}, u32[]{:S(2)}, u32[]{:S(2)}) collective-permute-start(bf16[48,2048]{1,0:T(8,128)(2,1)S(1)} %add.27), channel_id=1, source_target_pairs={{0,4},{1,5},{4,8},{5,9},{8,12},{9,13},{12,14},{13,15},{14,10},{15,... | collective-permute-start | bytes 589832 | tf_op jit(solution)/shard_map/ppermute | solution.py:375
  158.8 8.8 %collective-permute-start.76 = (bf16[48,2048]{1,0:T(8,128)(2,1)S(1)}, bf16[48,2048]{1,0:T(8,128)(2,1)S(1)}, u32[]{:S(2)}, u32[]{:S(2)}) collective-permute-start(bf16[48,2048]{1,0:T(8,128)(2,1)S(1)} %add.37), channel_id=1, source_target_pairs={{0,2},{1,3},{4,0},{5,1},{8,4},{9,5},{12,8},{13,9},{14,12},{15,13},... | collective-permute-start | bytes 589832 | tf_op jit(solution)/shard_map/ppermute | solution.py:375
  (26 other events, 204.4 us)

commit v4 on v3

--- a/solution.py
+++ b/solution.py
@@ -92,17 +92,20 @@
     return max(t for t in range(LANES, most + 1, LANES) if extent % t == 0)
 
 
-def serve_body(columns, share_ref, *refs):
-    blocks = len(columns)
+def serve_body(blocks, expert_ref, *refs):
     ins = refs[:blocks]
     gate_ref, up_ref, down_ref, own_ref, other_ref, x_ref, h_ref = refs[blocks:]
     width, wide = gate_ref.shape
     start = 0
     share = []
-    for ref, (column, low, high) in zip(ins, columns):
-        x_ref[start : start + high - low, :] = ref[...]
-        share.append(share_ref[low:high, column : column + 1])
-        start += high - low
+    for ref in ins:
+        size = ref.shape[0]
+        x_ref[start : start + size, :] = ref[:, :width]
+        tags = ref[:, width:].astype(jnp.float32)
+        mine = lax.broadcasted_iota(jnp.int32, tags.shape, 1) == expert_ref[0]
+        chosen = jnp.sum(jnp.where(mine, tags, 0.0), axis=1, keepdims=True)
+        share.append(chosen / jnp.sum(tags, axis=1, keepdims=True))
+        start += size
     share = jnp.concatenate(share, axis=0)
     tile = tile_of(wide, 256)
     for at in range(0, wide, tile):
@@ -121,13 +124,13 @@
 VMEM = pl.BlockSpec(memory_space=pltpu.VMEM)
 
 
-def serve(ins, columns, share, experts):
+def serve(ins, expert, experts):
     rows = sum(x.shape[0] for x in ins)
     width, wide = experts[0].shape
     return pl.pallas_call(
-        functools.partial(serve_body, columns),
+        functools.partial(serve_body, len(ins)),
         out_shape=[jax.ShapeDtypeStruct((rows // 2, width), jnp.bfloat16)] * 2,
-        in_specs=[VMEM] * (len(ins) + 4),
+        in_specs=[pl.BlockSpec(memory_space=pltpu.SMEM)] + [VMEM] * (len(ins) + 3),
         out_specs=[VMEM, VMEM],
         scratch_shapes=[pltpu.VMEM((rows, width), jnp.bfloat16), pltpu.VMEM((rows, wide), jnp.bfloat16)],
         compiler_params=pltpu.CompilerParams(vmem_limit_bytes=VMEM_LIMIT),
@@ -135,7 +138,7 @@
             flops=6 * rows * width * wide, bytes_accessed=6 * width * wide, transcendentals=rows * wide
         ),
         name="serve",
-    )(share, *ins, *experts)
+    )(expert, *ins, *experts)
 
 
 def bulk_body(offsets, act_ref, *refs):
@@ -196,9 +199,11 @@
 
 
 def norm_body(parts, *refs):
-    bias_ref, gain_ref, merged_ref, low_ref, high_ref = refs[3 * parts :]
+    bias_ref, gain_ref, tags_ref, merged_ref, low_ref, high_ref = refs[3 * parts :]
     width = merged_ref.shape[1]
     cut = low_ref.shape[0]
+    low_ref[:, width:] = tags_ref[:cut, :]
+    high_ref[:, width:] = tags_ref[cut:, :]
     at = 0
     square = 0.0
     for index in range(parts):
@@ -209,26 +214,27 @@
         square += jnp.sum(merged * merged, axis=1, keepdims=True)
         at = to
     scale = lax.rsqrt(square / width + 1e-06)
-    low_ref[...] = (merged_ref[:cut, :] * scale[:cut] * gain_ref[...]).astype(jnp.bfloat16)
-    high_ref[...] = (merged_ref[cut:, :] * scale[cut:] * gain_ref[...]).astype(jnp.bfloat16)
-
-
-def normalize(parts, bias, gain):
+    low_ref[:, :width] = (merged_ref[:cut, :] * scale[:cut] * gain_ref[...]).astype(jnp.bfloat16)
+    high_ref[:, :width] = (merged_ref[cut:, :] * scale[cut:] * gain_ref[...]).astype(jnp.bfloat16)
+
+
+def normalize(parts, bias, gain, tags):
     rows = parts[0][0].shape[0]
     width = bias.shape[0]
     flat = [array for part in parts for array in part]
-    half = jax.ShapeDtypeStruct((rows // 2, width), jnp.bfloat16)
+    half = jax.ShapeDtypeStruct((rows // 2, width + tags.shape[1]), jnp.bfloat16)
     return pl.pallas_call(
         functools.partial(norm_body, len(parts)),
         out_shape=[jax.ShapeDtypeStruct((rows, width), jnp.float32), half, half],
-        in_specs=[VMEM] * (len(flat) + 2),
+        in_specs=[VMEM] * (len(flat) + 3),
         out_specs=[VMEM] * 3,
-        compiler_params=pltpu.CompilerParams(vmem_limit_bytes=VMEM_LIMIT),
+        compiler_params=pltpu.CompilerParams(vmem_limit_bytes=SMALL_LIMIT),
         name="normalize",
-    )(*flat, bias[None], gain[None])
+    )(*flat, bias[None], gain[None], tags)
 
 
 VMEM_LIMIT = 24 * 1024 * 1024
+SMALL_LIMIT = 12 * 1024 * 1024
 PARTS = 2
 
 
@@ -313,10 +319,12 @@
     act = act.reshape(rows, chips, 2, 2, half)
     kept = jnp.where(first_core, act[:, :, 0], act[:, :, 1])
     given = jnp.where(first_core, act[:, :, 1], act[:, :, 0])
-    act = jnp.concatenate([kept, swap(given)], axis=0)
+    given = swap(given)
+    act = jnp.concatenate([kept, given], axis=0)
     kept = jnp.where(first_group, act[:, :, 0], act[:, :, 1])
     given = jnp.where(first_group, act[:, :, 1], act[:, :, 0])
-    act = jnp.concatenate([kept, cross(given)], axis=0)
+    given = cross(given)
+    act = jnp.concatenate([kept, given], axis=0)
     act = around(act.transpose(1, 0, 2), spot)
 
     mid = (half + 15) // 16 * 8
@@ -336,36 +344,28 @@
         theirs = (theirs + swap(theirs_other)).astype(jnp.bfloat16)
         theirs = cross(theirs)
         streams.append((own, swap(own_other), theirs))
-    merged, *block = normalize(streams, merger_bias, norm_gain)
-
-    counts = combine_ints.astype(jnp.float32)
-    weights = counts / jnp.sum(counts, axis=1, keepdims=True)
-    named = expert_ids[:, :, None] == jnp.arange(n, dtype=jnp.int32)[None, None, :]
-    spread = jnp.sum(jnp.where(named, weights[:, :, None], 0.0), axis=1)
-    share = lax.all_to_all(spread.T, "dp", split_axis=0, concat_axis=0, tiled=True)
-    share = share.reshape(chips, 2, rows)
-    share = jnp.where(first_core, share, share[:, ::-1])
-    share = around(share, spot).reshape(n, rows).T
+    lanes = jnp.arange(-(-n // LANES) * LANES, dtype=jnp.int32)
+    named = expert_ids[:, :, None] == lanes[None, None, :]
+    tags = jnp.sum(jnp.where(named, combine_ints[:, :, None], 0), axis=1).astype(jnp.bfloat16)
+    merged, *block = normalize(streams, merger_bias, norm_gain, tags)
 
     experts = [w[0] for w in (gate_weight, up_weight, down_weight)]
     cut = rows // 2
-    spans = [(0, cut), (cut, rows)]
+    expert = me.astype(jnp.int32)[None]
     outs = []
     left, right = list(block), list(block)
-    for half, span in enumerate(spans):
-        outs.append([serve([block[half], swap(block[half])], [(0, *span), (1, *span)], share, experts)])
-    for step in range(1, far):
-        lo, hi = 2 * (chips - step), 2 * step
-        for half, span in enumerate(spans):
+    for half in range(2):
+        other = swap(block[half])
+        outs.append([serve([block[half], other], expert, experts)])
+    for _ in range(1, far):
+        for half in range(2):
             left[half] = ahead(left[half])
             right[half] = back(right[half])
             others = swap(left[half]), swap(right[half])
-            columns = [(lo, *span), (hi, *span), (lo + 1, *span), (hi + 1, *span)]
-            outs[half].append(serve([left[half], right[half], *others], columns, share, experts))
+            outs[half].append(serve([left[half], right[half], *others], expert, experts))
     top = ahead(left[0])
     bottom = back(right[1])
-    columns = [(2 * far + side, *span) for side in (0, 1) for span in spans]
-    distant = serve([top, bottom, swap(top), swap(bottom)], columns, share, experts)
+    distant = serve([top, bottom, swap(top), swap(bottom)], expert, experts)
     distant = (distant[0], swap(distant[1]))
     outs = [[(own, swap(other)) for own, other in pairs] for pairs in outs]
 
@@ -377,8 +377,11 @@
 
     ahead_high = home(ahead, 1, cut, None)
     back_low = home(back, 0, 0, None)
-    ahead_low = home(ahead, 0, cut, ahead(add(*distant, 0, cut, None)))
-    back_high = home(back, 1, 0, back(add(*distant, cut, cut, None)))
+    top, bottom = add(*distant, 0, cut, None), add(*distant, cut, cut, None)
+    top = ahead(top)
+    bottom = back(bottom)
+    ahead_low = home(ahead, 0, cut, top)
+    back_high = home(back, 1, 0, bottom)
     return finish(merged, *outs[0][0], ahead_low, back_low, *outs[1][0], ahead_high, back_high)
 
 

time: 169 us -> 165 us (0.976)
  local copies, waits for them, and re-layouts: 7.66 us -> 19.2 us
  blocking collectives: 10.1 us -> 0 us
  waiting for transfers between devices: 57 us -> 52.7 us
  Pallas kernels: 33.3 us -> 30.4 us
  other arithmetic: 4 us -> 6.36 us
    unnamed x29 -> x83, local copies, waits for them, and re-layouts: 7.35 us -> 19 us
    all_to_all x1 -> x0, blocking collectives: 10.1 us -> none  [dense(): lax.all_to_all(spread.T, 'dp', split_axis=0, concat_axis=0, tiled=True)]
    ppermute x6, waiting for transfers between devices: 11.9 us -> 5.31 us  [dense(): left[half] = ahead(left[half])]
    pallas_call x9, Pallas kernels: 26.3 us -> 21.4 us  [serve(): pl.pallas_call(functools.partial(serve_body, len(ins)), out_shape=[jax.Sh...]
    ppermute x2, waiting for transfers between devices: 9.28 us -> 5.08 us  [dense(): theirs = cross(theirs)]
    ppermute x6, waiting for transfers between devices: 4.24 us -> 8.03 us  [dense(): right[half] = back(right[half])]
    ppermute x6, starting transfers between devices: 6.43 us -> 9.46 us  [dense(): left[half] = ahead(left[half])]
    ppermute x6, starting transfers between devices: 4.75 us -> 2.69 us  [dense(): right[half] = back(right[half])]
  transfers between devices with their start and end apart: 77 -> 77, of which waited for: 26 -> 26; matrix products, arithmetic and copies ran while one was open for 1% -> 4% of each run, Pallas kernels for 19% -> 17%
where the time goes in v4:
time: 165 us; the launch traced here: 164 us
  starting transfers between devices  55 us (33%)
  waiting for transfers between devices  52.7 us (32%)
  Pallas kernels  30.4 us (18%)
  local copies, waits for them, and re-layouts  19.2 us (12%)
  other arithmetic  6.36 us (4%)
    pallas_call x9, Pallas kernels, serve(): pl.pallas_call(functools.partial(serve_body, len(ins)), out_shape=[jax.Sh...  21.4 us
    unnamed x83, local copies, waits for them, and re-layouts  19 us
    ppermute x12, waiting for transfers between devices, home(): total = way(total)  12.8 us
    ppermute x12, starting transfers between devices, home(): total = way(total)  11.4 us
    ppermute x6, waiting for transfers between devices, dense(): left = ahead(left)  11 us
    ppermute x6, starting transfers between devices, dense(): left = ahead(left)  11 us
    ppermute x6, starting transfers between devices, dense(): left[half] = ahead(left[half])  9.46 us
    ppermute x6, waiting for transfers between devices, dense(): right[half] = back(right[half])  8.03 us
  transfers between devices with their start and end apart: 77, of which 26 were waited for; matrix products, arithmetic and copies ran while one was open for 4% of the time, Pallas kernels for 17%

profile of v4, /device:TPU:0, one launch (start us, length us, event | category | flops | bytes accessed | tf_op | source)
XLA Modules:
  0.0 164.2 jit_solution(11711353485140738239)
XLA Ops:
  0.0 1.3 copy.17
  1.3 2.6 %fusion.1 = bf16[96,2304]{0,1:T(8,128)(2,1)S(1)} fusion(bf16[96,2304]{0,1:T(8,128)(2,1)S(1)} %copy.17), kind=kLoop, calls=%fused_computation.8 | loop fusion | flops 14598144 | bytes 884736 | tf_op jit(solution)/shard_map/convert_element_type | solution.py:318
  5.4 3.1 %collective-permute-start.2 = (bf16[72,1024]{1,0:T(8,128)(2,1)S(1)}, bf16[72,1024]{1,0:T(8,128)(2,1)S(1)}, u32[]{:S(2)}, u32[]{:S(2)}) collective-permute-start(bf16[72,1024]{1,0:T(8,128)(2,1)S(1)} %get-tuple-element.72.refs_0_), channel_id=1, source_target_pairs={{0,4},{1,5},{4,8},{5,9},{8,12},{9,13},{12,14},{13,15},{14,10},{15,... | collective-permute-start | bytes 442376 | tf_op jit(solution)/shard_map/ppermute | solution.py:336
  8.7 2.0 %collective-permute-start.1 = (bf16[192,8,72]{2,0,1:T(8,128)(2,1)S(1)}, bf16[192,8,72]{2,0,1:T(8,128)(2,1)S(1)}, u32[]{:S(2)}, u32[]{:S(2)}) collective-permute-start(bf16[192,8,72]{2,0,1:T(8,128)(2,1)S(1)} %get-tuple-element.66), channel_id=1, source_target_pairs={{0,16},{16,0},{1,17},{17,1},{2,18},{18,2},{3,19},{19,3},{4,20},{20... | collective-permute-start | bytes 663560 | tf_op jit(solution)/shard_map/ppermute | solution.py:326
  10.7 1.6 collective-permute-start.13
  12.8 1.6 collective-permute-start.4
  14.8 2.7 %collective-permute-done.13.refs_1_ = bf16[72,1024]{1,0:T(8,128)(2,1)S(1)} collective-permute-done((bf16[72,1024]{1,0:T(8,128)(2,1)S(1)}, bf16[72,1024]{1,0:T(8,128)(2,1)S(1)}, u32[]{:S(2)}, u32[]{:S(2)}) %collective-permute-start.13) | collective-permute-done | bytes 147488 | tf_op jit(solution)/shard_map/ppermute | solution.py:336
  17.5 1.6 collective-permute-start.15
  20.6 1.6 collective-permute-start.6
  22.9 3.0 %collective-permute-done.6.refs_5_ = bf16[72,1024]{1,0:T(8,128)(2,1)S(1)} collective-permute-done((bf16[72,1024]{1,0:T(8,128)(2,1)S(1)}, bf16[72,1024]{1,0:T(8,128)(2,1)S(1)}, u32[]{:S(2)}, u32[]{:S(2)}) %collective-permute-start.6) | collective-permute-done | bytes 147488 | tf_op jit(solution)/shard_map/ppermute | solution.py:336
  25.9 1.6 collective-permute-start.8
  28.9 1.6 bulk.2.total_ref
  30.4 1.6 collective-permute-done.9.bottom_ref
  32.0 1.2 last.2
  33.3 1.6 collective-permute-start.17
  35.3 4.2 %collective-permute-done.17.refs_5_ = bf16[72,1024]{1,0:T(8,128)(2,1)S(1)} collective-permute-done((bf16[72,1024]{1,0:T(8,128)(2,1)S(1)}, bf16[72,1024]{1,0:T(8,128)(2,1)S(1)}, u32[]{:S(2)}, u32[]{:S(2)}) %collective-permute-start.17) | collective-permute-done | bytes 147488 | tf_op jit(solution)/shard_map/ppermute | solution.py:336
  39.5 1.6 collective-permute-start.19
  41.6 1.5 bulk.3.total_ref
  43.2 2.3 %collective-permute-done.20.bottom_ref = bf16[32,1024]{1,0:T(8,128)(2,1)S(1)} collective-permute-done((bf16[32,1024]{1,0:T(8,128)(2,1)S(1)}, bf16[32,1024]{1,0:T(8,128)(2,1)S(1)}, u32[]{:S(2)}, u32[]{:S(2)}) %collective-permute-start.20) | collective-permute-done | bytes 65568 | tf_op jit(solution)/shard_map/ppermute | solution.py:341
  45.4 1.2 last.3
  49.6 1.1 collective-permute-start.23
  50.8 1.4 copy.21
  52.2 1.4 copy.20
  54.7 1.4 collective-permute-done.12.refs_2_
  56.1 3.7 %collective-permute-done.23.refs_5_ = bf16[96,1024]{1,0:T(8,128)(2,1)} collective-permute-done((bf16[96,1024]{1,0:T(8,128)(2,1)}, bf16[96,1024]{1,0:T(8,128)(2,1)}, u32[]{:S(2)}, u32[]{:S(2)}) %collective-permute-start.23) | collective-permute-done | bytes 196640 | tf_op jit(solution)/shard_map/ppermute | solution.py:345
  60.8 1.5 normalize.1
  63.2 1.6 collective-permute-start.26
  65.7 1.6 collective-permute-start.58
  67.3 4.1 %collective-permute-done.26.refs_0_ = bf16[48,2176]{1,0:T(8,128)(2,1)} collective-permute-done((bf16[48,2176]{1,0:T(8,128)(2,1)S(1)}, bf16[48,2176]{1,0:T(8,128)(2,1)}, u32[]{:S(2)}, u32[]{:S(2)}) %collective-permute-start.26) | collective-permute-done | bytes 208928 | tf_op jit(solution)/shard_map/ppermute | solution.py:362
  71.4 1.6 collective-permute-start.31
  74.1 3.2 %collective-permute-done.42.refs_1_ = bf16[48,2176]{1,0:T(8,128)(2,1)S(1)} collective-permute-done((bf16[48,2176]{1,0:T(8,128)(2,1)S(1)}, bf16[48,2176]{1,0:T(8,128)(2,1)S(1)}, u32[]{:S(2)}, u32[]{:S(2)}) %collective-permute-start.42) | collective-permute-done | bytes 208928 | tf_op jit(solution)/shard_map/ppermute | solution.py:363
  77.8 1.6 collective-permute-start.62
  80.2 1.6 collective-permute-start.36
  83.6 2.7 %collective-permute-done.43.refs_1_ = bf16[48,2176]{1,0:T(8,128)(2,1)S(1)} collective-permute-done((bf16[48,2176]{1,0:T(8,128)(2,1)S(1)}, bf16[48,2176]{1,0:T(8,128)(2,1)S(1)}, u32[]{:S(2)}, u32[]{:S(2)}) %collective-permute-start.43) | collective-permute-done | bytes 208928 | tf_op jit(solution)/shard_map/ppermute | solution.py:363
  86.7 1.6 collective-permute-start.66
  88.7 2.1 %collective-permute-done.37.refs_1_ = bf16[48,2176]{1,0:T(8,128)(2,1)S(1)} collective-permute-done((bf16[48,2176]{1,0:T(8,128)(2,1)S(1)}, bf16[48,2176]{1,0:T(8,128)(2,1)S(1)}, u32[]{:S(2)}, u32[]{:S(2)}) %collective-permute-start.37) | collective-permute-done | bytes 208928 | tf_op jit(solution)/shard_map/ppermute | solution.py:363
  91.4 1.5 collective-permute-start.41
  96.1 3.0 %collective-permute-done.41.refs_0_ = bf16[48,2176]{1,0:T(8,128)(2,1)} collective-permute-done((bf16[48,2176]{1,0:T(8,128)(2,1)S(1)}, bf16[48,2176]{1,0:T(8,128)(2,1)}, u32[]{:S(2)}, u32[]{:S(2)}) %collective-permute-start.41) | collective-permute-done | bytes 208928 | tf_op jit(solution)/shard_map/ppermute | solution.py:366
  99.1 2.1 %collective-permute-done.45.refs_1_ = bf16[48,2176]{1,0:T(8,128)(2,1)} collective-permute-done((bf16[48,2176]{1,0:T(8,128)(2,1)}, bf16[48,2176]{1,0:T(8,128)(2,1)}, u32[]{:S(2)}, u32[]{:S(2)}) %collective-permute-start.45) | collective-permute-done | bytes 208928 | tf_op jit(solution)/shard_map/ppermute | solution.py:367
  101.2 1.9 %copy-done.1 = bf16[1,2048,768]{2,1,0:T(8,128)(2,1)S(1)} copy-done((bf16[1,2048,768]{2,1,0:T(8,128)(2,1)S(1)}, bf16[1,2048,768]{2,1,0:T(8,128)(2,1)}, u32[]{:S(2)}) %copy-start.1) | copy-done | bytes 3145752
  103.1 1.9 %copy-done.3 = bf16[1,768,2048]{2,1,0:T(8,128)(2,1)S(1)} copy-done((bf16[1,768,2048]{2,1,0:T(8,128)(2,1)S(1)}, bf16[1,768,2048]{2,1,0:T(8,128)(2,1)}, u32[]{:S(2)}) %copy-start.3) | copy-done | bytes 3145752
  108.8 2.1 %serve.12 = (bf16[96,2048]{1,0:T(8,128)(2,1)S(1)}, bf16[96,2048]{1,0:T(8,128)(2,1)S(1)}) custom-call(s32[1]{0:T(128)} %bitcast.8.expert_ref, bf16[48,2176]{1,0:T(8,128)(2,1)S(1)} %copy-done.29, bf16[48,2176]{1,0:T(8,128)(2,1)S(1)} %copy-done.31, bf16[48,2176]{1,0:T(8,128)(2,1)S(1)} %copy-done.33, bf16[48,2176]{1,0:T(8,128)(2,1)S(1)} %copy-done.35, ...), custom_call_target="tpu_custom_call" | custom-call | flops 1811939328 | bytes 9437184 | tf_op jit(solution)/shard_map/serve/pallas_call | solution.py:130
  112.1 3.3 %serve.17 = (bf16[96,2048]{1,0:T(8,128)(2,1)S(1)}, bf16[96,2048]{1,0:T(8,128)(2,1)S(1)}) custom-call(s32[1]{0:T(128)} %bitcast.8.expert_ref, bf16[48,2176]{1,0:T(8,128)(2,1)} %collective-permute-done.66.refs_0_, bf16[48,2176]{1,0:T(8,128)(2,1)} %collective-permute-done.44.refs_1_, bf16[48,2176]{1,0:T(8,128)(2,1)} %collective-permute-done.67.refs_2_, ...), custom_call_target="tpu_custom_call" | custom-call | flops 1811939328 | bytes 9437184 | tf_op jit(solution)/shard_map/serve/pallas_call | solution.py:130
  115.9 3.2 %serve.13 = (bf16[96,2048]{1,0:T(8,128)(2,1)S(1)}, bf16[96,2048]{1,0:T(8,128)(2,1)S(1)}) custom-call(s32[1]{0:T(128)} %bitcast.8.expert_ref, bf16[48,2176]{1,0:T(8,128)(2,1)} %collective-permute-done.41.refs_0_, bf16[48,2176]{1,0:T(8,128)(2,1)} %collective-permute-done.45.refs_1_, bf16[48,2176]{1,0:T(8,128)(2,1)} %collective-permute-done.46.refs_2_, ...), custom_call_target="tpu_custom_call" | custom-call | flops 1811939328 | bytes 9437184 | tf_op jit(solution)/shard_map/serve/pallas_call | solution.py:130
  120.3 2.1 %serve.11 = (bf16[96,2048]{1,0:T(8,128)(2,1)S(1)}, bf16[96,2048]{1,0:T(8,128)(2,1)S(1)}) custom-call(s32[1]{0:T(128)} %bitcast.8.expert_ref, bf16[48,2176]{1,0:T(8,128)(2,1)S(1)} %copy-done.21, bf16[48,2176]{1,0:T(8,128)(2,1)S(1)} %copy-done.25, bf16[48,2176]{1,0:T(8,128)(2,1)S(1)} %collective-permute-done.33.refs_2_, ...), custom_call_target="tpu_custom_call" | custom-call | flops 1811939328 | bytes 9437184 | tf_op jit(solution)/shard_map/serve/pallas_call | solution.py:130
  122.5 2.1 %serve.16 = (bf16[96,2048]{1,0:T(8,128)(2,1)S(1)}, bf16[96,2048]{1,0:T(8,128)(2,1)S(1)}) custom-call(s32[1]{0:T(128)} %bitcast.8.expert_ref, bf16[48,2176]{1,0:T(8,128)(2,1)S(1)} %copy-done.27, bf16[48,2176]{1,0:T(8,128)(2,1)S(1)} %copy-done.23, bf16[48,2176]{1,0:T(8,128)(2,1)S(1)} %collective-permute-done.63.refs_2_, ...), custom_call_target="tpu_custom_call" | custom-call | flops 1811939328 | bytes 9437184 | tf_op jit(solution)/shard_map/serve/pallas_call | solution.py:130
  125.7 1.8 %collective-permute-start.73 = (bf16[48,2048]{1,0:T(8,128)(2,1)S(1)}, bf16[48,2048]{1,0:T(8,128)(2,1)S(1)}, u32[]{:S(2)}, u32[]{:S(2)}) collective-permute-start(bf16[48,2048]{1,0:T(8,128)(2,1)S(1)} %add.34), channel_id=1, source_target_pairs={{0,2},{1,3},{4,0},{5,1},{8,4},{9,5},{12,8},{13,9},{14,12},{15,13},... | collective-permute-start | bytes 589832 | tf_op jit(solution)/shard_map/ppermute | solution.py:382
  127.5 3.1 %serve.10 = (bf16[96,2048]{1,0:T(8,128)(2,1)S(1)}, bf16[96,2048]{1,0:T(8,128)(2,1)S(1)}) custom-call(s32[1]{0:T(128)} %bitcast.8.expert_ref, bf16[48,2176]{1,0:T(8,128)(2,1)} %collective-permute-done.26.refs_0_, bf16[48,2176]{1,0:T(8,128)(2,1)S(1)} %copy-done.19, bf16[48,2176]{1,0:T(8,128)(2,1)} %collective-permute-done.28.refs_2_, ...), custom_call_target="tpu_custom_call" | custom-call | flops 1811939328 | bytes 9437184 | tf_op jit(solution)/shard_map/serve/pallas_call | solution.py:130
  131.3 1.3 collective-permute-done.49.refs_0_
  133.6 2.1 %serve.15 = (bf16[96,2048]{1,0:T(8,128)(2,1)S(1)}, bf16[96,2048]{1,0:T(8,128)(2,1)S(1)}) custom-call(s32[1]{0:T(128)} %bitcast.8.expert_ref, bf16[48,2176]{1,0:T(8,128)(2,1)S(1)} %copy-done.17, bf16[48,2176]{1,0:T(8,128)(2,1)S(1)} %copy-done.15, bf16[48,2176]{1,0:T(8,128)(2,1)S(1)} %collective-permute-done.59.refs_2_, ...), custom_call_target="tpu_custom_call" | custom-call | flops 1811939328 | bytes 9437184 | tf_op jit(solution)/shard_map/serve/pallas_call | solution.py:130
  135.9 1.6 collective-permute-done.53.refs_0_
  137.5 1.2 collective-permute-start.74
  138.7 1.6 collective-permute-done.70.refs_0_
  140.9 2.2 %collective-permute-done.50.refs_0_ = bf16[48,2048]{1,0:T(8,128)(2,1)S(1)} collective-permute-done((bf16[48,2048]{1,0:T(8,128)(2,1)S(1)}, bf16[48,2048]{1,0:T(8,128)(2,1)S(1)}, u32[]{:S(2)}, u32[]{:S(2)}) %collective-permute-start.50) | collective-permute-done | bytes 196640 | tf_op jit(solution)/shard_map/ppermute | solution.py:375
  143.2 1.2 collective-permute-start.71
  144.4 1.7 %serve.9 = (bf16[48,2048]{1,0:T(8,128)(2,1)S(1)}, bf16[48,2048]{1,0:T(8,128)(2,1)S(1)}) custom-call(s32[1]{0:T(128)} %bitcast.8.expert_ref, bf16[48,2176]{1,0:T(8,128)(2,1)S(1)} %copy-done.11, bf16[48,2176]{1,0:T(8,128)(2,1)S(1)} %copy-done.13, bf16[2048,768]{1,0:T(8,128)(2,1)S(1)} %bitcast.24, bf16[2048,768]{1,0:T(8,128)(2,1)S(1)} %bitcast.33, ...), custom_call_target="tpu_custom_call" | custom-call | flops 905969664 | bytes 9437184 | tf_op jit(solution)/shard_map/serve/pallas_call | solution.py:130
  146.6 1.8 %collective-permute-start.75 = (bf16[48,2048]{1,0:T(8,128)(2,1)S(1)}, bf16[48,2048]{1,0:T(8,128)(2,1)S(1)}, u32[]{:S(2)}, u32[]{:S(2)}) collective-permute-start(bf16[48,2048]{1,0:T(8,128)(2,1)S(1)} %add.36), channel_id=1, source_target_pairs={{0,2},{1,3},{4,0},{5,1},{8,4},{9,5},{12,8},{13,9},{14,12},{15,13},... | collective-permute-start | bytes 589832 | tf_op jit(solution)/shard_map/ppermute | solution.py:375
  148.4 1.7 %serve.14 = (bf16[48,2048]{1,0:T(8,128)(2,1)S(1)}, bf16[48,2048]{1,0:T(8,128)(2,1)S(1)}) custom-call(s32[1]{0:T(128)} %bitcast.8.expert_ref, bf16[48,2176]{1,0:T(8,128)(2,1)S(1)} %copy-done.9, bf16[48,2176]{1,0:T(8,128)(2,1)S(1)} %collective-permute-done.56.refs_1_, bf16[2048,768]{1,0:T(8,128)(2,1)S(1)} %bitcast.25, bf16[2048,768]{1,0:T(8,128)(2,1)S(1)} %bitcast.34, ...), custom_call_target="tpu_custom_call" | custom-call | flops 905969664 | bytes 9437184 | tf_op jit(solution)/shard_map/serve/pallas_call | solution.py:130
  151.6 1.4 collective-permute-done.51.refs_0_
  153.0 1.9 %collective-permute-start.72 = (bf16[48,2048]{1,0:T(8,128)(2,1)S(1)}, bf16[48,2048]{1,0:T(8,128)(2,1)S(1)}, u32[]{:S(2)}, u32[]{:S(2)}) collective-permute-start(bf16[48,2048]{1,0:T(8,128)(2,1)S(1)} %add.33), channel_id=1, source_target_pairs={{0,4},{1,5},{4,8},{5,9},{8,12},{9,13},{12,14},{13,15},{14,10},{15,... | collective-permute-start | bytes 589832 | tf_op jit(solution)/shard_map/ppermute | solution.py:375
  155.5 1.8 %collective-permute-start.76 = (bf16[48,2048]{1,0:T(8,128)(2,1)S(1)}, bf16[48,2048]{1,0:T(8,128)(2,1)S(1)}, u32[]{:S(2)}, u32[]{:S(2)}) collective-permute-start(bf16[48,2048]{1,0:T(8,128)(2,1)S(1)} %add.37), channel_id=1, source_target_pairs={{0,2},{1,3},{4,0},{5,1},{8,4},{9,5},{12,8},{13,9},{14,12},{15,13},... | collective-permute-start | bytes 589832 | tf_op jit(solution)/shard_map/ppermute | solution.py:375
  157.3 1.2 collective-permute-done.55.refs_3_
  158.5 2.3 %collective-permute-done.72.refs_6_ = bf16[48,2048]{1,0:T(8,128)(2,1)S(1)} collective-permute-done((bf16[48,2048]{1,0:T(8,128)(2,1)S(1)}, bf16[48,2048]{1,0:T(8,128)(2,1)S(1)}, u32[]{:S(2)}, u32[]{:S(2)}) %collective-permute-start.72) | collective-permute-done | bytes 196640 | tf_op jit(solution)/shard_map/ppermute | solution.py:375
  160.8 2.4 %collective-permute-done.52.refs_2_ = bf16[48,2048]{1,0:T(8,128)(2,1)S(1)} collective-permute-done((bf16[48,2048]{1,0:T(8,128)(2,1)S(1)}, bf16[48,2048]{1,0:T(8,128)(2,1)S(1)}, u32[]{:S(2)}, u32[]{:S(2)}) %collective-permute-start.52) | collective-permute-done | bytes 196640 | tf_op jit(solution)/shard_map/ppermute | solution.py:375
  (220 shorter events, 36.7 us)
Async XLA Ops:
  5.4 7.4 %collective-permute-start.2 = (bf16[72,1024]{1,0:T(8,128)(2,1)S(1)}, bf16[72,1024]{1,0:T(8,128)(2,1)S(1)}, u32[]{:S(2)}, u32[]{:S(2)}) collective-permute-start(bf16[72,1024]{1,0:T(8,128)(2,1)S(1)} %get-tuple-element.72.refs_0_), channel_id=1, source_target_pairs={{0,4},{1,5},{4,8},{5,9},{8,12},{9,13},{12,14},{13,15},{14,10},{15,... | collective-permute-start | bytes 442376 | tf_op jit(solution)/shard_map/ppermute | solution.py:336
  8.7 13.9 %collective-permute-start.1 = (bf16[192,8,72]{2,0,1:T(8,128)(2,1)S(1)}, bf16[192,8,72]{2,0,1:T(8,128)(2,1)S(1)}, u32[]{:S(2)}, u32[]{:S(2)}) collective-permute-start(bf16[192,8,72]{2,0,1:T(8,128)(2,1)S(1)} %get-tuple-element.66), channel_id=1, source_target_pairs={{0,16},{16,0},{1,17},{17,1},{2,18},{18,2},{3,19},{19,3},{4,20},{20... | collective-permute-start | bytes 663560 | tf_op jit(solution)/shard_map/ppermute | solution.py:326
  10.7 6.7 %collective-permute-start.13 = (bf16[72,1024]{1,0:T(8,128)(2,1)S(1)}, bf16[72,1024]{1,0:T(8,128)(2,1)S(1)}, u32[]{:S(2)}, u32[]{:S(2)}) collective-permute-start(bf16[72,1024]{1,0:T(8,128)(2,1)S(1)} %get-tuple-element.71.refs_0_), channel_id=1, source_target_pairs={{0,4},{1,5},{4,8},{5,9},{8,12},{9,13},{12,14},{13,15},{14,10},{15,... | collective-permute-start | bytes 442376 | tf_op jit(solution)/shard_map/ppermute | solution.py:336
  12.3 6.7 %collective-permute-start.14 = (bf16[72,1024]{1,0:T(8,128)(2,1)S(1)}, bf16[72,1024]{1,0:T(8,128)(2,1)S(1)}, u32[]{:S(2)}, u32[]{:S(2)}) collective-permute-start(bf16[72,1024]{1,0:T(8,128)(2,1)S(1)} %get-tuple-element.71.refs_0_), channel_id=1, source_target_pairs={{0,2},{1,3},{4,0},{5,1},{8,4},{9,5},{12,8},{13,9},{14,12},{15,13},... | collective-permute-start | bytes 442376 | tf_op jit(solution)/shard_map/ppermute | solution.py:337
  12.8 7.9 %collective-permute-start.4 = (bf16[72,1024]{1,0:T(8,128)(2,1)S(1)}, bf16[72,1024]{1,0:T(8,128)(2,1)S(1)}, u32[]{:S(2)}, u32[]{:S(2)}) collective-permute-start(bf16[72,1024]{1,0:T(8,128)(2,1)S(1)} %collective-permute-done.2.refs_1_), channel_id=1, source_target_pairs={{0,4},{1,5},{4,8},{5,9},{8,12},{9,13},{12,14},{13,15},{14,10},{15,... | collective-permute-start | bytes 442376 | tf_op jit(solution)/shard_map/ppermute | solution.py:336
  14.4 7.8 %collective-permute-start.5 = (bf16[72,1024]{1,0:T(8,128)(2,1)S(1)}, bf16[72,1024]{1,0:T(8,128)(2,1)S(1)}, u32[]{:S(2)}, u32[]{:S(2)}) collective-permute-start(bf16[72,1024]{1,0:T(8,128)(2,1)S(1)} %collective-permute-done.3.refs_2_), channel_id=1, source_target_pairs={{0,2},{1,3},{4,0},{5,1},{8,4},{9,5},{12,8},{13,9},{14,12},{15,13},... | collective-permute-start | bytes 442376 | tf_op jit(solution)/shard_map/ppermute | solution.py:337
  17.5 15.8 %collective-permute-start.15 = (bf16[72,1024]{1,0:T(8,128)(2,1)S(1)}, bf16[72,1024]{1,0:T(8,128)(2,1)S(1)}, u32[]{:S(2)}, u32[]{:S(2)}) collective-permute-start(bf16[72,1024]{1,0:T(8,128)(2,1)S(1)} %collective-permute-done.13.refs_1_), channel_id=1, source_target_pairs={{0,4},{1,5},{4,8},{5,9},{8,12},{9,13},{12,14},{13,15},{14,10},{15,... | collective-permute-start | bytes 442376 | tf_op jit(solution)/shard_map/ppermute | solution.py:336
  19.0 15.8 %collective-permute-start.16 = (bf16[72,1024]{1,0:T(8,128)(2,1)S(1)}, bf16[72,1024]{1,0:T(8,128)(2,1)S(1)}, u32[]{:S(2)}, u32[]{:S(2)}) collective-permute-start(bf16[72,1024]{1,0:T(8,128)(2,1)S(1)} %collective-permute-done.14.refs_2_), channel_id=1, source_target_pairs={{0,2},{1,3},{4,0},{5,1},{8,4},{9,5},{12,8},{13,9},{14,12},{15,13},... | collective-permute-start | bytes 442376 | tf_op jit(solution)/shard_map/ppermute | solution.py:337
  25.9 6.1 %collective-permute-start.8 = (bf16[40,1024]{1,0:T(8,128)(2,1)S(1)}, bf16[40,1024]{1,0:T(8,128)(2,1)S(1)}, u32[]{:S(2)}, u32[]{:S(2)}) collective-permute-start(bf16[40,1024]{1,0:T(8,128)(2,1)S(1)} %slice.65), channel_id=1, source_target_pairs={{0,4},{1,5},{4,8},{5,9},{8,12},{9,13},{12,14},{13,15},{14,10},{15,... | collective-permute-start | bytes 245768 | tf_op jit(solution)/shard_map/ppermute | solution.py:340
  33.3 14.0 %collective-permute-start.11 = (f32[96,1024]{1,0:T(8,128)S(1)}, f32[96,1024]{1,0:T(8,128)S(1)}, u32[]{:S(2)}, u32[]{:S(2)}) collective-permute-start(f32[96,1024]{1,0:T(8,128)S(1)} %get-tuple-element.37), channel_id=1, source_target_pairs={{0,1},{1,0},{2,3},{3,2},{4,5},{5,4},{6,7},{7,6},{8,9},{9,8},{10,11... | collective-permute-start | bytes 1179656 | tf_op jit(solution)/shard_map/ppermute | solution.py:344
  33.3 6.3 %collective-permute-start.17 = (bf16[72,1024]{1,0:T(8,128)(2,1)S(1)}, bf16[72,1024]{1,0:T(8,128)(2,1)S(1)}, u32[]{:S(2)}, u32[]{:S(2)}) collective-permute-start(bf16[72,1024]{1,0:T(8,128)(2,1)S(1)} %collective-permute-done.15.refs_3_), channel_id=1, source_target_pairs={{0,4},{1,5},{4,8},{5,9},{8,12},{9,13},{12,14},{13,15},{14,10},{15,... | collective-permute-start | bytes 442376 | tf_op jit(solution)/shard_map/ppermute | solution.py:336
  34.9 6.3 %collective-permute-start.18 = (bf16[72,1024]{1,0:T(8,128)(2,1)S(1)}, bf16[72,1024]{1,0:T(8,128)(2,1)S(1)}, u32[]{:S(2)}, u32[]{:S(2)}) collective-permute-start(bf16[72,1024]{1,0:T(8,128)(2,1)S(1)} %collective-permute-done.16.refs_4_), channel_id=1, source_target_pairs={{0,2},{1,3},{4,0},{5,1},{8,4},{9,5},{12,8},{13,9},{14,12},{15,13},... | collective-permute-start | bytes 442376 | tf_op jit(solution)/shard_map/ppermute | solution.py:337
  46.7 8.0 %collective-permute-start.10 = (f32[96,1024]{1,0:T(8,128)}, f32[96,1024]{1,0:T(8,128)}, u32[]{:S(2)}, u32[]{:S(2)}) collective-permute-start(f32[96,1024]{1,0:T(8,128)} %get-tuple-element.35), channel_id=1, source_target_pairs={{0,1},{1,0},{2,3},{3,2},{4,5},{5,4},{6,7},{7,6},{8,9},{9,8},{10,11... | collective-permute-start | bytes 1179656 | tf_op jit(solution)/shard_map/ppermute | solution.py:346
  47.2 7.5 %collective-permute-start.21 = (f32[96,1024]{1,0:T(8,128)}, f32[96,1024]{1,0:T(8,128)}, u32[]{:S(2)}, u32[]{:S(2)}) collective-permute-start(f32[96,1024]{1,0:T(8,128)} %get-tuple-element.39), channel_id=1, source_target_pairs={{0,1},{1,0},{2,3},{3,2},{4,5},{5,4},{6,7},{7,6},{8,9},{9,8},{10,11... | collective-permute-start | bytes 1179656 | tf_op jit(solution)/shard_map/ppermute | solution.py:346
  48.0 8.1 %collective-permute-start.12 = (bf16[96,1024]{1,0:T(8,128)(2,1)}, bf16[96,1024]{1,0:T(8,128)(2,1)}, u32[]{:S(2)}, u32[]{:S(2)}) collective-permute-start(bf16[96,1024]{1,0:T(8,128)(2,1)} %add_convert_fusion.1), channel_id=1, source_target_pairs={{0,16},{16,0},{1,17},{17,1},{2,18},{18,2},{3,19},{19,3},{4,20},{20... | collective-permute-start | bytes 589832 | tf_op jit(solution)/shard_map/ppermute | solution.py:345
  49.6 10.1 %collective-permute-start.23 = (bf16[96,1024]{1,0:T(8,128)(2,1)}, bf16[96,1024]{1,0:T(8,128)(2,1)}, u32[]{:S(2)}, u32[]{:S(2)}) collective-permute-start(bf16[96,1024]{1,0:T(8,128)(2,1)} %add_convert_fusion), channel_id=1, source_target_pairs={{0,16},{16,0},{1,17},{17,1},{2,18},{18,2},{3,19},{19,3},{4,20},{20... | collective-permute-start | bytes 589832 | tf_op jit(solution)/shard_map/ppermute | solution.py:345
  63.2 8.1 %collective-permute-start.26 = (bf16[48,2176]{1,0:T(8,128)(2,1)S(1)}, bf16[48,2176]{1,0:T(8,128)(2,1)}, u32[]{:S(2)}, u32[]{:S(2)}) collective-permute-start(bf16[48,2176]{1,0:T(8,128)(2,1)S(1)} %get-tuple-element.43.refs_0_), channel_id=1, source_target_pairs={{0,4},{1,5},{4,8},{5,9},{8,12},{9,13},{12,14},{13,15},{14,10},{15,... | collective-permute-start | bytes 626696 | tf_op jit(solution)/shard_map/ppermute | solution.py:362
  64.8 8.1 %collective-permute-start.27 = (bf16[48,2176]{1,0:T(8,128)(2,1)S(1)}, bf16[48,2176]{1,0:T(8,128)(2,1)S(1)}, u32[]{:S(2)}, u32[]{:S(2)}) collective-permute-start(bf16[48,2176]{1,0:T(8,128)(2,1)S(1)} %get-tuple-element.43.refs_0_), channel_id=1, source_target_pairs={{0,2},{1,3},{4,0},{5,1},{8,4},{9,5},{12,8},{13,9},{14,12},{15,13},... | collective-permute-start | bytes 626696 | tf_op jit(solution)/shard_map/ppermute | solution.py:363
  65.3 12.1 %collective-permute-start.42 = (bf16[48,2176]{1,0:T(8,128)(2,1)S(1)}, bf16[48,2176]{1,0:T(8,128)(2,1)S(1)}, u32[]{:S(2)}, u32[]{:S(2)}) collective-permute-start(bf16[48,2176]{1,0:T(8,128)(2,1)S(1)} %get-tuple-element.52.refs_0_), channel_id=1, source_target_pairs={{0,2},{1,3},{4,0},{5,1},{8,4},{9,5},{12,8},{13,9},{14,12},{15,13},... | collective-permute-start | bytes 626696 | tf_op jit(solution)/shard_map/ppermute | solution.py:363
  65.7 12.1 %collective-permute-start.58 = (bf16[48,2176]{1,0:T(8,128)(2,1)S(1)}, bf16[48,2176]{1,0:T(8,128)(2,1)S(1)}, u32[]{:S(2)}, u32[]{:S(2)}) collective-permute-start(bf16[48,2176]{1,0:T(8,128)(2,1)S(1)} %get-tuple-element.52.refs_0_), channel_id=1, source_target_pairs={{0,4},{1,5},{4,8},{5,9},{8,12},{9,13},{12,14},{13,15},{14,10},{15,... | collective-permute-start | bytes 626696 | tf_op jit(solution)/shard_map/ppermute | solution.py:362
  71.4 8.8 %collective-permute-start.31 = (bf16[48,2176]{1,0:T(8,128)(2,1)}, bf16[48,2176]{1,0:T(8,128)(2,1)S(1)}, u32[]{:S(2)}, u32[]{:S(2)}) collective-permute-start(bf16[48,2176]{1,0:T(8,128)(2,1)} %collective-permute-done.26.refs_0_), channel_id=1, source_target_pairs={{0,4},{1,5},{4,8},{5,9},{8,12},{9,13},{12,14},{13,15},{14,10},{15,... | collective-permute-start | bytes 626696 | tf_op jit(solution)/shard_map/ppermute | solution.py:362
  73.0 8.8 %collective-permute-start.32 = (bf16[48,2176]{1,0:T(8,128)(2,1)S(1)}, bf16[48,2176]{1,0:T(8,128)(2,1)S(1)}, u32[]{:S(2)}, u32[]{:S(2)}) collective-permute-start(bf16[48,2176]{1,0:T(8,128)(2,1)S(1)} %collective-permute-done.27.refs_1_), channel_id=1, source_target_pairs={{0,2},{1,3},{4,0},{5,1},{8,4},{9,5},{12,8},{13,9},{14,12},{15,13},... | collective-permute-start | bytes 626696 | tf_op jit(solution)/shard_map/ppermute | solution.py:363
  73.4 8.9 %collective-permute-start.24 = (bf16[48,2176]{1,0:T(8,128)(2,1)S(1)}, bf16[48,2176]{1,0:T(8,128)(2,1)S(1)}, u32[]{:S(2)}, u32[]{:S(2)}) collective-permute-start(bf16[48,2176]{1,0:T(8,128)(2,1)S(1)} %get-tuple-element.43.refs_0_), channel_id=1, source_target_pairs={{0,1},{1,0},{2,3},{3,2},{4,5},{5,4},{6,7},{7,6},{8,9},{9,8},{10,11... | collective-permute-start | bytes 626696 | tf_op jit(solution)/shard_map/ppermute | solution.py:358
  77.3 9.0 %collective-permute-start.43 = (bf16[48,2176]{1,0:T(8,128)(2,1)S(1)}, bf16[48,2176]{1,0:T(8,128)(2,1)S(1)}, u32[]{:S(2)}, u32[]{:S(2)}) collective-permute-start(bf16[48,2176]{1,0:T(8,128)(2,1)S(1)} %collective-permute-done.42.refs_1_), channel_id=1, source_target_pairs={{0,2},{1,3},{4,0},{5,1},{8,4},{9,5},{12,8},{13,9},{14,12},{15,13},... | collective-permute-start | bytes 626696 | tf_op jit(solution)/shard_map/ppermute | solution.py:363
  77.8 9.0 %collective-permute-start.62 = (bf16[48,2176]{1,0:T(8,128)(2,1)S(1)}, bf16[48,2176]{1,0:T(8,128)(2,1)S(1)}, u32[]{:S(2)}, u32[]{:S(2)}) collective-permute-start(bf16[48,2176]{1,0:T(8,128)(2,1)S(1)} %collective-permute-done.58.refs_0_), channel_id=1, source_target_pairs={{0,4},{1,5},{4,8},{5,9},{8,12},{9,13},{12,14},{13,15},{14,10},{15,... | collective-permute-start | bytes 626696 | tf_op jit(solution)/shard_map/ppermute | solution.py:362
  80.2 8.4 %collective-permute-start.36 = (bf16[48,2176]{1,0:T(8,128)(2,1)S(1)}, bf16[48,2176]{1,0:T(8,128)(2,1)S(1)}, u32[]{:S(2)}, u32[]{:S(2)}) collective-permute-start(bf16[48,2176]{1,0:T(8,128)(2,1)S(1)} %collective-permute-done.31.refs_0_), channel_id=1, source_target_pairs={{0,4},{1,5},{4,8},{5,9},{8,12},{9,13},{12,14},{13,15},{14,10},{15,... | collective-permute-start | bytes 626696 | tf_op jit(solution)/shard_map/ppermute | solution.py:362
  81.8 8.9 %collective-permute-start.37 = (bf16[48,2176]{1,0:T(8,128)(2,1)S(1)}, bf16[48,2176]{1,0:T(8,128)(2,1)S(1)}, u32[]{:S(2)}, u32[]{:S(2)}) collective-permute-start(bf16[48,2176]{1,0:T(8,128)(2,1)S(1)} %collective-permute-done.32.refs_1_), channel_id=1, source_target_pairs={{0,2},{1,3},{4,0},{5,1},{8,4},{9,5},{12,8},{13,9},{14,12},{15,13},... | collective-permute-start | bytes 626696 | tf_op jit(solution)/shard_map/ppermute | solution.py:363
  82.9 8.5 %collective-permute-start.56 = (bf16[48,2176]{1,0:T(8,128)(2,1)S(1)}, bf16[48,2176]{1,0:T(8,128)(2,1)S(1)}, u32[]{:S(2)}, u32[]{:S(2)}) collective-permute-start(bf16[48,2176]{1,0:T(8,128)(2,1)S(1)} %get-tuple-element.52.refs_0_), channel_id=1, source_target_pairs={{0,1},{1,0},{2,3},{3,2},{4,5},{5,4},{6,7},{7,6},{8,9},{9,8},{10,11... | collective-permute-start | bytes 626696 | tf_op jit(solution)/shard_map/ppermute | solution.py:358
  86.3 7.4 %collective-permute-start.44 = (bf16[48,2176]{1,0:T(8,128)(2,1)S(1)}, bf16[48,2176]{1,0:T(8,128)(2,1)}, u32[]{:S(2)}, u32[]{:S(2)}) collective-permute-start(bf16[48,2176]{1,0:T(8,128)(2,1)S(1)} %collective-permute-done.43.refs_1_), channel_id=1, source_target_pairs={{0,2},{1,3},{4,0},{5,1},{8,4},{9,5},{12,8},{13,9},{14,12},{15,13},... | collective-permute-start | bytes 626696 | tf_op jit(solution)/shard_map/ppermute | solution.py:363
  86.7 7.4 %collective-permute-start.66 = (bf16[48,2176]{1,0:T(8,128)(2,1)S(1)}, bf16[48,2176]{1,0:T(8,128)(2,1)}, u32[]{:S(2)}, u32[]{:S(2)}) collective-permute-start(bf16[48,2176]{1,0:T(8,128)(2,1)S(1)} %collective-permute-done.62.refs_0_), channel_id=1, source_target_pairs={{0,4},{1,5},{4,8},{5,9},{8,12},{9,13},{12,14},{13,15},{14,10},{15,... | collective-permute-start | bytes 626696 | tf_op jit(solution)/shard_map/ppermute | solution.py:362
  91.4 7.7 %collective-permute-start.41 = (bf16[48,2176]{1,0:T(8,128)(2,1)S(1)}, bf16[48,2176]{1,0:T(8,128)(2,1)}, u32[]{:S(2)}, u32[]{:S(2)}) collective-permute-start(bf16[48,2176]{1,0:T(8,128)(2,1)S(1)} %collective-permute-done.36.refs_0_), channel_id=1, source_target_pairs={{0,4},{1,5},{4,8},{5,9},{8,12},{9,13},{12,14},{13,15},{14,10},{15,... | collective-permute-start | bytes 626696 | tf_op jit(solution)/shard_map/ppermute | solution.py:366
  93.7 7.6 %collective-permute-start.45 = (bf16[48,2176]{1,0:T(8,128)(2,1)}, bf16[48,2176]{1,0:T(8,128)(2,1)}, u32[]{:S(2)}, u32[]{:S(2)}) collective-permute-start(bf16[48,2176]{1,0:T(8,128)(2,1)} %collective-permute-done.44.refs_1_), channel_id=1, source_target_pairs={{0,2},{1,3},{4,0},{5,1},{8,4},{9,5},{12,8},{13,9},{14,12},{15,13},... | collective-permute-start | bytes 626696 | tf_op jit(solution)/shard_map/ppermute | solution.py:367
  94.2 16.7 %collective-permute-start.28 = (bf16[48,2176]{1,0:T(8,128)(2,1)}, bf16[48,2176]{1,0:T(8,128)(2,1)}, u32[]{:S(2)}, u32[]{:S(2)}) collective-permute-start(bf16[48,2176]{1,0:T(8,128)(2,1)} %collective-permute-done.26.refs_0_), channel_id=1, source_target_pairs={{0,1},{1,0},{2,3},{3,2},{4,5},{5,4},{6,7},{7,6},{8,9},{9,8},{10,11... | collective-permute-start | bytes 626696 | tf_op jit(solution)/shard_map/ppermute | solution.py:364
  95.0 16.5 %collective-permute-start.67 = (bf16[48,2176]{1,0:T(8,128)(2,1)}, bf16[48,2176]{1,0:T(8,128)(2,1)}, u32[]{:S(2)}, u32[]{:S(2)}) collective-permute-start(bf16[48,2176]{1,0:T(8,128)(2,1)} %collective-permute-done.66.refs_0_), channel_id=1, source_target_pairs={{0,1},{1,0},{2,3},{3,2},{4,5},{5,4},{6,7},{7,6},{8,9},{9,8},{10,11... | collective-permute-start | bytes 626696 | tf_op jit(solution)/shard_map/ppermute | solution.py:364
  96.1 15.5 %collective-permute-start.68 = (bf16[48,2176]{1,0:T(8,128)(2,1)}, bf16[48,2176]{1,0:T(8,128)(2,1)}, u32[]{:S(2)}, u32[]{:S(2)}) collective-permute-start(bf16[48,2176]{1,0:T(8,128)(2,1)} %collective-permute-done.44.refs_1_), channel_id=1, source_target_pairs={{0,1},{1,0},{2,3},{3,2},{4,5},{5,4},{6,7},{7,6},{8,9},{9,8},{10,11... | collective-permute-start | bytes 626696 | tf_op jit(solution)/shard_map/ppermute | solution.py:364
  99.1 12.9 %collective-permute-start.46 = (bf16[48,2176]{1,0:T(8,128)(2,1)}, bf16[48,2176]{1,0:T(8,128)(2,1)}, u32[]{:S(2)}, u32[]{:S(2)}) collective-permute-start(bf16[48,2176]{1,0:T(8,128)(2,1)} %collective-permute-done.41.refs_0_), channel_id=1, source_target_pairs={{0,1},{1,0},{2,3},{3,2},{4,5},{5,4},{6,7},{7,6},{8,9},{9,8},{10,11... | collective-permute-start | bytes 626696 | tf_op jit(solution)/shard_map/ppermute | solution.py:368
  101.2 14.2 %collective-permute-start.47 = (bf16[48,2176]{1,0:T(8,128)(2,1)}, bf16[48,2176]{1,0:T(8,128)(2,1)S(1)}, u32[]{:S(2)}, u32[]{:S(2)}) collective-permute-start(bf16[48,2176]{1,0:T(8,128)(2,1)} %collective-permute-done.45.refs_1_), channel_id=1, source_target_pairs={{0,1},{1,0},{2,3},{3,2},{4,5},{5,4},{6,7},{7,6},{8,9},{9,8},{10,11... | collective-permute-start | bytes 626696 | tf_op jit(solution)/shard_map/ppermute | solution.py:368
  110.9 8.3 %collective-permute-start.29 = (bf16[48,2176]{1,0:T(8,128)(2,1)S(1)}, bf16[48,2176]{1,0:T(8,128)(2,1)S(1)}, u32[]{:S(2)}, u32[]{:S(2)}) collective-permute-start(bf16[48,2176]{1,0:T(8,128)(2,1)S(1)} %copy-done.19), channel_id=1, source_target_pairs={{0,1},{1,0},{2,3},{3,2},{4,5},{5,4},{6,7},{7,6},{8,9},{9,8},{10,11... | collective-permute-start | bytes 626696 | tf_op jit(solution)/shard_map/ppermute | solution.py:364
  111.5 7.8 %collective-permute-start.33 = (bf16[48,2176]{1,0:T(8,128)(2,1)S(1)}, bf16[48,2176]{1,0:T(8,128)(2,1)S(1)}, u32[]{:S(2)}, u32[]{:S(2)}) collective-permute-start(bf16[48,2176]{1,0:T(8,128)(2,1)S(1)} %copy-done.21), channel_id=1, source_target_pairs={{0,1},{1,0},{2,3},{3,2},{4,5},{5,4},{6,7},{7,6},{8,9},{9,8},{10,11... | collective-permute-start | bytes 626696 | tf_op jit(solution)/shard_map/ppermute | solution.py:364
  111.6 8.2 %collective-permute-start.34 = (bf16[48,2176]{1,0:T(8,128)(2,1)S(1)}, bf16[48,2176]{1,0:T(8,128)(2,1)S(1)}, u32[]{:S(2)}, u32[]{:S(2)}) collective-permute-start(bf16[48,2176]{1,0:T(8,128)(2,1)S(1)} %copy-done.25), channel_id=1, source_target_pairs={{0,1},{1,0},{2,3},{3,2},{4,5},{5,4},{6,7},{7,6},{8,9},{9,8},{10,11... | collective-permute-start | bytes 626696 | tf_op jit(solution)/shard_map/ppermute | solution.py:364
  112.0 7.8 %collective-permute-start.63 = (bf16[48,2176]{1,0:T(8,128)(2,1)S(1)}, bf16[48,2176]{1,0:T(8,128)(2,1)S(1)}, u32[]{:S(2)}, u32[]{:S(2)}) collective-permute-start(bf16[48,2176]{1,0:T(8,128)(2,1)S(1)} %copy-done.27), channel_id=1, source_target_pairs={{0,1},{1,0},{2,3},{3,2},{4,5},{5,4},{6,7},{7,6},{8,9},{9,8},{10,11... | collective-permute-start | bytes 626696 | tf_op jit(solution)/shard_map/ppermute | solution.py:364
  115.4 6.9 %collective-permute-start.64 = (bf16[48,2176]{1,0:T(8,128)(2,1)S(1)}, bf16[48,2176]{1,0:T(8,128)(2,1)S(1)}, u32[]{:S(2)}, u32[]{:S(2)}) collective-permute-start(bf16[48,2176]{1,0:T(8,128)(2,1)S(1)} %copy-done.23), channel_id=1, source_target_pairs={{0,1},{1,0},{2,3},{3,2},{4,5},{5,4},{6,7},{7,6},{8,9},{9,8},{10,11... | collective-permute-start | bytes 626696 | tf_op jit(solution)/shard_map/ppermute | solution.py:364
  119.3 6.0 %collective-permute-start.40 = (bf16[96,2048]{1,0:T(8,128)(2,1)S(1)}, bf16[96,2048]{1,0:T(8,128)(2,1)S(1)}, u32[]{:S(2)}, u32[]{:S(2)}) collective-permute-start(bf16[96,2048]{1,0:T(8,128)(2,1)S(1)} %get-tuple-element.51), channel_id=1, source_target_pairs={{0,1},{1,0},{2,3},{3,2},{4,5},{5,4},{6,7},{7,6},{8,9},{9,8},{10,11... | collective-permute-start | bytes 1179656 | tf_op jit(solution)/shard_map/ppermute | solution.py:370
  119.7 6.0 %collective-permute-start.69 = (bf16[96,2048]{1,0:T(8,128)(2,1)S(1)}, bf16[96,2048]{1,0:T(8,128)(2,1)S(1)}, u32[]{:S(2)}, u32[]{:S(2)}) collective-permute-start(bf16[96,2048]{1,0:T(8,128)(2,1)S(1)} %get-tuple-element.62), channel_id=1, source_target_pairs={{0,1},{1,0},{2,3},{3,2},{4,5},{5,4},{6,7},{7,6},{8,9},{9,8},{10,11... | collective-permute-start | bytes 1179656 | tf_op jit(solution)/shard_map/ppermute | solution.py:370
  122.4 8.9 %collective-permute-start.35 = (bf16[96,2048]{1,0:T(8,128)(2,1)S(1)}, bf16[96,2048]{1,0:T(8,128)(2,1)S(1)}, u32[]{:S(2)}, u32[]{:S(2)}) collective-permute-start(bf16[96,2048]{1,0:T(8,128)(2,1)S(1)} %get-tuple-element.49), channel_id=1, source_target_pairs={{0,1},{1,0},{2,3},{3,2},{4,5},{5,4},{6,7},{7,6},{8,9},{9,8},{10,11... | collective-permute-start | bytes 1179656 | tf_op jit(solution)/shard_map/ppermute | solution.py:370
  124.7 8.3 %collective-permute-start.65 = (bf16[96,2048]{1,0:T(8,128)(2,1)S(1)}, bf16[96,2048]{1,0:T(8,128)(2,1)S(1)}, u32[]{:S(2)}, u32[]{:S(2)}) collective-permute-start(bf16[96,2048]{1,0:T(8,128)(2,1)S(1)} %get-tuple-element.60), channel_id=1, source_target_pairs={{0,1},{1,0},{2,3},{3,2},{4,5},{5,4},{6,7},{7,6},{8,9},{9,8},{10,11... | collective-permute-start | bytes 1179656 | tf_op jit(solution)/shard_map/ppermute | solution.py:370
  125.3 7.3 %collective-permute-start.49 = (bf16[48,2048]{1,0:T(8,128)(2,1)S(1)}, bf16[48,2048]{1,0:T(8,128)(2,1)S(1)}, u32[]{:S(2)}, u32[]{:S(2)}) collective-permute-start(bf16[48,2048]{1,0:T(8,128)(2,1)S(1)} %add.24), channel_id=1, source_target_pairs={{0,4},{1,5},{4,8},{5,9},{8,12},{9,13},{12,14},{13,15},{14,10},{15,... | collective-permute-start | bytes 589832 | tf_op jit(solution)/shard_map/ppermute | solution.py:381
  125.7 10.0 %collective-permute-start.73 = (bf16[48,2048]{1,0:T(8,128)(2,1)S(1)}, bf16[48,2048]{1,0:T(8,128)(2,1)S(1)}, u32[]{:S(2)}, u32[]{:S(2)}) collective-permute-start(bf16[48,2048]{1,0:T(8,128)(2,1)S(1)} %add.34), channel_id=1, source_target_pairs={{0,2},{1,3},{4,0},{5,1},{8,4},{9,5},{12,8},{13,9},{14,12},{15,13},... | collective-permute-start | bytes 589832 | tf_op jit(solution)/shard_map/ppermute | solution.py:382
  130.7 6.7 %collective-permute-start.53 = (bf16[48,2048]{1,0:T(8,128)(2,1)S(1)}, bf16[48,2048]{1,0:T(8,128)(2,1)S(1)}, u32[]{:S(2)}, u32[]{:S(2)}) collective-permute-start(bf16[48,2048]{1,0:T(8,128)(2,1)S(1)} %add.28), channel_id=1, source_target_pairs={{0,2},{1,3},{4,0},{5,1},{8,4},{9,5},{12,8},{13,9},{14,12},{15,13},... | collective-permute-start | bytes 589832 | tf_op jit(solution)/shard_map/ppermute | solution.py:375
  131.3 15.3 %collective-permute-start.30 = (bf16[96,2048]{1,0:T(8,128)(2,1)S(1)}, bf16[96,2048]{1,0:T(8,128)(2,1)S(1)}, u32[]{:S(2)}, u32[]{:S(2)}) collective-permute-start(bf16[96,2048]{1,0:T(8,128)(2,1)S(1)} %get-tuple-element.47), channel_id=1, source_target_pairs={{0,1},{1,0},{2,3},{3,2},{4,5},{5,4},{6,7},{7,6},{8,9},{9,8},{10,11... | collective-permute-start | bytes 1179656 | tf_op jit(solution)/shard_map/ppermute | solution.py:370
  132.6 7.8 %collective-permute-start.70 = (bf16[48,2048]{1,0:T(8,128)(2,1)S(1)}, bf16[48,2048]{1,0:T(8,128)(2,1)S(1)}, u32[]{:S(2)}, u32[]{:S(2)}) collective-permute-start(bf16[48,2048]{1,0:T(8,128)(2,1)S(1)} %add.31), channel_id=1, source_target_pairs={{0,4},{1,5},{4,8},{5,9},{8,12},{9,13},{12,14},{13,15},{14,10},{15,... | collective-permute-start | bytes 589832 | tf_op jit(solution)/shard_map/ppermute | solution.py:375
  133.0 10.2 %collective-permute-start.50 = (bf16[48,2048]{1,0:T(8,128)(2,1)S(1)}, bf16[48,2048]{1,0:T(8,128)(2,1)S(1)}, u32[]{:S(2)}, u32[]{:S(2)}) collective-permute-start(bf16[48,2048]{1,0:T(8,128)(2,1)S(1)} %add.25), channel_id=1, source_target_pairs={{0,4},{1,5},{4,8},{5,9},{8,12},{9,13},{12,14},{13,15},{14,10},{15,... | collective-permute-start | bytes 589832 | tf_op jit(solution)/shard_map/ppermute | solution.py:375
  135.7 14.4 %collective-permute-start.61 = (bf16[96,2048]{1,0:T(8,128)(2,1)S(1)}, bf16[96,2048]{1,0:T(8,128)(2,1)S(1)}, u32[]{:S(2)}, u32[]{:S(2)}) collective-permute-start(bf16[96,2048]{1,0:T(8,128)(2,1)S(1)} %get-tuple-element.58), channel_id=1, source_target_pairs={{0,1},{1,0},{2,3},{3,2},{4,5},{5,4},{6,7},{7,6},{8,9},{9,8},{10,11... | collective-permute-start | bytes 1179656 | tf_op jit(solution)/shard_map/ppermute | solution.py:370
  137.5 8.7 %collective-permute-start.74 = (bf16[48,2048]{1,0:T(8,128)(2,1)S(1)}, bf16[48,2048]{1,0:T(8,128)(2,1)S(1)}, u32[]{:S(2)}, u32[]{:S(2)}) collective-permute-start(bf16[48,2048]{1,0:T(8,128)(2,1)S(1)} %add.35), channel_id=1, source_target_pairs={{0,2},{1,3},{4,0},{5,1},{8,4},{9,5},{12,8},{13,9},{14,12},{15,13},... | collective-permute-start | bytes 589832 | tf_op jit(solution)/shard_map/ppermute | solution.py:375
  140.4 8.0 %collective-permute-start.54 = (bf16[48,2048]{1,0:T(8,128)(2,1)S(1)}, bf16[48,2048]{1,0:T(8,128)(2,1)S(1)}, u32[]{:S(2)}, u32[]{:S(2)}) collective-permute-start(bf16[48,2048]{1,0:T(8,128)(2,1)S(1)} %add.29), channel_id=1, source_target_pairs={{0,2},{1,3},{4,0},{5,1},{8,4},{9,5},{12,8},{13,9},{14,12},{15,13},... | collective-permute-start | bytes 589832 | tf_op jit(solution)/shard_map/ppermute | solution.py:375
  143.2 7.5 %collective-permute-start.71 = (bf16[48,2048]{1,0:T(8,128)(2,1)S(1)}, bf16[48,2048]{1,0:T(8,128)(2,1)S(1)}, u32[]{:S(2)}, u32[]{:S(2)}) collective-permute-start(bf16[48,2048]{1,0:T(8,128)(2,1)S(1)} %add.32), channel_id=1, source_target_pairs={{0,4},{1,5},{4,8},{5,9},{8,12},{9,13},{12,14},{13,15},{14,10},{15,... | collective-permute-start | bytes 589832 | tf_op jit(solution)/shard_map/ppermute | solution.py:375
  146.1 6.9 %collective-permute-start.51 = (bf16[48,2048]{1,0:T(8,128)(2,1)S(1)}, bf16[48,2048]{1,0:T(8,128)(2,1)S(1)}, u32[]{:S(2)}, u32[]{:S(2)}) collective-permute-start(bf16[48,2048]{1,0:T(8,128)(2,1)S(1)} %add.26), channel_id=1, source_target_pairs={{0,4},{1,5},{4,8},{5,9},{8,12},{9,13},{12,14},{13,15},{14,10},{15,... | collective-permute-start | bytes 589832 | tf_op jit(solution)/shard_map/ppermute | solution.py:375
  146.6 8.5 %collective-permute-start.75 = (bf16[48,2048]{1,0:T(8,128)(2,1)S(1)}, bf16[48,2048]{1,0:T(8,128)(2,1)S(1)}, u32[]{:S(2)}, u32[]{:S(2)}) collective-permute-start(bf16[48,2048]{1,0:T(8,128)(2,1)S(1)} %add.36), channel_id=1, source_target_pairs={{0,2},{1,3},{4,0},{5,1},{8,4},{9,5},{12,8},{13,9},{14,12},{15,13},... | collective-permute-start | bytes 589832 | tf_op jit(solution)/shard_map/ppermute | solution.py:375
  148.4 7.1 %collective-permute-start.25 = (bf16[48,2048]{1,0:T(8,128)(2,1)S(1)}, bf16[48,2048]{1,0:T(8,128)(2,1)S(1)}, u32[]{:S(2)}, u32[]{:S(2)}) collective-permute-start(bf16[48,2048]{1,0:T(8,128)(2,1)S(1)} %get-tuple-element.45), channel_id=1, source_target_pairs={{0,1},{1,0},{2,3},{3,2},{4,5},{5,4},{6,7},{7,6},{8,9},{9,8},{10,11... | collective-permute-start | bytes 589832 | tf_op jit(solution)/shard_map/ppermute | solution.py:370
  150.1 7.1 %collective-permute-start.57 = (bf16[48,2048]{1,0:T(8,128)(2,1)S(1)}, bf16[48,2048]{1,0:T(8,128)(2,1)S(1)}, u32[]{:S(2)}, u32[]{:S(2)}) collective-permute-start(bf16[48,2048]{1,0:T(8,128)(2,1)S(1)} %get-tuple-element.56), channel_id=1, source_target_pairs={{0,1},{1,0},{2,3},{3,2},{4,5},{5,4},{6,7},{7,6},{8,9},{9,8},{10,11... | collective-permute-start | bytes 589832 | tf_op jit(solution)/shard_map/ppermute | solution.py:370
  150.7 7.8 %collective-permute-start.55 = (bf16[48,2048]{1,0:T(8,128)(2,1)S(1)}, bf16[48,2048]{1,0:T(8,128)(2,1)S(1)}, u32[]{:S(2)}, u32[]{:S(2)}) collective-permute-start(bf16[48,2048]{1,0:T(8,128)(2,1)S(1)} %add.30), channel_id=1, source_target_pairs={{0,2},{1,3},{4,0},{5,1},{8,4},{9,5},{12,8},{13,9},{14,12},{15,13},... | collective-permute-start | bytes 589832 | tf_op jit(solution)/shard_map/ppermute | solution.py:375
  153.0 7.8 %collective-permute-start.72 = (bf16[48,2048]{1,0:T(8,128)(2,1)S(1)}, bf16[48,2048]{1,0:T(8,128)(2,1)S(1)}, u32[]{:S(2)}, u32[]{:S(2)}) collective-permute-start(bf16[48,2048]{1,0:T(8,128)(2,1)S(1)} %add.33), channel_id=1, source_target_pairs={{0,4},{1,5},{4,8},{5,9},{8,12},{9,13},{12,14},{13,15},{14,10},{15,... | collective-permute-start | bytes 589832 | tf_op jit(solution)/shard_map/ppermute | solution.py:375
  155.1 8.2 %collective-permute-start.52 = (bf16[48,2048]{1,0:T(8,128)(2,1)S(1)}, bf16[48,2048]{1,0:T(8,128)(2,1)S(1)}, u32[]{:S(2)}, u32[]{:S(2)}) collective-permute-start(bf16[48,2048]{1,0:T(8,128)(2,1)S(1)} %add.27), channel_id=1, source_target_pairs={{0,4},{1,5},{4,8},{5,9},{8,12},{9,13},{12,14},{13,15},{14,10},{15,... | collective-permute-start | bytes 589832 | tf_op jit(solution)/shard_map/ppermute | solution.py:375
  155.5 7.8 %collective-permute-start.76 = (bf16[48,2048]{1,0:T(8,128)(2,1)S(1)}, bf16[48,2048]{1,0:T(8,128)(2,1)S(1)}, u32[]{:S(2)}, u32[]{:S(2)}) collective-permute-start(bf16[48,2048]{1,0:T(8,128)(2,1)S(1)} %add.37), channel_id=1, source_target_pairs={{0,2},{1,3},{4,0},{5,1},{8,4},{9,5},{12,8},{13,9},{14,12},{15,13},... | collective-permute-start | bytes 589832 | tf_op jit(solution)/shard_map/ppermute | solution.py:375
  (52 other events, 304.8 us)
